TPU v7x, 32 devices: a whole 2x2x4 slice. The times are simulated.
32 devices in a mesh: groups: 2 (over x), replica: 2 (over core), tensor: 8 (over z, y).
Axes of the slice: x: 2, y: 2, z: 4, core: 2. Of those that a mesh axis runs over, the one named last changes fastest.
Arguments:
- hidden: bfloat16 [128, 8192], P(('groups', 'replica'), 'tensor'), parts along dimension 0, may hold values from -6 to 6
- w_query: bfloat16 [8192, 8192], P(None, 'tensor'), may hold values from -0.0625 to 0.0625
- output_weight: bfloat16 [8192, 8192], P('tensor'), may hold values from -0.09375 to 0.09375
- keys: bfloat16 [128, 8, 32, 128], P(('groups', 'replica')), parts along dimension 0
- values: bfloat16 [128, 8, 32, 128], P(('groups', 'replica')), parts along dimension 0, may hold values from -6 to 6
- query_down_maps: bfloat16 [16, 64, 8192], P(('groups', 'replica'), None, 'tensor'), parts along dimension 0, may hold values from -0.0625 to 0.0625
- query_up_maps: bfloat16 [16, 64, 8192], P(('groups', 'replica'), None, 'tensor'), parts along dimension 0, may hold values from -0.75 to 0.75
- output_down_maps: bfloat16 [16, 64, 8192], P(('groups', 'replica'), None, 'tensor'), parts along dimension 0, may hold values from -0.0625 to 0.0625
- output_up_maps: bfloat16 [16, 64, 8192], P(('groups', 'replica'), None, 'tensor'), parts along dimension 0, may hold values from -0.75 to 0.75
- adapter_ids: int32 [128], P('groups'), parts along dimension 0, may hold values from 0 to 7
- owner_map: int32 [16], P('groups'), parts along dimension 0, may hold values from 0 to 7, each once
- kv_lengths: int32 [128], P(('groups', 'replica')), parts along dimension 0, may hold values from 1 to 32, as said below
Outputs:
- attn_out: bfloat16 [128, 8192], P(('groups', 'replica'), 'tensor'), parts along dimension 0
There are 2 independent parts, one for each index of `groups`. A program takes and returns all parts, laid end to end along the dimension named above; an argument that names none is the same for every part. Nothing has to cross between parts.
Inputs may be any that keep to these rules, and one draw needn't show every extreme that they name: `owner_map`: every request's adapter has a slot; slot s is stored at replica index s // 4. Request r attends to its first kv_lengths[r] cached positions; some request holds all 32.
All inputs are finite; a program needn't handle non-finite values.
Results may differ from a plain program's by a relative error of at most 0.0092.
Values may be sent and summed in bfloat16 or wider, within the bound.
No kernel may reach another device: no remote copies, remote signals or barrier semaphores. Data moves between devices by JAX's collectives and lax.ppermute only.
A program may use at most 128 MiB of HBM per device.

v0:
```python
import functools
import math

import jax
import jax.numpy as jnp
from jax import lax
from jax.experimental import pallas as pl
from jax.experimental.pallas import tpu as pltpu
from jax.sharding import PartitionSpec as P

HEADS = 64
KVS = 8
VMEM = pl.BlockSpec(memory_space=pltpu.VMEM)
SMEM = pl.BlockSpec(memory_space=pltpu.SMEM)
HBM = pl.BlockSpec(memory_space=pltpu.HBM)
LANES = 128
PIECES = 2
GRANT = 49 << 20


def dot(a, b):
    return jnp.dot(a, b, preferred_element_type=jnp.float32)


def dot_t(a, b):
    return lax.dot_general(a, b, (((1,), (1,)), ((), ())), preferred_element_type=jnp.float32)


def params(flops_bytes, limit=GRANT):
    return dict(
        compiler_params=pltpu.CompilerParams(vmem_limit_bytes=limit),
        cost_estimate=pl.CostEstimate(
            flops=flops_bytes[0], bytes_accessed=flops_bytes[1], transcendentals=0
        ),
    )


def low_of(x, downs, picks):
    total = 0.0
    at = 0
    for down in downs:
        wide = down.shape[0]
        part = dot_t(x, down[...]) * picks[:, at : at + wide]
        for g in range(0, wide, LANES):
            total = total + part[:, g : g + LANES]
        at += wide
    return total


def lora_of(low, ups, picks):
    total = 0.0
    at = 0
    low = low.astype(jnp.bfloat16).astype(jnp.float32)
    for up in ups:
        wide = up.shape[0]
        spread = jnp.concatenate([low] * (wide // LANES), axis=1) * picks[:, at : at + wide]
        total = total + dot(spread.astype(jnp.bfloat16), up[...])
        at += wide
    return total


def load_all(pairs, sems):
    copies = [pltpu.make_async_copy(src, dst, sems.at[i]) for i, (src, dst) in enumerate(pairs)]
    for c in copies:
        c.start()
    return copies


def low_kernel(count, x_hbm, picks_ref, *rest):
    downs, out_ref, x_ref, bufs, sems = rest[:count], rest[count], rest[count + 1], rest[count + 2 : -1], rest[-1]
    for c in load_all([(x_hbm, x_ref)] + list(zip(downs, bufs)), sems):
        c.wait()
    out_ref[...] = low_of(x_ref[...], bufs, picks_ref[...])


def low_call(x, picks, downs):
    return pl.pallas_call(
        functools.partial(low_kernel, len(downs)),
        in_specs=[HBM, VMEM] + [HBM] * len(downs),
        out_specs=VMEM,
        out_shape=jax.ShapeDtypeStruct((x.shape[0], LANES), jnp.float32),
        scratch_shapes=[pltpu.VMEM(x.shape, x.dtype)]
        + [pltpu.VMEM(d.shape, d.dtype) for d in downs]
        + [pltpu.SemaphoreType.DMA((1 + len(downs),))],
        name="low",
        **params((10**8, 10**6)),
    )(x, picks, *downs)


def weight_copies(weight, buf, sems, j, block, along):
    depth, wide = buf.shape[1], buf.shape[2]
    piece = depth // PIECES
    copies = []
    for p in range(PIECES):
        if along == 0:
            src = weight.at[pl.ds(pl.multiple_of(block * depth + p * piece, piece), piece), :]
        else:
            src = weight.at[p * piece : (p + 1) * piece, pl.ds(pl.multiple_of(block * wide, LANES), wide)]
        copies.append(
            pltpu.make_async_copy(src, buf.at[j, p * piece : (p + 1) * piece, :], sems.at[j, p])
        )
    return copies


def block_dot(x_ref_read, buf, j, copies, total):
    piece = buf.shape[1] // PIECES
    for p in range(PIECES):
        copies[p].wait()
        total = total + dot(
            x_ref_read(p * piece, piece), buf[j, p * piece : (p + 1) * piece, :]
        )
    return total


def project_kernel(ks, spans, first, tensor_ref, *rest):
    given = len(set(i for i, _ in spans))
    chunks, rest = rest[:given], rest[given:]
    weight, rest = rest[0], rest[1:]
    if first:
        total = 0.0
    else:
        total, rest = rest[0][...], rest[1:]
    out_ref, buf, sems = rest
    rows = out_ref.shape[0]
    copies = [weight_copies(weight, buf, sems, j, tensor_ref[0] ^ k, 0) for j, k in enumerate(ks)]
    for pieces in copies:
        for c in pieces:
            c.start()
    for j, (i, r) in enumerate(spans):
        total = block_dot(
            lambda a, n, i=i, r=r: chunks[i][r : r + rows, a : a + n], buf, j, copies[j], total
        )
    out_ref[...] = total


def project_call(where, ks, tensor_at, weight, before, rows, width):
    wide = weight.shape[1]
    count = len(ks)
    arrays, spans = [], []
    for k in ks:
        array, r = where[k]
        if not any(a is array for a in arrays):
            arrays.append(array)
        spans.append(([a is array for a in arrays].index(True), r))
    extra = [] if before is None else [before]
    return pl.pallas_call(
        functools.partial(project_kernel, ks, spans, before is None),
        in_specs=[SMEM] + [VMEM] * len(arrays) + [HBM] + [VMEM] * len(extra),
        out_specs=VMEM,
        out_shape=jax.ShapeDtypeStruct((rows, wide), jnp.float32),
        scratch_shapes=[
            pltpu.VMEM((count, width, wide), weight.dtype),
            pltpu.SemaphoreType.DMA((count, PIECES)),
        ],
        **params(
            (2 * count * rows * width * wide, 2 * count * width * wide),
        ),
    )(tensor_at, *arrays, weight, *extra)


def mix_kernel(sizes, *refs):
    k_in, k_out, maps, kv_count, group, head, local_heads, group_all, _ = sizes
    refs = list(refs)
    tensor_ref, chunk, w_in, w_out, before, low, picks = [refs.pop(0) for _ in range(7)]
    ups = [refs.pop(0) for _ in range(maps)]
    downs = [refs.pop(0) for _ in range(maps)]
    keys, values, live = [refs.pop(0) for _ in range(3)]
    block_out, low_out, mixed_out = [refs.pop(0) for _ in range(3)]
    buf_in, sem_in, buf_out, sem_out, k_buf, v_buf, up_buf, down_buf, sems = refs

    tensor_at = tensor_ref[0]
    copies_in = weight_copies(w_in, buf_in, sem_in, 0, tensor_at ^ k_in, 0)
    copies_out = weight_copies(w_out, buf_out, sem_out, 0, tensor_at ^ k_out, 1)
    kv = pl.ds(tensor_at * local_heads // group_all, kv_count)
    up_copies = load_all([(u, up_buf.at[i]) for i, u in enumerate(ups)], sems.at[0])
    for c in copies_in:
        c.start()
    kv_copies = load_all([(keys.at[:, kv], k_buf), (values.at[:, kv], v_buf)], sems.at[1])
    down_copies = load_all([(d, down_buf.at[i]) for i, d in enumerate(downs)], sems.at[2])
    for c in copies_out:
        c.start()

    rows = before.shape[0]
    picked = picks[...]
    for c in up_copies:
        c.wait()
    total = before[...] + 0.5 * lora_of(low[...], [up_buf.at[i] for i in range(maps)], picked)
    total = block_dot(lambda a, n: chunk[:, a : a + n], buf_in, 0, copies_in, total)
    query = total.astype(jnp.bfloat16)
    for c in kv_copies:
        c.wait()
    length = k_buf.shape[2]
    heads = [None] * (kv_count * group)
    alive = jnp.concatenate([live[...]] * group, axis=0) > 0
    for kvh in range(kv_count):
        flat_k = k_buf[:, kvh].reshape(rows * length, head)
        flat_v = v_buf[:, kvh].reshape(rows * length, head)
        q = jnp.concatenate(
            [query[:, (kvh * group + g) * head : (kvh * group + g + 1) * head] for g in range(group)],
            axis=0,
        )
        scores = dot_t(q, flat_k) / math.sqrt(head)
        scores = jnp.where(alive, scores, -1e30)
        top = jnp.max(scores, axis=1, keepdims=True)
        weights = jnp.exp(scores - top)
        probs = (weights / jnp.sum(weights, axis=1, keepdims=True)).astype(jnp.bfloat16)
        got = dot(probs, flat_v).astype(jnp.bfloat16)
        for g in range(group):
            heads[kvh * group + g] = got[g * rows : (g + 1) * rows]
    mixed = jnp.concatenate(heads, axis=1)
    mixed_out[...] = mixed
    for c in down_copies:
        c.wait()
    low_part = low_of(mixed, [down_buf.at[i] for i in range(maps)], picked)
    low_out[...] = low_part
    block = block_dot(lambda a, n: mixed[:, a : a + n], buf_out, 0, copies_out, 0.0)
    wide = block.shape[1]
    block_out[:, :wide] = block.astype(block_out.dtype)
    block_out[:, wide:] = low_part.astype(block_out.dtype)


def out_kernel(ks, spans, tensor_ref, x_ref, weight, *rest):
    outs, (buf, sems) = rest[:-2], rest[-2:]
    rows = x_ref.shape[0]
    copies = [weight_copies(weight, buf, sems, j, tensor_ref[0] ^ k, 1) for j, k in enumerate(ks)]
    for pieces in copies:
        for c in pieces:
            c.start()
    for j, (i, r) in enumerate(spans):
        block = block_dot(lambda a, n: x_ref[:, a : a + n], buf, j, copies[j], 0.0)
        outs[i][r : r + rows, :] = block.astype(outs[i].dtype)


def out_call(groups, tensor_at, mixed, weight, out_width):
    rows, depth = mixed.shape
    ks = [k for group, _ in groups for k in group]
    spans = [(i, r * rows) for i, (group, _) in enumerate(groups) for r in range(len(group))]
    return pl.pallas_call(
        functools.partial(out_kernel, ks, spans),
        in_specs=[SMEM, VMEM, HBM],
        out_specs=[VMEM] * len(groups),
        out_shape=[jax.ShapeDtypeStruct((rows * len(group), out_width), kind) for group, kind in groups],
        scratch_shapes=[
            pltpu.VMEM((len(ks), depth, out_width), weight.dtype),
            pltpu.SemaphoreType.DMA((len(ks), PIECES)),
        ],
        **params((2 * len(ks) * rows * depth * out_width, 2 * len(ks) * depth * out_width)),
    )(tensor_at, mixed, weight)


def final_kernel(wide, count, maps, picks_ref, low_ref, *rest):
    ups, rest = rest[:maps], rest[maps:]
    lows, rest = rest[: count[0]], rest[count[0] :]
    terms, rest = rest[: count[1]], rest[count[1] :]
    out_ref, up_buf, sems = rest
    copies = load_all([(u, up_buf.at[i]) for i, u in enumerate(ups)], sems)
    low = low_ref[...]
    total = 0.0
    for ref in lows:
        low = low + ref[:, wide:].astype(jnp.float32)
    total = lows[-1][:, :wide].astype(jnp.float32)
    for t in terms:
        total = total + t[:, :wide].astype(jnp.float32)
    for c in copies:
        c.wait()
    total = total + 0.5 * lora_of(low, [up_buf.at[i] for i in range(maps)], picks_ref[...])
    out_ref[...] = total.astype(out_ref.dtype)


def low_bit(k):
    return k & -k


def per_device(
    mesh_shape,
    hidden,
    w_query,
    output_weight,
    keys,
    values,
    query_down_maps,
    query_up_maps,
    output_down_maps,
    output_up_maps,
    adapter_ids,
    owner_map,
    kv_lengths,
):
    rows, width = hidden.shape
    head = keys.shape[3]
    length = keys.shape[2]
    shards = mesh_shape["tensor"]
    replicas = mesh_shape["replica"]
    stored, rank = query_down_maps.shape[:2]
    replica_at = lax.axis_index("replica")
    tensor_at = lax.axis_index("tensor").astype(jnp.int32).reshape(1)
    bits = []
    while (1 << len(bits)) < shards:
        bits.append(1 << len(bits))

    def across(x, bit):
        return lax.ppermute(x, "tensor", [(i, i ^ bit) for i in range(shards)])

    def with_swapped(x):
        x = x.reshape(stored * rank, x.shape[2])
        return [x] + [
            lax.ppermute(x, "replica", [(i, (i + k) % replicas) for i in range(replicas)])
            for k in range(1, replicas)
        ]

    id_table = lax.broadcasted_iota(jnp.int32, (1, owner_map.shape[0]), 1)
    slots_all = jnp.sum(jnp.where(adapter_ids[:, None] == id_table, owner_map[None, :], 0), axis=1)
    slots = lax.dynamic_slice_in_dim(slots_all, replica_at * rows, rows)
    lane = lax.broadcasted_iota(jnp.int32, (1, stored * rank), 1) // rank
    picks = jnp.concatenate(
        [
            (slots[:, None] == ((replica_at - k) % replicas) * stored + lane).astype(jnp.float32)
            for k in range(replicas)
        ],
        axis=1,
    )
    column = lax.broadcasted_iota(jnp.int32, (rows, rows * length), 1)
    row = lax.broadcasted_iota(jnp.int32, (rows, rows * length), 0)
    live = ((column // length == row) & (column % length < kv_lengths[:, None])).astype(jnp.float32)

    query_down = with_swapped(query_down_maps)
    query_up = with_swapped(query_up_maps)
    output_down = with_swapped(output_down_maps)
    output_up = with_swapped(output_up_maps)

    low = low_call(hidden, picks, query_down)
    where = {0: (hidden, 0)}
    chain = 0
    for bit in reversed(bits):
        held = list(where)
        if bit != 1:
            for k in held:
                where[k | bit] = (across(where[k][0], bit), 0)
            low = low + across(low, bit)
        else:
            where[1] = (across(hidden, 1), 0)
            rest = [k for k in held if k not in (0, chain)]
            if rest:
                got = across(jnp.concatenate([where[k][0] for k in rest], axis=0), 1)
                for i, k in enumerate(rest):
                    where[k | 1] = (got, i * rows)
            if chain:
                joined = jnp.concatenate([where[chain][0], low.astype(jnp.bfloat16)], axis=1)
                got = across(joined, 1)
                where[chain | 1] = (got, 0)
                low = low + got[:, width:].astype(jnp.float32)
            else:
                low = low + across(low, 1)
        chain |= bit

    top = bits[-1] if bits else 0
    order = sorted(where, key=lambda k: (bin(k).count("1"), -k))
    last = order[-1]
    early = order[:-1]
    first = [k for k in early if k in (0, top >> 1, top)]
    others = [k for k in early if k not in first]
    query = project_call(where, first, tensor_at, w_query, None, rows, width)
    for i in range(0, len(others), 6):
        query = project_call(where, others[i : i + 6], tensor_at, w_query, query, rows, width)

    wide = w_query.shape[1]
    local_heads = wide // head
    group_all = HEADS // KVS
    kv_count = max(1, local_heads // group_all)
    group = local_heads // kv_count
    out_width = output_weight.shape[1] // shards
    depth = output_weight.shape[0]
    whole = shards - 1
    sizes = (last, whole, replicas, kv_count, group, head, local_heads, group_all, width)
    map_in, map_out = (stored * rank, wide), (stored * rank, depth)
    payload, low2, mixed = pl.pallas_call(
        functools.partial(mix_kernel, sizes),
        in_specs=[SMEM, VMEM, HBM, HBM, VMEM, VMEM, VMEM] + [HBM] * (2 * replicas) + [HBM, HBM, VMEM],
        out_specs=[VMEM] * 3,
        out_shape=[
            jax.ShapeDtypeStruct((rows, out_width + LANES), jnp.bfloat16),
            jax.ShapeDtypeStruct((rows, LANES), jnp.float32),
            jax.ShapeDtypeStruct((rows, wide), jnp.bfloat16),
        ],
        scratch_shapes=[
            pltpu.VMEM((1, width, wide), w_query.dtype),
            pltpu.SemaphoreType.DMA((1, PIECES)),
            pltpu.VMEM((1, depth, out_width), output_weight.dtype),
            pltpu.SemaphoreType.DMA((1, PIECES)),
            pltpu.VMEM((rows, kv_count, length, head), keys.dtype),
            pltpu.VMEM((rows, kv_count, length, head), values.dtype),
            pltpu.VMEM((replicas,) + map_in, keys.dtype),
            pltpu.VMEM((replicas,) + map_out, keys.dtype),
            pltpu.SemaphoreType.DMA((3, max(2, replicas))),
        ],
        name="mix",
        **params((10**9, 6 << 20)),
    )(
        tensor_at,
        where[last][0],
        w_query,
        output_weight,
        query,
        low,
        picks,
        *query_up,
        *output_down,
        keys,
        values,
        live,
    )

    came = {whole: across(payload, 1)}
    chain = [whole]
    while chain[-1]:
        chain.append(chain[-1] & (chain[-1] - 1))
    odd = [k for k in sorted(where, reverse=True) if k & 1 and k not in (whole, 1)]
    even = [k for k in sorted(where, reverse=True) if not k & 1]
    f32, bf16 = jnp.float32, jnp.bfloat16
    plan = [([k], f32) for k in even[:1]] + [(odd, bf16)] * bool(odd)
    plan = [plan, [([k], f32) for k in even[1:-1]] + [([1], bf16)], [([k], f32) for k in even[-1:]]]
    parts = {}
    for groups in plan:
        arrays = out_call(groups, tensor_at, mixed, output_weight, out_width)
        for (g, kind), array in zip(groups, arrays):
            if kind == bf16:
                got = across(array, 1)
                for i, k in enumerate(g):
                    came[k] = got[i * rows : (i + 1) * rows]
            else:
                parts[g[0]] = array
    for k in sorted((k for k in where if k and not k & 1), key=lambda k: (low_bit(k), -k)):
        main = parts[k]
        bit = 1
        while bit < low_bit(k):
            main = main + came[k | bit][:, :out_width].astype(jnp.float32)
            bit *= 2
        if k in chain:
            carried = low2
            for c in chain[: chain.index(k)]:
                carried = carried + came[c][:, out_width:].astype(jnp.float32)
            main = jnp.concatenate([main, carried], axis=1)
        came[k] = across(main.astype(jnp.bfloat16), low_bit(k))
    lows = [came[k] for k in chain[:-1]]
    terms = [parts[0]] + [came[1 << i] for i in range(len(bits) - 1)]
    return pl.pallas_call(
        functools.partial(final_kernel, out_width, (len(lows), len(terms)), replicas),
        in_specs=[VMEM, VMEM] + [HBM] * replicas + [VMEM] * (len(lows) + len(terms)),
        out_specs=VMEM,
        out_shape=jax.ShapeDtypeStruct((rows, out_width), jnp.bfloat16),
        scratch_shapes=[
            pltpu.VMEM((replicas,) + map_in, keys.dtype),
            pltpu.SemaphoreType.DMA((replicas,)),
        ],
        name="final",
        **params((10**8, 10**6)),
    )(picks, low2, *output_up, *lows, *terms)


def solution(mesh):
    sizes = dict(mesh.shape)

    def body(*arrays):
        return per_device(sizes, *arrays)

    return jax.shard_map(
        body,
        mesh=mesh,
        in_specs=(
            P(("groups", "replica"), "tensor"),
            P(None, "tensor"),
            P("tensor", None),
            P(("groups", "replica"), None, None, None),
            P(("groups", "replica"), None, None, None),
            P(("groups", "replica"), None, "tensor"),
            P(("groups", "replica"), None, "tensor"),
            P(("groups", "replica"), None, "tensor"),
            P(("groups", "replica"), None, "tensor"),
            P("groups"),
            P("groups"),
            P(("groups", "replica")),
        ),
        out_specs=P(("groups", "replica"), "tensor"),
        check_vma=False,
    )
```

profile of v0, /device:TPU:0, one launch (start us, length us, event | category | flops | bytes accessed | tf_op | source)
XLA Modules:
  0.0 55.7 jit_solution(14991331297591031231)
XLA Ops:
  0.0 3.0 %collective-permute-start.6 = (bf16[32,1024]{1,0:T(8,128)(2,1)}, bf16[32,1024]{1,0:T(8,128)(2,1)S(1)}, u32[]{:S(2)}, u32[]{:S(2)}) collective-permute-start(bf16[32,1024]{1,0:T(8,128)(2,1)} %rest_0_.1), channel_id=1, source_target_pairs={{0,1},{1,0},{2,3},{3,2},{4,5},{5,4},{6,7},{7,6},{8,9},{9,8},{10,11... | collective-permute-start | bytes 196616 | tf_op jit(solution)/shard_map/ppermute | solution.py:302
  3.0 2.6 %collective-permute-start = (bf16[32,1024]{1,0:T(8,128)(2,1)}, bf16[32,1024]{1,0:T(8,128)(2,1)S(1)}, u32[]{:S(2)}, u32[]{:S(2)}) collective-permute-start(bf16[32,1024]{1,0:T(8,128)(2,1)} %rest_0_.1), channel_id=1, source_target_pairs={{0,4},{1,5},{2,6},{3,7},{4,0},{5,1},{6,2},{7,3},{8,12},{9,13},{10,... | collective-permute-start | bytes 196616 | tf_op jit(solution)/shard_map/ppermute | solution.py:302
  5.6 1.6 %collective-permute-start.7 = (bf16[32,1024]{1,0:T(8,128)(2,1)}, bf16[32,1024]{1,0:T(8,128)(2,1)S(1)}, u32[]{:S(2)}, u32[]{:S(2)}) collective-permute-start(bf16[32,1024]{1,0:T(8,128)(2,1)} %rest_0_.1), channel_id=1, source_target_pairs={{0,2},{1,3},{2,0},{3,1},{4,6},{5,7},{6,4},{7,5},{8,10},{9,11},{10,... | collective-permute-start | bytes 196616 | tf_op jit(solution)/shard_map/ppermute | solution.py:302
  7.2 0.0 collective-permute-start.2
  7.2 0.5 collective-permute-start.9
  7.7 0.8 %select_reduce_fusion = s32[64]{0:T(128)S(1)} fusion(s32[8]{0:T(128)} %param.22, s32[64]{0:T(128)} %param.21), kind=kLoop, calls=%fused_computation.27 | loop fusion | flops 1472 | bytes 544 | tf_op jit(solution)/shard_map/reduce_sum | solution.py:312
  8.4 0.1 dynamic_slice.3
  8.5 0.1 broadcast_compare_fusion.1
  8.6 0.7 %collective-permute-done.2.rest_1_ = bf16[256,1024]{1,0:T(8,128)(2,1)S(1)} collective-permute-done((bf16[256,1024]{1,0:T(8,128)(2,1)}, bf16[256,1024]{1,0:T(8,128)(2,1)S(1)}, u32[]{:S(2)}, u32[]{:S(2)}) %collective-permute-start.2) | collective-permute-done | bytes 524320 | tf_op jit(solution)/shard_map/ppermute | solution.py:307
  9.3 0.0 copy-start.4
  9.3 1.0 %copy-done.4 = bf16[4,64,1024]{2,1,0:T(8,128)(2,1)S(1)} copy-done((bf16[4,64,1024]{2,1,0:T(8,128)(2,1)S(1)}, bf16[4,64,1024]{2,1,0:T(8,128)(2,1)}, u32[]{:S(2)}) %copy-start.4) | copy-done | bytes 524312
  10.3 0.0 copy-start.5
  10.3 0.8 %copy-done.5 = bf16[32,1024]{1,0:T(8,128)(2,1)S(1)} copy-done((bf16[32,1024]{1,0:T(8,128)(2,1)S(1)}, bf16[32,1024]{1,0:T(8,128)(2,1)}, u32[]{:S(2)}) %copy-start.5) | copy-done | bytes 65560
  11.2 0.6 %low.1 = f32[32,128]{1,0:T(8,128)S(1)} custom-call(bf16[32,1024]{1,0:T(8,128)(2,1)S(1)} %copy-done.5, f32[32,512]{1,0:T(8,128)S(1)} %add_convert_fusion.3.picks_ref.refs_6_, bf16[256,1024]{1,0:T(8,128)(2,1)S(1)} %bitcast.12, bf16[256,1024]{1,0:T(8,128)(2,1)S(1)} %collective-permute-done.2.rest_1_), custom_call_target="tpu_custom_call" | custom-call | flops 100000000 | bytes 1000000 | tf_op jit(solution)/shard_map/low/pallas_call | solution.py:77
  11.8 0.4 collective-permute-start.3
  12.2 4.4 %collective-permute-done.3 = f32[32,128]{1,0:T(8,128)S(1)} collective-permute-done((f32[32,128]{1,0:T(8,128)S(1)}, f32[32,128]{1,0:T(8,128)S(1)}, u32[]{:S(2)}, u32[]{:S(2)}) %collective-permute-start.3) | collective-permute-done | bytes 16416 | tf_op jit(solution)/shard_map/ppermute | solution.py:302
  16.5 0.0 collective-permute-start.10
  16.5 0.0 collective-permute-done.rest_1_
  16.5 0.5 collective-permute-start.4
  17.0 0.0 collective-permute-done.7.rest_2_
  17.0 0.6 %collective-permute-start.8 = (bf16[64,1024]{1,0:T(8,128)(2,1)S(1)}, bf16[64,1024]{1,0:T(8,128)(2,1)S(1)}, u32[]{:S(2)}, u32[]{:S(2)}) collective-permute-start(bf16[64,1024]{1,0:T(8,128)(2,1)S(1)} %pad_maximum_fusion), channel_id=1, source_target_pairs={{0,1},{1,0},{2,3},{3,2},{4,5},{5,4},{6,7},{7,6},{8,9},{9,8},{10,11... | collective-permute-start | bytes 393224 | tf_op jit(solution)/shard_map/ppermute | solution.py:302
  17.6 2.8 %collective-permute-done.4 = f32[32,128]{1,0:T(8,128)S(1)} collective-permute-done((f32[32,128]{1,0:T(8,128)S(1)}, f32[32,128]{1,0:T(8,128)S(1)}, u32[]{:S(2)}, u32[]{:S(2)}) %collective-permute-start.4) | collective-permute-done | bytes 16416 | tf_op jit(solution)/shard_map/ppermute | solution.py:302
  20.3 0.4 collective-permute-start.1
  20.7 3.9 %collective-permute-done.1.rest_1_ = bf16[32,1024]{1,0:T(8,128)(2,1)S(1)} collective-permute-done((bf16[32,1024]{1,0:T(8,128)(2,1)S(1)}, bf16[32,1024]{1,0:T(8,128)(2,1)S(1)}, u32[]{:S(2)}, u32[]{:S(2)}) %collective-permute-start.1) | collective-permute-done | bytes 65568 | tf_op jit(solution)/shard_map/ppermute | solution.py:302
  24.6 0.5 collective-permute-start.5
  25.1 0.7 %fusion.1.refs_13_ = f32[32,1024]{1,0:T(8,128)S(1)} fusion(s32[32]{0:T(128)} %param.23, s32[1024]{0:T(1024)S(1)} %get-tuple-element.30, s32[1024]{0:T(1024)S(1)} %get-tuple-element.31, s32[1024]{0:T(1024)S(1)} %get-tuple-element.29, s32[1024]{0:T(1024)S(1)} %get-tuple-element.32, pred[1024]{0:T(1024)(128)(4,1)S(1)} %get-tuple-element.33, ...), kind=kLoop, calls=%fused_computation.7 | loop fusion | flops 196608 | bytes 149632 | tf_op jit(solution)/shard_map/convert_element_type | solution.py:324
  25.9 0.0 copy-start.6
  25.9 0.8 %copy-done.6 = bf16[32,1024]{1,0:T(8,128)(2,1)S(1)} copy-done((bf16[32,1024]{1,0:T(8,128)(2,1)S(1)}, bf16[32,1024]{1,0:T(8,128)(2,1)}, u32[]{:S(2)}) %copy-start.6) | copy-done | bytes 65560
  26.7 0.0 copy-start
  26.7 0.0 copy-start.1
  26.7 0.0 copy-start.2
  26.7 3.3 %shard_map.118.rest_4_ = f32[32,1024]{1,0:T(8,128)S(1)} custom-call(s32[1]{0:T(128)} %bitcast.tensor_ref.refs_0_, bf16[32,1024]{1,0:T(8,128)(2,1)S(1)} %copy-done.6, bf16[32,1024]{1,0:T(8,128)(2,1)S(1)} %collective-permute-done.rest_1_, bf16[32,1024]{1,0:T(8,128)(2,1)S(1)} %collective-permute-done.7.rest_2_, bf16[8192,1024]{1,0:T(8,128)(2,1)} %refs_2_.1), custom_call_target="tpu_custom_call" | custom-call | flops 201326592 | bytes 6291456 | tf_op jit(solution)/shard_map/pallas_call | solution.py:146
  30.0 0.0 collective-permute-done.6.rest_0_
  30.0 0.0 collective-permute-done.8.rest_2_
  30.0 3.8 %shard_map.119.refs_4_ = f32[32,1024]{1,0:T(8,128)S(1)} custom-call(s32[1]{0:T(128)} %bitcast.tensor_ref.refs_0_, bf16[32,1024]{1,0:T(8,128)(2,1)S(1)} %collective-permute-done.6.rest_0_, bf16[32,1024]{1,0:T(8,128)(2,1)S(1)} %collective-permute-done.1.rest_1_, bf16[64,1024]{1,0:T(8,128)(2,1)S(1)} %collective-permute-done.8.rest_2_, ...), custom_call_target="tpu_custom_call" | custom-call | flops 268435456 | bytes 8388608 | tf_op jit(solution)/shard_map/pallas_call | solution.py:146
  33.8 0.0 collective-permute-done.5.refs_1_
  33.8 0.0 collective-permute-done.9.refs_8_
  33.9 0.0 collective-permute-done.10.refs_10_
  33.9 0.0 copy-done
  33.9 0.0 copy-done.1
  33.9 0.0 copy-done.2
  33.9 3.8 %mix.1 = (bf16[32,1152]{1,0:T(8,128)(2,1)S(1)}, f32[32,128]{1,0:T(8,128)S(1)}, bf16[32,1024]{1,0:T(8,128)(2,1)S(1)}) custom-call(s32[1]{0:T(128)} %bitcast.tensor_ref.refs_0_, bf16[32,1152]{1,0:T(8,128)(2,1)S(1)} %collective-permute-done.5.refs_1_, bf16[8192,1024]{1,0:T(8,128)(2,1)} %refs_2_.1, bf16[1024,8192]{1,0:T(8,128)(2,1)} %weight.5, ...), custom_call_target="tpu_custom_call" | custom-call | flops 1000000000 | bytes 6291456 | tf_op jit(solution)/shard_map/mix/pallas_call | solution.py:376
  37.7 0.0 copy-start.3
  37.7 1.6 %collective-permute-start.12 = (bf16[32,1152]{1,0:T(8,128)(2,1)S(1)}, bf16[32,1152]{1,0:T(8,128)(2,1)S(1)}, u32[]{:S(2)}, u32[]{:S(2)}) collective-permute-start(bf16[32,1152]{1,0:T(8,128)(2,1)S(1)} %get-tuple-element.14), channel_id=1, source_target_pairs={{0,1},{1,0},{2,3},{3,2},{4,5},{5,4},{6,7},{7,6},{8,9},{9,8},{10,11... | collective-permute-start | bytes 221192 | tf_op jit(solution)/shard_map/ppermute | solution.py:302
  39.3 3.3 %shard_map.120 = (f32[32,1024]{1,0:T(8,128)S(1)}, bf16[64,1024]{1,0:T(8,128)(2,1)S(1)}) custom-call(s32[1]{0:T(128)} %bitcast.tensor_ref.refs_0_, bf16[32,1024]{1,0:T(8,128)(2,1)S(1)} %get-tuple-element.15.x_ref, bf16[1024,8192]{1,0:T(8,128)(2,1)} %weight.5), custom_call_target="tpu_custom_call" | custom-call | flops 201326592 | bytes 6291456 | tf_op jit(solution)/shard_map/pallas_call | solution.py:238
  42.6 0.6 %collective-permute-start.14 = (bf16[64,1024]{1,0:T(8,128)(2,1)S(1)}, bf16[64,1024]{1,0:T(8,128)(2,1)S(1)}, u32[]{:S(2)}, u32[]{:S(2)}) collective-permute-start(bf16[64,1024]{1,0:T(8,128)(2,1)S(1)} %get-tuple-element.18), channel_id=1, source_target_pairs={{0,1},{1,0},{2,3},{3,2},{4,5},{5,4},{6,7},{7,6},{8,9},{9,8},{10,11... | collective-permute-start | bytes 393224 | tf_op jit(solution)/shard_map/ppermute | solution.py:302
  43.2 0.0 collective-permute-done.12.rest_2_
  43.2 0.5 collective-permute-start.13
  43.7 0.0 copy-done.3
  43.7 0.0 collective-permute-start.11
  43.7 3.3 %shard_map.121 = (f32[32,1024]{1,0:T(8,128)S(1)}, f32[32,1024]{1,0:T(8,128)S(1)}, bf16[32,1024]{1,0:T(8,128)(2,1)S(1)}) custom-call(s32[1]{0:T(128)} %bitcast.tensor_ref.refs_0_, bf16[32,1024]{1,0:T(8,128)(2,1)S(1)} %get-tuple-element.15.x_ref, bf16[1024,8192]{1,0:T(8,128)(2,1)} %weight.5), custom_call_target="tpu_custom_call" | custom-call | flops 201326592 | bytes 6291456 | tf_op jit(solution)/shard_map/pallas_call | solution.py:238
  47.0 0.6 %collective-permute-done.14 = bf16[64,1024]{1,0:T(8,128)(2,1)S(1)} collective-permute-done((bf16[64,1024]{1,0:T(8,128)(2,1)S(1)}, bf16[64,1024]{1,0:T(8,128)(2,1)S(1)}, u32[]{:S(2)}, u32[]{:S(2)}) %collective-permute-start.14) | collective-permute-done | bytes 131104 | tf_op jit(solution)/shard_map/ppermute | solution.py:302
  47.6 0.0 collective-permute-done.13.rest_3_
  47.7 0.3 collective-permute-start.15
  48.1 1.5 %collective-permute-start.16 = (bf16[32,1024]{1,0:T(8,128)(2,1)S(1)}, bf16[32,1024]{1,0:T(8,128)(2,1)S(1)}, u32[]{:S(2)}, u32[]{:S(2)}) collective-permute-start(bf16[32,1024]{1,0:T(8,128)(2,1)S(1)} %get-tuple-element.19), channel_id=1, source_target_pairs={{0,1},{1,0},{2,3},{3,2},{4,5},{5,4},{6,7},{7,6},{8,9},{9,8},{10,11... | collective-permute-start | bytes 196616 | tf_op jit(solution)/shard_map/ppermute | solution.py:302
  49.6 1.1 %collective-permute-start.17 = (bf16[32,1024]{1,0:T(8,128)(2,1)S(1)}, bf16[32,1024]{1,0:T(8,128)(2,1)S(1)}, u32[]{:S(2)}, u32[]{:S(2)}) collective-permute-start(bf16[32,1024]{1,0:T(8,128)(2,1)S(1)} %get-tuple-element.23), channel_id=1, source_target_pairs={{0,2},{1,3},{2,0},{3,1},{4,6},{5,7},{6,4},{7,5},{8,10},{9,11},{10,... | collective-permute-start | bytes 196616 | tf_op jit(solution)/shard_map/ppermute | solution.py:302
  50.6 2.0 %shard_map.122.rest_5_ = f32[32,1024]{1,0:T(8,128)S(1)} custom-call(s32[1]{0:T(128)} %bitcast.tensor_ref.refs_0_, bf16[32,1024]{1,0:T(8,128)(2,1)S(1)} %get-tuple-element.15.x_ref, bf16[1024,8192]{1,0:T(8,128)(2,1)} %weight.5), custom_call_target="tpu_custom_call" | custom-call | flops 67108864 | bytes 2097152 | tf_op jit(solution)/shard_map/pallas_call | solution.py:238
  52.7 0.0 collective-permute-done.11.rest_1_
  52.7 0.0 collective-permute-done.16.rest_6_
  52.7 1.3 %collective-permute-done.17.rest_7_ = bf16[32,1024]{1,0:T(8,128)(2,1)S(1)} collective-permute-done((bf16[32,1024]{1,0:T(8,128)(2,1)S(1)}, bf16[32,1024]{1,0:T(8,128)(2,1)S(1)}, u32[]{:S(2)}, u32[]{:S(2)}) %collective-permute-start.17) | collective-permute-done | bytes 65568 | tf_op jit(solution)/shard_map/ppermute | solution.py:302
  54.0 0.7 %collective-permute-done.15.rest_4_ = bf16[32,1152]{1,0:T(8,128)(2,1)S(1)} collective-permute-done((bf16[32,1152]{1,0:T(8,128)(2,1)S(1)}, bf16[32,1152]{1,0:T(8,128)(2,1)S(1)}, u32[]{:S(2)}, u32[]{:S(2)}) %collective-permute-start.15) | collective-permute-done | bytes 73760 | tf_op jit(solution)/shard_map/ppermute | solution.py:302
  54.6 1.0 %final.1 = bf16[32,1024]{1,0:T(8,128)(2,1)} custom-call(f32[32,512]{1,0:T(8,128)S(1)} %add_convert_fusion.3.picks_ref.refs_6_, f32[32,128]{1,0:T(8,128)S(1)} %get-tuple-element.13.low_ref, bf16[256,1024]{1,0:T(8,128)(2,1)S(1)} %bitcast.10, bf16[256,1024]{1,0:T(8,128)(2,1)S(1)} %collective-permute-done.11.rest_1_, ...), custom_call_target="tpu_custom_call" | custom-call | flops 100000000 | bytes 1000000 | tf_op jit(solution)/shard_map/final/pallas_call | solution.py:446
  (16 shorter events, 0.1 us)
Async XLA Ops:
  0.0 30.0 %collective-permute-start.6 = (bf16[32,1024]{1,0:T(8,128)(2,1)}, bf16[32,1024]{1,0:T(8,128)(2,1)S(1)}, u32[]{:S(2)}, u32[]{:S(2)}) collective-permute-start(bf16[32,1024]{1,0:T(8,128)(2,1)} %rest_0_.1), channel_id=1, source_target_pairs={{0,1},{1,0},{2,3},{3,2},{4,5},{5,4},{6,7},{7,6},{8,9},{9,8},{10,11... | collective-permute-start | bytes 196616 | tf_op jit(solution)/shard_map/ppermute | solution.py:302
  3.0 13.5 %collective-permute-start = (bf16[32,1024]{1,0:T(8,128)(2,1)}, bf16[32,1024]{1,0:T(8,128)(2,1)S(1)}, u32[]{:S(2)}, u32[]{:S(2)}) collective-permute-start(bf16[32,1024]{1,0:T(8,128)(2,1)} %rest_0_.1), channel_id=1, source_target_pairs={{0,4},{1,5},{2,6},{3,7},{4,0},{5,1},{6,2},{7,3},{8,12},{9,13},{10,... | collective-permute-start | bytes 196616 | tf_op jit(solution)/shard_map/ppermute | solution.py:302
  5.6 11.4 %collective-permute-start.7 = (bf16[32,1024]{1,0:T(8,128)(2,1)}, bf16[32,1024]{1,0:T(8,128)(2,1)S(1)}, u32[]{:S(2)}, u32[]{:S(2)}) collective-permute-start(bf16[32,1024]{1,0:T(8,128)(2,1)} %rest_0_.1), channel_id=1, source_target_pairs={{0,2},{1,3},{2,0},{3,1},{4,6},{5,7},{6,4},{7,5},{8,10},{9,11},{10,... | collective-permute-start | bytes 196616 | tf_op jit(solution)/shard_map/ppermute | solution.py:302
  7.2 2.1 %collective-permute-start.2 = (bf16[256,1024]{1,0:T(8,128)(2,1)}, bf16[256,1024]{1,0:T(8,128)(2,1)S(1)}, u32[]{:S(2)}, u32[]{:S(2)}) collective-permute-start(bf16[256,1024]{1,0:T(8,128)(2,1)} %bitcast.11), channel_id=1, source_target_pairs={{0,8},{8,0},{1,9},{9,1},{2,10},{10,2},{3,11},{11,3},{4,12},{12,4},... | collective-permute-start | bytes 1572872 | tf_op jit(solution)/shard_map/ppermute | solution.py:307
  7.2 26.7 %collective-permute-start.9 = (bf16[256,1024]{1,0:T(8,128)(2,1)}, bf16[256,1024]{1,0:T(8,128)(2,1)S(1)}, u32[]{:S(2)}, u32[]{:S(2)}) collective-permute-start(bf16[256,1024]{1,0:T(8,128)(2,1)} %bitcast.5), channel_id=1, source_target_pairs={{0,8},{8,0},{1,9},{9,1},{2,10},{10,2},{3,11},{11,3},{4,12},{12,4},... | collective-permute-start | bytes 1572872 | tf_op jit(solution)/shard_map/ppermute | solution.py:307
  9.3 1.0 %copy-start.4 = (bf16[4,64,1024]{2,1,0:T(8,128)(2,1)S(1)}, bf16[4,64,1024]{2,1,0:T(8,128)(2,1)}, u32[]{:S(2)}) copy-start(bf16[4,64,1024]{2,1,0:T(8,128)(2,1)} %param.17) | copy-start | bytes 1572868
  10.3 0.8 %copy-start.5 = (bf16[32,1024]{1,0:T(8,128)(2,1)S(1)}, bf16[32,1024]{1,0:T(8,128)(2,1)}, u32[]{:S(2)}) copy-start(bf16[32,1024]{1,0:T(8,128)(2,1)} %rest_0_.1) | copy-start | bytes 196612
  11.8 4.8 %collective-permute-start.3 = (f32[32,128]{1,0:T(8,128)S(1)}, f32[32,128]{1,0:T(8,128)S(1)}, u32[]{:S(2)}, u32[]{:S(2)}) collective-permute-start(f32[32,128]{1,0:T(8,128)S(1)} %low.1), channel_id=1, source_target_pairs={{0,4},{1,5},{2,6},{3,7},{4,0},{5,1},{6,2},{7,3},{8,12},{9,13},{10,... | collective-permute-start | bytes 49160 | tf_op jit(solution)/shard_map/ppermute | solution.py:302
  16.5 17.3 %collective-permute-start.10 = (bf16[256,1024]{1,0:T(8,128)(2,1)}, bf16[256,1024]{1,0:T(8,128)(2,1)S(1)}, u32[]{:S(2)}, u32[]{:S(2)}) collective-permute-start(bf16[256,1024]{1,0:T(8,128)(2,1)} %bitcast.7), channel_id=1, source_target_pairs={{0,8},{8,0},{1,9},{9,1},{2,10},{10,2},{3,11},{11,3},{4,12},{12,4},... | collective-permute-start | bytes 1572872 | tf_op jit(solution)/shard_map/ppermute | solution.py:307
  16.5 3.8 %collective-permute-start.4 = (f32[32,128]{1,0:T(8,128)S(1)}, f32[32,128]{1,0:T(8,128)S(1)}, u32[]{:S(2)}, u32[]{:S(2)}) collective-permute-start(f32[32,128]{1,0:T(8,128)S(1)} %add.86), channel_id=1, source_target_pairs={{0,2},{1,3},{2,0},{3,1},{4,6},{5,7},{6,4},{7,5},{8,10},{9,11},{10,... | collective-permute-start | bytes 49160 | tf_op jit(solution)/shard_map/ppermute | solution.py:302
  17.0 13.0 %collective-permute-start.8 = (bf16[64,1024]{1,0:T(8,128)(2,1)S(1)}, bf16[64,1024]{1,0:T(8,128)(2,1)S(1)}, u32[]{:S(2)}, u32[]{:S(2)}) collective-permute-start(bf16[64,1024]{1,0:T(8,128)(2,1)S(1)} %pad_maximum_fusion), channel_id=1, source_target_pairs={{0,1},{1,0},{2,3},{3,2},{4,5},{5,4},{6,7},{7,6},{8,9},{9,8},{10,11... | collective-permute-start | bytes 393224 | tf_op jit(solution)/shard_map/ppermute | solution.py:302
  20.3 4.3 %collective-permute-start.1 = (bf16[32,1024]{1,0:T(8,128)(2,1)S(1)}, bf16[32,1024]{1,0:T(8,128)(2,1)S(1)}, u32[]{:S(2)}, u32[]{:S(2)}) collective-permute-start(bf16[32,1024]{1,0:T(8,128)(2,1)S(1)} %collective-permute-done.rest_1_), channel_id=1, source_target_pairs={{0,2},{1,3},{2,0},{3,1},{4,6},{5,7},{6,4},{7,5},{8,10},{9,11},{10,... | collective-permute-start | bytes 196616 | tf_op jit(solution)/shard_map/ppermute | solution.py:302
  24.6 9.2 %collective-permute-start.5 = (bf16[32,1152]{1,0:T(8,128)(2,1)S(1)}, bf16[32,1152]{1,0:T(8,128)(2,1)S(1)}, u32[]{:S(2)}, u32[]{:S(2)}) collective-permute-start(bf16[32,1152]{1,0:T(8,128)(2,1)S(1)} %pad_maximum_fusion.1), channel_id=1, source_target_pairs={{0,1},{1,0},{2,3},{3,2},{4,5},{5,4},{6,7},{7,6},{8,9},{9,8},{10,11... | collective-permute-start | bytes 221192 | tf_op jit(solution)/shard_map/ppermute | solution.py:302
  25.9 0.8 %copy-start.6 = (bf16[32,1024]{1,0:T(8,128)(2,1)S(1)}, bf16[32,1024]{1,0:T(8,128)(2,1)}, u32[]{:S(2)}) copy-start(bf16[32,1024]{1,0:T(8,128)(2,1)} %rest_0_.1) | copy-start | bytes 196612
  26.7 7.2 %copy-start = (bf16[32,8,32,128]{3,2,1,0:T(8,128)(2,1)S(1)}, bf16[32,8,32,128]{3,2,1,0:T(8,128)(2,1)}, u32[]{:S(2)}) copy-start(bf16[32,8,32,128]{3,2,1,0:T(8,128)(2,1)} %refs_11_.1) | copy-start | bytes 6291460
  26.7 7.2 %copy-start.1 = (bf16[4,64,1024]{2,1,0:T(8,128)(2,1)S(1)}, bf16[4,64,1024]{2,1,0:T(8,128)(2,1)}, u32[]{:S(2)}) copy-start(bf16[4,64,1024]{2,1,0:T(8,128)(2,1)} %param.18) | copy-start | bytes 1572868
  26.7 7.2 %copy-start.2 = (bf16[4,64,1024]{2,1,0:T(8,128)(2,1)S(1)}, bf16[4,64,1024]{2,1,0:T(8,128)(2,1)}, u32[]{:S(2)}) copy-start(bf16[4,64,1024]{2,1,0:T(8,128)(2,1)} %param.19) | copy-start | bytes 1572868
  37.7 6.0 %copy-start.3 = (bf16[4,64,1024]{2,1,0:T(8,128)(2,1)S(1)}, bf16[4,64,1024]{2,1,0:T(8,128)(2,1)}, u32[]{:S(2)}) copy-start(bf16[4,64,1024]{2,1,0:T(8,128)(2,1)} %param.20) | copy-start | bytes 1572868
  37.7 5.5 %collective-permute-start.12 = (bf16[32,1152]{1,0:T(8,128)(2,1)S(1)}, bf16[32,1152]{1,0:T(8,128)(2,1)S(1)}, u32[]{:S(2)}, u32[]{:S(2)}) collective-permute-start(bf16[32,1152]{1,0:T(8,128)(2,1)S(1)} %get-tuple-element.14), channel_id=1, source_target_pairs={{0,1},{1,0},{2,3},{3,2},{4,5},{5,4},{6,7},{7,6},{8,9},{9,8},{10,11... | collective-permute-start | bytes 221192 | tf_op jit(solution)/shard_map/ppermute | solution.py:302
  42.6 5.0 %collective-permute-start.14 = (bf16[64,1024]{1,0:T(8,128)(2,1)S(1)}, bf16[64,1024]{1,0:T(8,128)(2,1)S(1)}, u32[]{:S(2)}, u32[]{:S(2)}) collective-permute-start(bf16[64,1024]{1,0:T(8,128)(2,1)S(1)} %get-tuple-element.18), channel_id=1, source_target_pairs={{0,1},{1,0},{2,3},{3,2},{4,5},{5,4},{6,7},{7,6},{8,9},{9,8},{10,11... | collective-permute-start | bytes 393224 | tf_op jit(solution)/shard_map/ppermute | solution.py:302
  43.2 4.4 %collective-permute-start.13 = (bf16[32,1152]{1,0:T(8,128)(2,1)S(1)}, bf16[32,1152]{1,0:T(8,128)(2,1)S(1)}, u32[]{:S(2)}, u32[]{:S(2)}) collective-permute-start(bf16[32,1152]{1,0:T(8,128)(2,1)S(1)} %pad_maximum_fusion.2), channel_id=1, source_target_pairs={{0,2},{1,3},{2,0},{3,1},{4,6},{5,7},{6,4},{7,5},{8,10},{9,11},{10,... | collective-permute-start | bytes 221192 | tf_op jit(solution)/shard_map/ppermute | solution.py:302
  43.7 9.0 %collective-permute-start.11 = (bf16[256,1024]{1,0:T(8,128)(2,1)S(1)}, bf16[256,1024]{1,0:T(8,128)(2,1)S(1)}, u32[]{:S(2)}, u32[]{:S(2)}) collective-permute-start(bf16[256,1024]{1,0:T(8,128)(2,1)S(1)} %bitcast.9), channel_id=1, source_target_pairs={{0,8},{8,0},{1,9},{9,1},{2,10},{10,2},{3,11},{11,3},{4,12},{12,4},... | collective-permute-start | bytes 1572872 | tf_op jit(solution)/shard_map/ppermute | solution.py:307
  47.7 6.9 %collective-permute-start.15 = (bf16[32,1152]{1,0:T(8,128)(2,1)S(1)}, bf16[32,1152]{1,0:T(8,128)(2,1)S(1)}, u32[]{:S(2)}, u32[]{:S(2)}) collective-permute-start(bf16[32,1152]{1,0:T(8,128)(2,1)S(1)} %pad_maximum_fusion.3), channel_id=1, source_target_pairs={{0,4},{1,5},{2,6},{3,7},{4,0},{5,1},{6,2},{7,3},{8,12},{9,13},{10,... | collective-permute-start | bytes 221192 | tf_op jit(solution)/shard_map/ppermute | solution.py:302
  48.1 4.6 %collective-permute-start.16 = (bf16[32,1024]{1,0:T(8,128)(2,1)S(1)}, bf16[32,1024]{1,0:T(8,128)(2,1)S(1)}, u32[]{:S(2)}, u32[]{:S(2)}) collective-permute-start(bf16[32,1024]{1,0:T(8,128)(2,1)S(1)} %get-tuple-element.19), channel_id=1, source_target_pairs={{0,1},{1,0},{2,3},{3,2},{4,5},{5,4},{6,7},{7,6},{8,9},{9,8},{10,11... | collective-permute-start | bytes 196616 | tf_op jit(solution)/shard_map/ppermute | solution.py:302
  49.6 4.4 %collective-permute-start.17 = (bf16[32,1024]{1,0:T(8,128)(2,1)S(1)}, bf16[32,1024]{1,0:T(8,128)(2,1)S(1)}, u32[]{:S(2)}, u32[]{:S(2)}) collective-permute-start(bf16[32,1024]{1,0:T(8,128)(2,1)S(1)} %get-tuple-element.23), channel_id=1, source_target_pairs={{0,2},{1,3},{2,0},{3,1},{4,6},{5,7},{6,4},{7,5},{8,10},{9,11},{10,... | collective-permute-start | bytes 196616 | tf_op jit(solution)/shard_map/ppermute | solution.py:302
where the time goes:
time: 56 us; the launch traced here: 55.7 us
  Pallas kernels  21.2 us (38%)
  starting transfers between devices  15.5 us (28%)
  waiting for transfers between devices  14.2 us (25%)
  local copies, waits for them, and re-layouts  2.81 us (5%)
  other arithmetic  1.72 us (3%)
    ppermute x14, starting transfers between devices, across(): return lax.ppermute(x, 'tensor', [(i, i ^ bit) for i in range(shards)])  15 us
    ppermute x14, waiting for transfers between devices, across(): return lax.ppermute(x, 'tensor', [(i, i ^ bit) for i in range(shards)])  13.5 us
    pallas_call x3, Pallas kernels, out_call(): pl.pallas_call(functools.partial(out_kernel, ks, spans), in_specs=[SMEM,...  8.72 us
    pallas_call x2, Pallas kernels, project_call(): pl.pallas_call(functools.partial(project_kernel, ks, spans, before is Non...  7.06 us
    pallas_call x1, Pallas kernels, per_device(): pl.pallas_call(functools.partial(mix_kernel, sizes), in_specs=[SMEM, VMEM...  3.75 us
    unnamed x14, local copies, waits for them, and re-layouts  2.73 us
  transfers between devices with their start and end apart: 18, of which 7 were waited for; matrix products, arithmetic and copies ran while one was open for 3% of the time, Pallas kernels for 29%

commit v1 on v0

--- a/solution.py
+++ b/solution.py
@@ -15,7 +15,7 @@
 HBM = pl.BlockSpec(memory_space=pltpu.HBM)
 LANES = 128
 PIECES = 2
-GRANT = 49 << 20
+GRANT = 24 << 20
 
 
 def dot(a, b):
@@ -59,6 +59,10 @@
     return total
 
 
+def in_hbm(x):
+    return pltpu.with_memory_space_constraint(x, pltpu.HBM)
+
+
 def load_all(pairs, sems):
     copies = [pltpu.make_async_copy(src, dst, sems.at[i]) for i, (src, dst) in enumerate(pairs)]
     for c in copies:
@@ -67,7 +71,7 @@
 
 
 def low_kernel(count, x_hbm, picks_ref, *rest):
-    downs, out_ref, x_ref, bufs, sems = rest[:count], rest[count], rest[count + 1], rest[count + 2 : -1], rest[-1]
+    downs, (out_ref, x_ref), bufs, sems = rest[:count], rest[count : count + 2], rest[count + 2 : -1], rest[-1]
     for c in load_all([(x_hbm, x_ref)] + list(zip(downs, bufs)), sems):
         c.wait()
     out_ref[...] = low_of(x_ref[...], bufs, picks_ref[...])
@@ -77,14 +81,16 @@
     return pl.pallas_call(
         functools.partial(low_kernel, len(downs)),
         in_specs=[HBM, VMEM] + [HBM] * len(downs),
-        out_specs=VMEM,
-        out_shape=jax.ShapeDtypeStruct((x.shape[0], LANES), jnp.float32),
-        scratch_shapes=[pltpu.VMEM(x.shape, x.dtype)]
-        + [pltpu.VMEM(d.shape, d.dtype) for d in downs]
+        out_specs=[VMEM] * 2,
+        out_shape=[
+            jax.ShapeDtypeStruct((x.shape[0], LANES), jnp.float32),
+            jax.ShapeDtypeStruct(x.shape, x.dtype),
+        ],
+        scratch_shapes=[pltpu.VMEM(d.shape, d.dtype) for d in downs]
         + [pltpu.SemaphoreType.DMA((1 + len(downs),))],
         name="low",
         **params((10**8, 10**6)),
-    )(x, picks, *downs)
+    )(in_hbm(x), picks, in_hbm(downs[0]), *downs[1:])
 
 
 def weight_copies(weight, buf, sems, j, block, along):
@@ -155,30 +161,34 @@
         **params(
             (2 * count * rows * width * wide, 2 * count * width * wide),
         ),
-    )(tensor_at, *arrays, weight, *extra)
+    )(tensor_at, *arrays, in_hbm(weight), *extra)
 
 
 def mix_kernel(sizes, *refs):
-    k_in, k_out, maps, kv_count, group, head, local_heads, group_all, _ = sizes
+    k_in, k_outs, maps, kv_count, group, head, local_heads, group_all, _ = sizes
     refs = list(refs)
     tensor_ref, chunk, w_in, w_out, before, low, picks = [refs.pop(0) for _ in range(7)]
     ups = [refs.pop(0) for _ in range(maps)]
     downs = [refs.pop(0) for _ in range(maps)]
     keys, values, live = [refs.pop(0) for _ in range(3)]
-    block_out, low_out, mixed_out = [refs.pop(0) for _ in range(3)]
+    low_out, mixed_out, block_out = [refs.pop(0) for _ in range(3)]
+    more_outs = [refs.pop(0) for _ in k_outs[1:]]
     buf_in, sem_in, buf_out, sem_out, k_buf, v_buf, up_buf, down_buf, sems = refs
 
     tensor_at = tensor_ref[0]
     copies_in = weight_copies(w_in, buf_in, sem_in, 0, tensor_at ^ k_in, 0)
-    copies_out = weight_copies(w_out, buf_out, sem_out, 0, tensor_at ^ k_out, 1)
+    copies_out = [
+        weight_copies(w_out, buf_out, sem_out, j, tensor_at ^ k, 1) for j, k in enumerate(k_outs)
+    ]
     kv = pl.ds(tensor_at * local_heads // group_all, kv_count)
     up_copies = load_all([(u, up_buf.at[i]) for i, u in enumerate(ups)], sems.at[0])
     for c in copies_in:
         c.start()
     kv_copies = load_all([(keys.at[:, kv], k_buf), (values.at[:, kv], v_buf)], sems.at[1])
     down_copies = load_all([(d, down_buf.at[i]) for i, d in enumerate(downs)], sems.at[2])
-    for c in copies_out:
-        c.start()
+    for pieces in copies_out:
+        for c in pieces:
+            c.start()
 
     rows = before.shape[0]
     picked = picks[...]
@@ -213,10 +223,14 @@
         c.wait()
     low_part = low_of(mixed, [down_buf.at[i] for i in range(maps)], picked)
     low_out[...] = low_part
-    block = block_dot(lambda a, n: mixed[:, a : a + n], buf_out, 0, copies_out, 0.0)
+    block = block_dot(lambda a, n: mixed[:, a : a + n], buf_out, 0, copies_out[0], 0.0)
     wide = block.shape[1]
     block_out[:, :wide] = block.astype(block_out.dtype)
     block_out[:, wide:] = low_part.astype(block_out.dtype)
+    for j, ref in enumerate(more_outs):
+        ref[...] = block_dot(
+            lambda a, n: mixed[:, a : a + n], buf_out, j + 1, copies_out[j + 1], 0.0
+        )
 
 
 def out_kernel(ks, spans, tensor_ref, x_ref, weight, *rest):
@@ -245,7 +259,7 @@
             pltpu.SemaphoreType.DMA((len(ks), PIECES)),
         ],
         **params((2 * len(ks) * rows * depth * out_width, 2 * len(ks) * depth * out_width)),
-    )(tensor_at, mixed, weight)
+    )(tensor_at, mixed, in_hbm(weight))
 
 
 def final_kernel(wide, count, maps, picks_ref, low_ref, *rest):
@@ -328,29 +342,27 @@
     output_down = with_swapped(output_down_maps)
     output_up = with_swapped(output_up_maps)
 
-    low = low_call(hidden, picks, query_down)
-    where = {0: (hidden, 0)}
+    low, near = low_call(hidden, picks, query_down)
+    where = {0: (near, 0)}
     chain = 0
     for bit in reversed(bits):
-        held = list(where)
-        if bit != 1:
-            for k in held:
-                where[k | bit] = (across(where[k][0], bit), 0)
+        rest = [k for k in where if k not in (0, chain)]
+        where[bit] = (across(hidden, bit), 0)
+        if chain:
+            joined = jnp.concatenate([where[chain][0][:, :width], low.astype(jnp.bfloat16)], axis=1)
+            got = across(joined, bit)
+            where[chain | bit] = (got, 0)
+            low = low + got[:, width:].astype(jnp.float32)
+        else:
             low = low + across(low, bit)
+        if rest and bit == 1:
+            got = jnp.concatenate([where[k][0][:, :width] for k in rest], axis=0)
+            got = across(got, 1)
+            for i, k in enumerate(rest):
+                where[k | 1] = (got, i * rows)
         else:
-            where[1] = (across(hidden, 1), 0)
-            rest = [k for k in held if k not in (0, chain)]
-            if rest:
-                got = across(jnp.concatenate([where[k][0] for k in rest], axis=0), 1)
-                for i, k in enumerate(rest):
-                    where[k | 1] = (got, i * rows)
-            if chain:
-                joined = jnp.concatenate([where[chain][0], low.astype(jnp.bfloat16)], axis=1)
-                got = across(joined, 1)
-                where[chain | 1] = (got, 0)
-                low = low + got[:, width:].astype(jnp.float32)
-            else:
-                low = low + across(low, 1)
+            for k in rest:
+                where[k | bit] = (across(where[k][0][:, :width], bit), 0)
         chain |= bit
 
     top = bits[-1] if bits else 0
@@ -371,22 +383,25 @@
     out_width = output_weight.shape[1] // shards
     depth = output_weight.shape[0]
     whole = shards - 1
-    sizes = (last, whole, replicas, kv_count, group, head, local_heads, group_all, width)
+    even = [k for k in sorted(where, reverse=True) if not k & 1]
+    k_outs = [whole] + even[:-1][:1]
+    sizes = (last, k_outs, replicas, kv_count, group, head, local_heads, group_all, width)
     map_in, map_out = (stored * rank, wide), (stored * rank, depth)
-    payload, low2, mixed = pl.pallas_call(
+    low2, mixed, payload, *blocks = pl.pallas_call(
         functools.partial(mix_kernel, sizes),
         in_specs=[SMEM, VMEM, HBM, HBM, VMEM, VMEM, VMEM] + [HBM] * (2 * replicas) + [HBM, HBM, VMEM],
-        out_specs=[VMEM] * 3,
+        out_specs=[VMEM] * (2 + len(k_outs)),
         out_shape=[
-            jax.ShapeDtypeStruct((rows, out_width + LANES), jnp.bfloat16),
             jax.ShapeDtypeStruct((rows, LANES), jnp.float32),
             jax.ShapeDtypeStruct((rows, wide), jnp.bfloat16),
-        ],
+            jax.ShapeDtypeStruct((rows, out_width + LANES), jnp.bfloat16),
+        ]
+        + [jax.ShapeDtypeStruct((rows, out_width), jnp.float32)] * (len(k_outs) - 1),
         scratch_shapes=[
             pltpu.VMEM((1, width, wide), w_query.dtype),
             pltpu.SemaphoreType.DMA((1, PIECES)),
-            pltpu.VMEM((1, depth, out_width), output_weight.dtype),
-            pltpu.SemaphoreType.DMA((1, PIECES)),
+            pltpu.VMEM((len(k_outs), depth, out_width), output_weight.dtype),
+            pltpu.SemaphoreType.DMA((len(k_outs), PIECES)),
             pltpu.VMEM((rows, kv_count, length, head), keys.dtype),
             pltpu.VMEM((rows, kv_count, length, head), values.dtype),
             pltpu.VMEM((replicas,) + map_in, keys.dtype),
@@ -398,15 +413,15 @@
     )(
         tensor_at,
         where[last][0],
-        w_query,
-        output_weight,
+        in_hbm(w_query),
+        in_hbm(output_weight),
         query,
         low,
         picks,
         *query_up,
         *output_down,
-        keys,
-        values,
+        in_hbm(keys),
+        in_hbm(values),
         live,
     )
 
@@ -415,11 +430,15 @@
     while chain[-1]:
         chain.append(chain[-1] & (chain[-1] - 1))
     odd = [k for k in sorted(where, reverse=True) if k & 1 and k not in (whole, 1)]
-    even = [k for k in sorted(where, reverse=True) if not k & 1]
     f32, bf16 = jnp.float32, jnp.bfloat16
-    plan = [([k], f32) for k in even[:1]] + [(odd, bf16)] * bool(odd)
-    plan = [plan, [([k], f32) for k in even[1:-1]] + [([1], bf16)], [([k], f32) for k in even[-1:]]]
-    parts = {}
+    parts = dict(zip(k_outs[1:], blocks))
+    even = [k for k in even if k not in parts]
+    plan = [
+        [(odd, bf16)] * bool(odd),
+        [([k], f32) for k in even[:-1]] + [([1], bf16)] * (whole > 1),
+        [([k], f32) for k in even[-1:]],
+    ]
+    plan = [groups for groups in plan if groups]
     for groups in plan:
         arrays = out_call(groups, tensor_at, mixed, output_weight, out_width)
         for (g, kind), array in zip(groups, arrays):

time: 56 us -> 50.8 us (0.907)
  waiting for transfers between devices: 14.2 us -> 11.3 us
  local copies, waits for them, and re-layouts: 2.81 us -> 0.1 us
  Pallas kernels: 21.2 us -> 22 us
    ppermute x14 -> x13, waiting for transfers between devices: 13.5 us -> 10.6 us  [across(): return lax.ppermute(x, 'tensor', [(i, i ^ bit) for i in range(shards)])]
    unnamed x14 -> x6, local copies, waits for them, and re-layouts: 2.73 us -> 0.02 us
    pallas_call x1, Pallas kernels: 0.58 us -> 1.53 us  [low_call(): pl.pallas_call(functools.partial(low_kernel, len(downs)), in_specs=[HBM,...]
    pallas_call x3, Pallas kernels: 8.72 us -> 8.07 us  [out_call(): pl.pallas_call(functools.partial(out_kernel, ks, spans), in_specs=[SMEM,...]
    pallas_call x1, Pallas kernels: 3.75 us -> 4.39 us  [per_device(): pl.pallas_call(functools.partial(mix_kernel, sizes), in_specs=[SMEM, VMEM...]
    ppermute x14 -> x13, starting transfers between devices: 15 us -> 14.7 us  [across(): return lax.ppermute(x, 'tensor', [(i, i ^ bit) for i in range(shards)])]
  transfers between devices with their start and end apart: 18 -> 17, of which waited for: 7 -> 6; matrix products, arithmetic and copies ran while one was open for 3% -> 4% of each run, Pallas kernels for 29% -> 33%
where the time goes in v1:
time: 50.8 us; the launch traced here: 50.6 us
  Pallas kernels  22 us (43%)
  starting transfers between devices  15.2 us (30%)
  waiting for transfers between devices  11.3 us (22%)
  other arithmetic  1.74 us (3%)
    ppermute x13, starting transfers between devices, across(): return lax.ppermute(x, 'tensor', [(i, i ^ bit) for i in range(shards)])  14.7 us
    ppermute x13, waiting for transfers between devices, across(): return lax.ppermute(x, 'tensor', [(i, i ^ bit) for i in range(shards)])  10.6 us
    pallas_call x3, Pallas kernels, out_call(): pl.pallas_call(functools.partial(out_kernel, ks, spans), in_specs=[SMEM,...  8.07 us
    pallas_call x2, Pallas kernels, project_call(): pl.pallas_call(functools.partial(project_kernel, ks, spans, before is Non...  7.01 us
    pallas_call x1, Pallas kernels, per_device(): pl.pallas_call(functools.partial(mix_kernel, sizes), in_specs=[SMEM, VMEM...  4.39 us
    pallas_call x1, Pallas kernels, low_call(): pl.pallas_call(functools.partial(low_kernel, len(downs)), in_specs=[HBM,...  1.53 us
    pallas_call x1, Pallas kernels, per_device(): pl.pallas_call(functools.partial(final_kernel, out_width, (len(lows), len...  1.05 us
  transfers between devices with their start and end apart: 17, of which 6 were waited for; matrix products, arithmetic and copies ran while one was open for 4% of the time, Pallas kernels for 33%

profile of v1, /device:TPU:0, one launch (start us, length us, event | category | flops | bytes accessed | tf_op | source)
XLA Modules:
  0.0 50.6 jit_solution(15239592292452135385)
XLA Ops:
  0.0 4.1 %collective-permute-start = (bf16[32,1024]{1,0:T(8,128)(2,1)}, bf16[32,1024]{1,0:T(8,128)(2,1)S(1)}, u32[]{:S(2)}, u32[]{:S(2)}) collective-permute-start(bf16[32,1024]{1,0:T(8,128)(2,1)} %x_hbm.1), channel_id=1, source_target_pairs={{0,4},{1,5},{2,6},{3,7},{4,0},{5,1},{6,2},{7,3},{8,12},{9,13},{10,... | collective-permute-start | bytes 196616 | tf_op jit(solution)/shard_map/ppermute | solution.py:316
  4.1 1.6 %collective-permute-start.6 = (bf16[32,1024]{1,0:T(8,128)(2,1)}, bf16[32,1024]{1,0:T(8,128)(2,1)S(1)}, u32[]{:S(2)}, u32[]{:S(2)}) collective-permute-start(bf16[32,1024]{1,0:T(8,128)(2,1)} %x_hbm.1), channel_id=1, source_target_pairs={{0,2},{1,3},{2,0},{3,1},{4,6},{5,7},{6,4},{7,5},{8,10},{9,11},{10,... | collective-permute-start | bytes 196616 | tf_op jit(solution)/shard_map/ppermute | solution.py:316
  5.6 1.5 %collective-permute-start.5 = (bf16[32,1024]{1,0:T(8,128)(2,1)}, bf16[32,1024]{1,0:T(8,128)(2,1)S(1)}, u32[]{:S(2)}, u32[]{:S(2)}) collective-permute-start(bf16[32,1024]{1,0:T(8,128)(2,1)} %x_hbm.1), channel_id=1, source_target_pairs={{0,1},{1,0},{2,3},{3,2},{4,5},{5,4},{6,7},{7,6},{8,9},{9,8},{10,11... | collective-permute-start | bytes 196616 | tf_op jit(solution)/shard_map/ppermute | solution.py:316
  7.2 0.0 collective-permute-start.1
  7.2 0.5 %collective-permute-start.8 = (bf16[256,1024]{1,0:T(8,128)(2,1)}, bf16[256,1024]{1,0:T(8,128)(2,1)S(1)}, u32[]{:S(2)}, u32[]{:S(2)}) collective-permute-start(bf16[256,1024]{1,0:T(8,128)(2,1)} %bitcast.5), channel_id=1, source_target_pairs={{0,8},{8,0},{1,9},{9,1},{2,10},{10,2},{3,11},{11,3},{4,12},{12,4},... | collective-permute-start | bytes 1572872 | tf_op jit(solution)/shard_map/ppermute | solution.py:321
  7.7 0.8 %select_reduce_fusion = s32[64]{0:T(128)S(1)} fusion(s32[8]{0:T(128)} %param.22, s32[64]{0:T(128)} %param.21), kind=kLoop, calls=%fused_computation.30 | loop fusion | flops 1472 | bytes 544 | tf_op jit(solution)/shard_map/reduce_sum | solution.py:326
  8.4 0.1 dynamic_slice.3
  8.5 0.1 broadcast_compare_fusion.1
  8.6 0.7 %collective-permute-done.1.rest_1_ = bf16[256,1024]{1,0:T(8,128)(2,1)S(1)} collective-permute-done((bf16[256,1024]{1,0:T(8,128)(2,1)}, bf16[256,1024]{1,0:T(8,128)(2,1)S(1)}, u32[]{:S(2)}, u32[]{:S(2)}) %collective-permute-start.1) | collective-permute-done | bytes 524320 | tf_op jit(solution)/shard_map/ppermute | solution.py:321
  9.3 1.5 %low.1 = (f32[32,128]{1,0:T(8,128)S(1)}, bf16[32,1024]{1,0:T(8,128)(2,1)S(1)}) custom-call(bf16[32,1024]{1,0:T(8,128)(2,1)} %x_hbm.1, f32[32,512]{1,0:T(8,128)S(1)} %add_convert_fusion.3.picks_ref.refs_6_, bf16[256,1024]{1,0:T(8,128)(2,1)} %bitcast.12, bf16[256,1024]{1,0:T(8,128)(2,1)S(1)} %collective-permute-done.1.rest_1_), custom_call_target="tpu_custom_call" | custom-call | flops 100000000 | bytes 1000000 | tf_op jit(solution)/shard_map/low/pallas_call | solution.py:81
  10.8 0.4 collective-permute-start.2
  11.2 4.4 %collective-permute-done.2 = f32[32,128]{1,0:T(8,128)S(1)} collective-permute-done((f32[32,128]{1,0:T(8,128)S(1)}, f32[32,128]{1,0:T(8,128)S(1)}, u32[]{:S(2)}, u32[]{:S(2)}) %collective-permute-start.2) | collective-permute-done | bytes 16416 | tf_op jit(solution)/shard_map/ppermute | solution.py:316
  15.6 0.0 collective-permute-start.9
  15.6 0.0 collective-permute-done.rest_1_
  15.6 0.5 collective-permute-start.3
  16.1 0.0 collective-permute-done.6.rest_2_
  16.1 0.6 %collective-permute-start.7 = (bf16[64,1024]{1,0:T(8,128)(2,1)S(1)}, bf16[64,1024]{1,0:T(8,128)(2,1)S(1)}, u32[]{:S(2)}, u32[]{:S(2)}) collective-permute-start(bf16[64,1024]{1,0:T(8,128)(2,1)S(1)} %pad_maximum_fusion), channel_id=1, source_target_pairs={{0,1},{1,0},{2,3},{3,2},{4,5},{5,4},{6,7},{7,6},{8,9},{9,8},{10,11... | collective-permute-start | bytes 393224 | tf_op jit(solution)/shard_map/ppermute | solution.py:316
  16.7 3.7 %collective-permute-done.3.rest_1_ = bf16[32,1152]{1,0:T(8,128)(2,1)S(1)} collective-permute-done((bf16[32,1152]{1,0:T(8,128)(2,1)S(1)}, bf16[32,1152]{1,0:T(8,128)(2,1)S(1)}, u32[]{:S(2)}, u32[]{:S(2)}) %collective-permute-start.3) | collective-permute-done | bytes 73760 | tf_op jit(solution)/shard_map/ppermute | solution.py:316
  20.4 0.6 %collective-permute-start.4 = (bf16[32,1152]{1,0:T(8,128)(2,1)S(1)}, bf16[32,1152]{1,0:T(8,128)(2,1)S(1)}, u32[]{:S(2)}, u32[]{:S(2)}) collective-permute-start(bf16[32,1152]{1,0:T(8,128)(2,1)S(1)} %pad_maximum_fusion.2), channel_id=1, source_target_pairs={{0,1},{1,0},{2,3},{3,2},{4,5},{5,4},{6,7},{7,6},{8,9},{9,8},{10,11... | collective-permute-start | bytes 221192 | tf_op jit(solution)/shard_map/ppermute | solution.py:316
  21.0 0.7 %fusion.1.refs_13_ = f32[32,1024]{1,0:T(8,128)S(1)} fusion(s32[32]{0:T(128)} %param.23, s32[1024]{0:T(1024)S(1)} %get-tuple-element.32, s32[1024]{0:T(1024)S(1)} %get-tuple-element.33, s32[1024]{0:T(1024)S(1)} %get-tuple-element.31, s32[1024]{0:T(1024)S(1)} %get-tuple-element.34, pred[1024]{0:T(1024)(128)(4,1)S(1)} %get-tuple-element.35, ...), kind=kLoop, calls=%fused_computation.7 | loop fusion | flops 196608 | bytes 149632 | tf_op jit(solution)/shard_map/convert_element_type | solution.py:338
  21.7 0.0 copy-start
  21.7 0.0 copy-start.1
  21.7 3.2 %shard_map.118.rest_4_ = f32[32,1024]{1,0:T(8,128)S(1)} custom-call(s32[1]{0:T(128)} %bitcast.tensor_ref.refs_0_, bf16[32,1024]{1,0:T(8,128)(2,1)S(1)} %get-tuple-element.15.rest_0_, bf16[32,1024]{1,0:T(8,128)(2,1)S(1)} %collective-permute-done.rest_1_, bf16[32,1024]{1,0:T(8,128)(2,1)S(1)} %collective-permute-done.6.rest_2_, bf16[8192,1024]{1,0:T(8,128)(2,1)} %refs_2_.1), custom_call_target="tpu_custom_call" | custom-call | flops 201326592 | bytes 6291456 | tf_op jit(solution)/shard_map/pallas_call | solution.py:152
  25.0 0.0 collective-permute-done.5.rest_0_
  25.0 0.0 collective-permute-done.7.rest_2_
  25.0 3.8 %shard_map.119.refs_4_ = f32[32,1024]{1,0:T(8,128)S(1)} custom-call(s32[1]{0:T(128)} %bitcast.tensor_ref.refs_0_, bf16[32,1024]{1,0:T(8,128)(2,1)S(1)} %collective-permute-done.5.rest_0_, bf16[32,1152]{1,0:T(8,128)(2,1)S(1)} %collective-permute-done.3.rest_1_, bf16[64,1024]{1,0:T(8,128)(2,1)S(1)} %collective-permute-done.7.rest_2_, ...), custom_call_target="tpu_custom_call" | custom-call | flops 268435456 | bytes 8388608 | tf_op jit(solution)/shard_map/pallas_call | solution.py:152
  28.8 0.0 collective-permute-done.4.refs_1_
  28.8 0.0 collective-permute-done.8.refs_8_
  28.8 0.0 collective-permute-done.9.refs_10_
  28.8 0.0 copy-done
  28.8 0.0 copy-done.1
  28.9 4.4 %mix.1 = (f32[32,128]{1,0:T(8,128)S(1)}, bf16[32,1024]{1,0:T(8,128)(2,1)S(1)}, bf16[32,1152]{1,0:T(8,128)(2,1)S(1)}, f32[32,1024]{1,0:T(8,128)S(1)}) custom-call(s32[1]{0:T(128)} %bitcast.tensor_ref.refs_0_, bf16[32,1152]{1,0:T(8,128)(2,1)S(1)} %collective-permute-done.4.refs_1_, bf16[8192,1024]{1,0:T(8,128)(2,1)} %refs_2_.1, bf16[1024,8192]{1,0:T(8,128)(2,1)} %weight.5, ...), custom_call_target="tpu_custom_call" | custom-call | flops 1000000000 | bytes 6291456 | tf_op jit(solution)/shard_map/mix/pallas_call | solution.py:390
  33.3 0.0 copy-start.2
  33.3 1.6 %collective-permute-start.11 = (bf16[32,1152]{1,0:T(8,128)(2,1)S(1)}, bf16[32,1152]{1,0:T(8,128)(2,1)S(1)}, u32[]{:S(2)}, u32[]{:S(2)}) collective-permute-start(bf16[32,1152]{1,0:T(8,128)(2,1)S(1)} %get-tuple-element.17), channel_id=1, source_target_pairs={{0,1},{1,0},{2,3},{3,2},{4,5},{5,4},{6,7},{7,6},{8,9},{9,8},{10,11... | collective-permute-start | bytes 221192 | tf_op jit(solution)/shard_map/ppermute | solution.py:316
  34.9 2.7 %shard_map.121 = bf16[64,1024]{1,0:T(8,128)(2,1)S(1)} custom-call(s32[1]{0:T(128)} %bitcast.tensor_ref.refs_0_, bf16[32,1024]{1,0:T(8,128)(2,1)S(1)} %get-tuple-element.19.x_ref, bf16[1024,8192]{1,0:T(8,128)(2,1)} %weight.5), custom_call_target="tpu_custom_call" | custom-call | flops 134217728 | bytes 4194304 | tf_op jit(solution)/shard_map/pallas_call | solution.py:252
  37.5 0.6 %collective-permute-start.13 = (bf16[64,1024]{1,0:T(8,128)(2,1)S(1)}, bf16[64,1024]{1,0:T(8,128)(2,1)S(1)}, u32[]{:S(2)}, u32[]{:S(2)}) collective-permute-start(bf16[64,1024]{1,0:T(8,128)(2,1)S(1)} %shard_map.121), channel_id=1, source_target_pairs={{0,1},{1,0},{2,3},{3,2},{4,5},{5,4},{6,7},{7,6},{8,9},{9,8},{10,11... | collective-permute-start | bytes 393224 | tf_op jit(solution)/shard_map/ppermute | solution.py:316
  38.1 0.0 collective-permute-done.11.rest_2_
  38.2 0.5 collective-permute-start.12
  38.6 0.0 copy-done.2
  38.6 0.0 collective-permute-start.10
  38.6 3.3 %shard_map.120 = (f32[32,1024]{1,0:T(8,128)S(1)}, f32[32,1024]{1,0:T(8,128)S(1)}, bf16[32,1024]{1,0:T(8,128)(2,1)S(1)}) custom-call(s32[1]{0:T(128)} %bitcast.tensor_ref.refs_0_, bf16[32,1024]{1,0:T(8,128)(2,1)S(1)} %get-tuple-element.19.x_ref, bf16[1024,8192]{1,0:T(8,128)(2,1)} %weight.5), custom_call_target="tpu_custom_call" | custom-call | flops 201326592 | bytes 6291456 | tf_op jit(solution)/shard_map/pallas_call | solution.py:252
  42.0 0.6 %collective-permute-done.13 = bf16[64,1024]{1,0:T(8,128)(2,1)S(1)} collective-permute-done((bf16[64,1024]{1,0:T(8,128)(2,1)S(1)}, bf16[64,1024]{1,0:T(8,128)(2,1)S(1)}, u32[]{:S(2)}, u32[]{:S(2)}) %collective-permute-start.13) | collective-permute-done | bytes 131104 | tf_op jit(solution)/shard_map/ppermute | solution.py:316
  42.6 0.0 collective-permute-done.12.rest_3_
  42.7 0.3 collective-permute-start.14
  43.0 1.5 %collective-permute-start.15 = (bf16[32,1024]{1,0:T(8,128)(2,1)S(1)}, bf16[32,1024]{1,0:T(8,128)(2,1)S(1)}, u32[]{:S(2)}, u32[]{:S(2)}) collective-permute-start(bf16[32,1024]{1,0:T(8,128)(2,1)S(1)} %get-tuple-element.21), channel_id=1, source_target_pairs={{0,1},{1,0},{2,3},{3,2},{4,5},{5,4},{6,7},{7,6},{8,9},{9,8},{10,11... | collective-permute-start | bytes 196616 | tf_op jit(solution)/shard_map/ppermute | solution.py:316
  44.5 1.1 %collective-permute-start.16 = (bf16[32,1024]{1,0:T(8,128)(2,1)S(1)}, bf16[32,1024]{1,0:T(8,128)(2,1)S(1)}, u32[]{:S(2)}, u32[]{:S(2)}) collective-permute-start(bf16[32,1024]{1,0:T(8,128)(2,1)S(1)} %get-tuple-element.25), channel_id=1, source_target_pairs={{0,2},{1,3},{2,0},{3,1},{4,6},{5,7},{6,4},{7,5},{8,10},{9,11},{10,... | collective-permute-start | bytes 196616 | tf_op jit(solution)/shard_map/ppermute | solution.py:316
  45.6 2.0 %shard_map.122.rest_5_ = f32[32,1024]{1,0:T(8,128)S(1)} custom-call(s32[1]{0:T(128)} %bitcast.tensor_ref.refs_0_, bf16[32,1024]{1,0:T(8,128)(2,1)S(1)} %get-tuple-element.19.x_ref, bf16[1024,8192]{1,0:T(8,128)(2,1)} %weight.5), custom_call_target="tpu_custom_call" | custom-call | flops 67108864 | bytes 2097152 | tf_op jit(solution)/shard_map/pallas_call | solution.py:252
  47.6 0.0 collective-permute-done.10.rest_1_
  47.6 0.0 collective-permute-done.15.rest_6_
  47.6 1.3 %collective-permute-done.16.rest_7_ = bf16[32,1024]{1,0:T(8,128)(2,1)S(1)} collective-permute-done((bf16[32,1024]{1,0:T(8,128)(2,1)S(1)}, bf16[32,1024]{1,0:T(8,128)(2,1)S(1)}, u32[]{:S(2)}, u32[]{:S(2)}) %collective-permute-start.16) | collective-permute-done | bytes 65568 | tf_op jit(solution)/shard_map/ppermute | solution.py:316
  48.9 0.7 %collective-permute-done.14.rest_4_ = bf16[32,1152]{1,0:T(8,128)(2,1)S(1)} collective-permute-done((bf16[32,1152]{1,0:T(8,128)(2,1)S(1)}, bf16[32,1152]{1,0:T(8,128)(2,1)S(1)}, u32[]{:S(2)}, u32[]{:S(2)}) %collective-permute-start.14) | collective-permute-done | bytes 73760 | tf_op jit(solution)/shard_map/ppermute | solution.py:316
  49.6 1.0 %final.1 = bf16[32,1024]{1,0:T(8,128)(2,1)} custom-call(f32[32,512]{1,0:T(8,128)S(1)} %add_convert_fusion.3.picks_ref.refs_6_, f32[32,128]{1,0:T(8,128)S(1)} %get-tuple-element.16.low_ref, bf16[256,1024]{1,0:T(8,128)(2,1)S(1)} %bitcast.10, bf16[256,1024]{1,0:T(8,128)(2,1)S(1)} %collective-permute-done.10.rest_1_, ...), custom_call_target="tpu_custom_call" | custom-call | flops 100000000 | bytes 1000000 | tf_op jit(solution)/shard_map/final/pallas_call | solution.py:465
  (18 shorter events, 0.2 us)
Async XLA Ops:
  0.0 15.6 %collective-permute-start = (bf16[32,1024]{1,0:T(8,128)(2,1)}, bf16[32,1024]{1,0:T(8,128)(2,1)S(1)}, u32[]{:S(2)}, u32[]{:S(2)}) collective-permute-start(bf16[32,1024]{1,0:T(8,128)(2,1)} %x_hbm.1), channel_id=1, source_target_pairs={{0,4},{1,5},{2,6},{3,7},{4,0},{5,1},{6,2},{7,3},{8,12},{9,13},{10,... | collective-permute-start | bytes 196616 | tf_op jit(solution)/shard_map/ppermute | solution.py:316
  4.1 12.0 %collective-permute-start.6 = (bf16[32,1024]{1,0:T(8,128)(2,1)}, bf16[32,1024]{1,0:T(8,128)(2,1)S(1)}, u32[]{:S(2)}, u32[]{:S(2)}) collective-permute-start(bf16[32,1024]{1,0:T(8,128)(2,1)} %x_hbm.1), channel_id=1, source_target_pairs={{0,2},{1,3},{2,0},{3,1},{4,6},{5,7},{6,4},{7,5},{8,10},{9,11},{10,... | collective-permute-start | bytes 196616 | tf_op jit(solution)/shard_map/ppermute | solution.py:316
  5.6 19.3 %collective-permute-start.5 = (bf16[32,1024]{1,0:T(8,128)(2,1)}, bf16[32,1024]{1,0:T(8,128)(2,1)S(1)}, u32[]{:S(2)}, u32[]{:S(2)}) collective-permute-start(bf16[32,1024]{1,0:T(8,128)(2,1)} %x_hbm.1), channel_id=1, source_target_pairs={{0,1},{1,0},{2,3},{3,2},{4,5},{5,4},{6,7},{7,6},{8,9},{9,8},{10,11... | collective-permute-start | bytes 196616 | tf_op jit(solution)/shard_map/ppermute | solution.py:316
  7.2 2.1 %collective-permute-start.1 = (bf16[256,1024]{1,0:T(8,128)(2,1)}, bf16[256,1024]{1,0:T(8,128)(2,1)S(1)}, u32[]{:S(2)}, u32[]{:S(2)}) collective-permute-start(bf16[256,1024]{1,0:T(8,128)(2,1)} %bitcast.11), channel_id=1, source_target_pairs={{0,8},{8,0},{1,9},{9,1},{2,10},{10,2},{3,11},{11,3},{4,12},{12,4},... | collective-permute-start | bytes 1572872 | tf_op jit(solution)/shard_map/ppermute | solution.py:321
  7.2 21.6 %collective-permute-start.8 = (bf16[256,1024]{1,0:T(8,128)(2,1)}, bf16[256,1024]{1,0:T(8,128)(2,1)S(1)}, u32[]{:S(2)}, u32[]{:S(2)}) collective-permute-start(bf16[256,1024]{1,0:T(8,128)(2,1)} %bitcast.5), channel_id=1, source_target_pairs={{0,8},{8,0},{1,9},{9,1},{2,10},{10,2},{3,11},{11,3},{4,12},{12,4},... | collective-permute-start | bytes 1572872 | tf_op jit(solution)/shard_map/ppermute | solution.py:321
  10.8 4.8 %collective-permute-start.2 = (f32[32,128]{1,0:T(8,128)S(1)}, f32[32,128]{1,0:T(8,128)S(1)}, u32[]{:S(2)}, u32[]{:S(2)}) collective-permute-start(f32[32,128]{1,0:T(8,128)S(1)} %get-tuple-element.14), channel_id=1, source_target_pairs={{0,4},{1,5},{2,6},{3,7},{4,0},{5,1},{6,2},{7,3},{8,12},{9,13},{10,... | collective-permute-start | bytes 49160 | tf_op jit(solution)/shard_map/ppermute | solution.py:316
  15.6 13.2 %collective-permute-start.9 = (bf16[256,1024]{1,0:T(8,128)(2,1)}, bf16[256,1024]{1,0:T(8,128)(2,1)S(1)}, u32[]{:S(2)}, u32[]{:S(2)}) collective-permute-start(bf16[256,1024]{1,0:T(8,128)(2,1)} %bitcast.7), channel_id=1, source_target_pairs={{0,8},{8,0},{1,9},{9,1},{2,10},{10,2},{3,11},{11,3},{4,12},{12,4},... | collective-permute-start | bytes 1572872 | tf_op jit(solution)/shard_map/ppermute | solution.py:321
  15.6 4.7 %collective-permute-start.3 = (bf16[32,1152]{1,0:T(8,128)(2,1)S(1)}, bf16[32,1152]{1,0:T(8,128)(2,1)S(1)}, u32[]{:S(2)}, u32[]{:S(2)}) collective-permute-start(bf16[32,1152]{1,0:T(8,128)(2,1)S(1)} %pad_maximum_fusion.1), channel_id=1, source_target_pairs={{0,2},{1,3},{2,0},{3,1},{4,6},{5,7},{6,4},{7,5},{8,10},{9,11},{10,... | collective-permute-start | bytes 221192 | tf_op jit(solution)/shard_map/ppermute | solution.py:316
  16.1 8.9 %collective-permute-start.7 = (bf16[64,1024]{1,0:T(8,128)(2,1)S(1)}, bf16[64,1024]{1,0:T(8,128)(2,1)S(1)}, u32[]{:S(2)}, u32[]{:S(2)}) collective-permute-start(bf16[64,1024]{1,0:T(8,128)(2,1)S(1)} %pad_maximum_fusion), channel_id=1, source_target_pairs={{0,1},{1,0},{2,3},{3,2},{4,5},{5,4},{6,7},{7,6},{8,9},{9,8},{10,11... | collective-permute-start | bytes 393224 | tf_op jit(solution)/shard_map/ppermute | solution.py:316
  20.4 8.4 %collective-permute-start.4 = (bf16[32,1152]{1,0:T(8,128)(2,1)S(1)}, bf16[32,1152]{1,0:T(8,128)(2,1)S(1)}, u32[]{:S(2)}, u32[]{:S(2)}) collective-permute-start(bf16[32,1152]{1,0:T(8,128)(2,1)S(1)} %pad_maximum_fusion.2), channel_id=1, source_target_pairs={{0,1},{1,0},{2,3},{3,2},{4,5},{5,4},{6,7},{7,6},{8,9},{9,8},{10,11... | collective-permute-start | bytes 221192 | tf_op jit(solution)/shard_map/ppermute | solution.py:316
  21.7 7.1 %copy-start = (bf16[4,64,1024]{2,1,0:T(8,128)(2,1)S(1)}, bf16[4,64,1024]{2,1,0:T(8,128)(2,1)}, u32[]{:S(2)}) copy-start(bf16[4,64,1024]{2,1,0:T(8,128)(2,1)} %param.18) | copy-start | bytes 1572868
  21.7 7.1 %copy-start.1 = (bf16[4,64,1024]{2,1,0:T(8,128)(2,1)S(1)}, bf16[4,64,1024]{2,1,0:T(8,128)(2,1)}, u32[]{:S(2)}) copy-start(bf16[4,64,1024]{2,1,0:T(8,128)(2,1)} %param.19) | copy-start | bytes 1572868
  33.3 5.4 %copy-start.2 = (bf16[4,64,1024]{2,1,0:T(8,128)(2,1)S(1)}, bf16[4,64,1024]{2,1,0:T(8,128)(2,1)}, u32[]{:S(2)}) copy-start(bf16[4,64,1024]{2,1,0:T(8,128)(2,1)} %param.20) | copy-start | bytes 1572868
  33.3 4.9 %collective-permute-start.11 = (bf16[32,1152]{1,0:T(8,128)(2,1)S(1)}, bf16[32,1152]{1,0:T(8,128)(2,1)S(1)}, u32[]{:S(2)}, u32[]{:S(2)}) collective-permute-start(bf16[32,1152]{1,0:T(8,128)(2,1)S(1)} %get-tuple-element.17), channel_id=1, source_target_pairs={{0,1},{1,0},{2,3},{3,2},{4,5},{5,4},{6,7},{7,6},{8,9},{9,8},{10,11... | collective-permute-start | bytes 221192 | tf_op jit(solution)/shard_map/ppermute | solution.py:316
  37.5 5.0 %collective-permute-start.13 = (bf16[64,1024]{1,0:T(8,128)(2,1)S(1)}, bf16[64,1024]{1,0:T(8,128)(2,1)S(1)}, u32[]{:S(2)}, u32[]{:S(2)}) collective-permute-start(bf16[64,1024]{1,0:T(8,128)(2,1)S(1)} %shard_map.121), channel_id=1, source_target_pairs={{0,1},{1,0},{2,3},{3,2},{4,5},{5,4},{6,7},{7,6},{8,9},{9,8},{10,11... | collective-permute-start | bytes 393224 | tf_op jit(solution)/shard_map/ppermute | solution.py:316
  38.2 4.4 %collective-permute-start.12 = (bf16[32,1152]{1,0:T(8,128)(2,1)S(1)}, bf16[32,1152]{1,0:T(8,128)(2,1)S(1)}, u32[]{:S(2)}, u32[]{:S(2)}) collective-permute-start(bf16[32,1152]{1,0:T(8,128)(2,1)S(1)} %pad_maximum_fusion.3), channel_id=1, source_target_pairs={{0,2},{1,3},{2,0},{3,1},{4,6},{5,7},{6,4},{7,5},{8,10},{9,11},{10,... | collective-permute-start | bytes 221192 | tf_op jit(solution)/shard_map/ppermute | solution.py:316
  38.6 9.0 %collective-permute-start.10 = (bf16[256,1024]{1,0:T(8,128)(2,1)S(1)}, bf16[256,1024]{1,0:T(8,128)(2,1)S(1)}, u32[]{:S(2)}, u32[]{:S(2)}) collective-permute-start(bf16[256,1024]{1,0:T(8,128)(2,1)S(1)} %bitcast.9), channel_id=1, source_target_pairs={{0,8},{8,0},{1,9},{9,1},{2,10},{10,2},{3,11},{11,3},{4,12},{12,4},... | collective-permute-start | bytes 1572872 | tf_op jit(solution)/shard_map/ppermute | solution.py:321
  42.7 6.9 %collective-permute-start.14 = (bf16[32,1152]{1,0:T(8,128)(2,1)S(1)}, bf16[32,1152]{1,0:T(8,128)(2,1)S(1)}, u32[]{:S(2)}, u32[]{:S(2)}) collective-permute-start(bf16[32,1152]{1,0:T(8,128)(2,1)S(1)} %pad_maximum_fusion.4), channel_id=1, source_target_pairs={{0,4},{1,5},{2,6},{3,7},{4,0},{5,1},{6,2},{7,3},{8,12},{9,13},{10,... | collective-permute-start | bytes 221192 | tf_op jit(solution)/shard_map/ppermute | solution.py:316
  43.0 4.6 %collective-permute-start.15 = (bf16[32,1024]{1,0:T(8,128)(2,1)S(1)}, bf16[32,1024]{1,0:T(8,128)(2,1)S(1)}, u32[]{:S(2)}, u32[]{:S(2)}) collective-permute-start(bf16[32,1024]{1,0:T(8,128)(2,1)S(1)} %get-tuple-element.21), channel_id=1, source_target_pairs={{0,1},{1,0},{2,3},{3,2},{4,5},{5,4},{6,7},{7,6},{8,9},{9,8},{10,11... | collective-permute-start | bytes 196616 | tf_op jit(solution)/shard_map/ppermute | solution.py:316
  44.5 4.4 %collective-permute-start.16 = (bf16[32,1024]{1,0:T(8,128)(2,1)S(1)}, bf16[32,1024]{1,0:T(8,128)(2,1)S(1)}, u32[]{:S(2)}, u32[]{:S(2)}) collective-permute-start(bf16[32,1024]{1,0:T(8,128)(2,1)S(1)} %get-tuple-element.25), channel_id=1, source_target_pairs={{0,2},{1,3},{2,0},{3,1},{4,6},{5,7},{6,4},{7,5},{8,10},{9,11},{10,... | collective-permute-start | bytes 196616 | tf_op jit(solution)/shard_map/ppermute | solution.py:316

commit v2 on v1

--- a/solution.py
+++ b/solution.py
@@ -173,7 +173,7 @@
     keys, values, live = [refs.pop(0) for _ in range(3)]
     low_out, mixed_out, block_out = [refs.pop(0) for _ in range(3)]
     more_outs = [refs.pop(0) for _ in k_outs[1:]]
-    buf_in, sem_in, buf_out, sem_out, k_buf, v_buf, up_buf, down_buf, sems = refs
+    buf_in, sem_in, buf_out, sem_out, k_buf, v_buf, sems = refs
 
     tensor_at = tensor_ref[0]
     copies_in = weight_copies(w_in, buf_in, sem_in, 0, tensor_at ^ k_in, 0)
@@ -181,20 +181,16 @@
         weight_copies(w_out, buf_out, sem_out, j, tensor_at ^ k, 1) for j, k in enumerate(k_outs)
     ]
     kv = pl.ds(tensor_at * local_heads // group_all, kv_count)
-    up_copies = load_all([(u, up_buf.at[i]) for i, u in enumerate(ups)], sems.at[0])
     for c in copies_in:
         c.start()
-    kv_copies = load_all([(keys.at[:, kv], k_buf), (values.at[:, kv], v_buf)], sems.at[1])
-    down_copies = load_all([(d, down_buf.at[i]) for i, d in enumerate(downs)], sems.at[2])
+    kv_copies = load_all([(keys.at[:, kv], k_buf), (values.at[:, kv], v_buf)], sems)
     for pieces in copies_out:
         for c in pieces:
             c.start()
 
     rows = before.shape[0]
     picked = picks[...]
-    for c in up_copies:
-        c.wait()
-    total = before[...] + 0.5 * lora_of(low[...], [up_buf.at[i] for i in range(maps)], picked)
+    total = before[...] + 0.5 * lora_of(low[...], ups, picked)
     total = block_dot(lambda a, n: chunk[:, a : a + n], buf_in, 0, copies_in, total)
     query = total.astype(jnp.bfloat16)
     for c in kv_copies:
@@ -219,18 +215,15 @@
             heads[kvh * group + g] = got[g * rows : (g + 1) * rows]
     mixed = jnp.concatenate(heads, axis=1)
     mixed_out[...] = mixed
-    for c in down_copies:
-        c.wait()
-    low_part = low_of(mixed, [down_buf.at[i] for i in range(maps)], picked)
+    low_part = low_of(mixed, downs, picked)
     low_out[...] = low_part
     block = block_dot(lambda a, n: mixed[:, a : a + n], buf_out, 0, copies_out[0], 0.0)
     wide = block.shape[1]
     block_out[:, :wide] = block.astype(block_out.dtype)
     block_out[:, wide:] = low_part.astype(block_out.dtype)
     for j, ref in enumerate(more_outs):
-        ref[...] = block_dot(
-            lambda a, n: mixed[:, a : a + n], buf_out, j + 1, copies_out[j + 1], 0.0
-        )
+        block = block_dot(lambda a, n: mixed[:, a : a + n], buf_out, j + 1, copies_out[j + 1], 0.0)
+        ref[...] = block.astype(ref.dtype)
 
 
 def out_kernel(ks, spans, tensor_ref, x_ref, weight, *rest):
@@ -266,8 +259,7 @@
     ups, rest = rest[:maps], rest[maps:]
     lows, rest = rest[: count[0]], rest[count[0] :]
     terms, rest = rest[: count[1]], rest[count[1] :]
-    out_ref, up_buf, sems = rest
-    copies = load_all([(u, up_buf.at[i]) for i, u in enumerate(ups)], sems)
+    (out_ref,) = rest
     low = low_ref[...]
     total = 0.0
     for ref in lows:
@@ -275,9 +267,7 @@
     total = lows[-1][:, :wide].astype(jnp.float32)
     for t in terms:
         total = total + t[:, :wide].astype(jnp.float32)
-    for c in copies:
-        c.wait()
-    total = total + 0.5 * lora_of(low, [up_buf.at[i] for i in range(maps)], picks_ref[...])
+    total = total + 0.5 * lora_of(low, ups, picks_ref[...])
     out_ref[...] = total.astype(out_ref.dtype)
 
 
@@ -384,19 +374,19 @@
     depth = output_weight.shape[0]
     whole = shards - 1
     even = [k for k in sorted(where, reverse=True) if not k & 1]
-    k_outs = [whole] + even[:-1][:1]
+    odd = [k for k in sorted(where, reverse=True) if k & 1 and k != whole]
+    k_outs = [whole] + odd[:-1][:1]
     sizes = (last, k_outs, replicas, kv_count, group, head, local_heads, group_all, width)
-    map_in, map_out = (stored * rank, wide), (stored * rank, depth)
     low2, mixed, payload, *blocks = pl.pallas_call(
         functools.partial(mix_kernel, sizes),
-        in_specs=[SMEM, VMEM, HBM, HBM, VMEM, VMEM, VMEM] + [HBM] * (2 * replicas) + [HBM, HBM, VMEM],
+        in_specs=[SMEM, VMEM, HBM, HBM, VMEM, VMEM, VMEM] + [VMEM] * (2 * replicas) + [HBM, HBM, VMEM],
         out_specs=[VMEM] * (2 + len(k_outs)),
         out_shape=[
             jax.ShapeDtypeStruct((rows, LANES), jnp.float32),
             jax.ShapeDtypeStruct((rows, wide), jnp.bfloat16),
             jax.ShapeDtypeStruct((rows, out_width + LANES), jnp.bfloat16),
         ]
-        + [jax.ShapeDtypeStruct((rows, out_width), jnp.float32)] * (len(k_outs) - 1),
+        + [jax.ShapeDtypeStruct((rows, out_width), jnp.bfloat16)] * (len(k_outs) - 1),
         scratch_shapes=[
             pltpu.VMEM((1, width, wide), w_query.dtype),
             pltpu.SemaphoreType.DMA((1, PIECES)),
@@ -404,9 +394,7 @@
             pltpu.SemaphoreType.DMA((len(k_outs), PIECES)),
             pltpu.VMEM((rows, kv_count, length, head), keys.dtype),
             pltpu.VMEM((rows, kv_count, length, head), values.dtype),
-            pltpu.VMEM((replicas,) + map_in, keys.dtype),
-            pltpu.VMEM((replicas,) + map_out, keys.dtype),
-            pltpu.SemaphoreType.DMA((3, max(2, replicas))),
+            pltpu.SemaphoreType.DMA((2,)),
         ],
         name="mix",
         **params((10**9, 6 << 20)),
@@ -429,25 +417,21 @@
     chain = [whole]
     while chain[-1]:
         chain.append(chain[-1] & (chain[-1] - 1))
-    odd = [k for k in sorted(where, reverse=True) if k & 1 and k not in (whole, 1)]
-    f32, bf16 = jnp.float32, jnp.bfloat16
-    parts = dict(zip(k_outs[1:], blocks))
-    even = [k for k in even if k not in parts]
-    plan = [
-        [(odd, bf16)] * bool(odd),
-        [([k], f32) for k in even[:-1]] + [([1], bf16)] * (whole > 1),
-        [([k], f32) for k in even[-1:]],
-    ]
-    plan = [groups for groups in plan if groups]
-    for groups in plan:
+    for k, array in zip(k_outs[1:], blocks):
+        came[k] = across(array, 1)
+    odd = [k for k in odd if k not in k_outs]
+    parts = {}
+    plan = [even[:1] + odd[:-1] + even[1:2], even[2:-1] + odd[-1:], even[-1:]]
+    for ks in plan:
+        if not ks:
+            continue
+        groups = [([k], jnp.bfloat16 if k & 1 else jnp.float32) for k in ks if k not in parts]
         arrays = out_call(groups, tensor_at, mixed, output_weight, out_width)
-        for (g, kind), array in zip(groups, arrays):
-            if kind == bf16:
-                got = across(array, 1)
-                for i, k in enumerate(g):
-                    came[k] = got[i * rows : (i + 1) * rows]
+        for k, array in zip(ks, arrays):
+            if k & 1:
+                came[k] = across(array, 1)
             else:
-                parts[g[0]] = array
+                parts[k] = array
     for k in sorted((k for k in where if k and not k & 1), key=lambda k: (low_bit(k), -k)):
         main = parts[k]
         bit = 1
@@ -464,13 +448,9 @@
     terms = [parts[0]] + [came[1 << i] for i in range(len(bits) - 1)]
     return pl.pallas_call(
         functools.partial(final_kernel, out_width, (len(lows), len(terms)), replicas),
-        in_specs=[VMEM, VMEM] + [HBM] * replicas + [VMEM] * (len(lows) + len(terms)),
+        in_specs=[VMEM] * (2 + replicas + len(lows) + len(terms)),
         out_specs=VMEM,
         out_shape=jax.ShapeDtypeStruct((rows, out_width), jnp.bfloat16),
-        scratch_shapes=[
-            pltpu.VMEM((replicas,) + map_in, keys.dtype),
-            pltpu.SemaphoreType.DMA((replicas,)),
-        ],
         name="final",
         **params((10**8, 10**6)),
     )(picks, low2, *output_up, *lows, *terms)

time: 50.8 us -> 54.7 us (1.077)
  starting transfers between devices: 15.2 us -> 16.9 us
  waiting for transfers between devices: 11.3 us -> 12.7 us
  Pallas kernels: 22 us -> 22.8 us
    ppermute x13 -> x14, starting transfers between devices: 14.7 us -> 16.4 us  [across(): return lax.ppermute(x, 'tensor', [(i, i ^ bit) for i in range(shards)])]
    ppermute x13 -> x14, waiting for transfers between devices: 10.6 us -> 12.1 us  [across(): return lax.ppermute(x, 'tensor', [(i, i ^ bit) for i in range(shards)])]
    pallas_call x1, Pallas kernels: 4.39 us -> 5.28 us  [per_device(): pl.pallas_call(functools.partial(mix_kernel, sizes), in_specs=[SMEM, VMEM...]
  transfers between devices with their start and end apart: 17 -> 18, of which waited for: 6 -> 5; matrix products, arithmetic and copies ran while one was open for 4% -> 3% of each run, Pallas kernels for 33% -> 30%
where the time goes in v2:
time: 54.7 us; the launch traced here: 54.6 us
  Pallas kernels  22.8 us (42%)
  starting transfers between devices  16.9 us (31%)
  waiting for transfers between devices  12.7 us (23%)
  other arithmetic  1.75 us (3%)
    ppermute x14, starting transfers between devices, across(): return lax.ppermute(x, 'tensor', [(i, i ^ bit) for i in range(shards)])  16.4 us
    ppermute x14, waiting for transfers between devices, across(): return lax.ppermute(x, 'tensor', [(i, i ^ bit) for i in range(shards)])  12.1 us
    pallas_call x3, Pallas kernels, out_call(): pl.pallas_call(functools.partial(out_kernel, ks, spans), in_specs=[SMEM,...  8.06 us
    pallas_call x2, Pallas kernels, project_call(): pl.pallas_call(functools.partial(project_kernel, ks, spans, before is Non...  7.01 us
    pallas_call x1, Pallas kernels, per_device(): pl.pallas_call(functools.partial(mix_kernel, sizes), in_specs=[SMEM, VMEM...  5.28 us
    pallas_call x1, Pallas kernels, low_call(): pl.pallas_call(functools.partial(low_kernel, len(downs)), in_specs=[HBM,...  1.53 us
  transfers between devices with their start and end apart: 18, of which 5 were waited for; matrix products, arithmetic and copies ran while one was open for 3% of the time, Pallas kernels for 30%

profile of v2, /device:TPU:0, one launch (start us, length us, event | category | flops | bytes accessed | tf_op | source)
XLA Modules:
  0.0 54.6 jit_solution(4771939467561426519)
XLA Ops:
  0.0 4.1 %collective-permute-start = (bf16[32,1024]{1,0:T(8,128)(2,1)}, bf16[32,1024]{1,0:T(8,128)(2,1)S(1)}, u32[]{:S(2)}, u32[]{:S(2)}) collective-permute-start(bf16[32,1024]{1,0:T(8,128)(2,1)} %x_hbm.1), channel_id=1, source_target_pairs={{0,4},{1,5},{2,6},{3,7},{4,0},{5,1},{6,2},{7,3},{8,12},{9,13},{10,... | collective-permute-start | bytes 196616 | tf_op jit(solution)/shard_map/ppermute | solution.py:306
  4.1 1.6 %collective-permute-start.6 = (bf16[32,1024]{1,0:T(8,128)(2,1)}, bf16[32,1024]{1,0:T(8,128)(2,1)S(1)}, u32[]{:S(2)}, u32[]{:S(2)}) collective-permute-start(bf16[32,1024]{1,0:T(8,128)(2,1)} %x_hbm.1), channel_id=1, source_target_pairs={{0,2},{1,3},{2,0},{3,1},{4,6},{5,7},{6,4},{7,5},{8,10},{9,11},{10,... | collective-permute-start | bytes 196616 | tf_op jit(solution)/shard_map/ppermute | solution.py:306
  5.6 1.5 %collective-permute-start.5 = (bf16[32,1024]{1,0:T(8,128)(2,1)}, bf16[32,1024]{1,0:T(8,128)(2,1)S(1)}, u32[]{:S(2)}, u32[]{:S(2)}) collective-permute-start(bf16[32,1024]{1,0:T(8,128)(2,1)} %x_hbm.1), channel_id=1, source_target_pairs={{0,1},{1,0},{2,3},{3,2},{4,5},{5,4},{6,7},{7,6},{8,9},{9,8},{10,11... | collective-permute-start | bytes 196616 | tf_op jit(solution)/shard_map/ppermute | solution.py:306
  7.2 0.0 collective-permute-start.1
  7.2 0.5 collective-permute-start.8
  7.7 0.8 %select_reduce_fusion = s32[64]{0:T(128)S(1)} fusion(s32[8]{0:T(128)} %param.22, s32[64]{0:T(128)} %param.21), kind=kLoop, calls=%fused_computation.30 | loop fusion | flops 1472 | bytes 544 | tf_op jit(solution)/shard_map/reduce_sum | solution.py:316
  8.4 0.1 dynamic_slice.3
  8.5 0.1 broadcast_compare_fusion.1
  8.6 0.7 %collective-permute-done.1.rest_1_ = bf16[256,1024]{1,0:T(8,128)(2,1)S(1)} collective-permute-done((bf16[256,1024]{1,0:T(8,128)(2,1)}, bf16[256,1024]{1,0:T(8,128)(2,1)S(1)}, u32[]{:S(2)}, u32[]{:S(2)}) %collective-permute-start.1) | collective-permute-done | bytes 524320 | tf_op jit(solution)/shard_map/ppermute | solution.py:311
  9.3 1.5 %low.1 = (f32[32,128]{1,0:T(8,128)S(1)}, bf16[32,1024]{1,0:T(8,128)(2,1)S(1)}) custom-call(bf16[32,1024]{1,0:T(8,128)(2,1)} %x_hbm.1, f32[32,512]{1,0:T(8,128)S(1)} %add_convert_fusion.3.picks_ref.refs_6_, bf16[256,1024]{1,0:T(8,128)(2,1)} %bitcast.12, bf16[256,1024]{1,0:T(8,128)(2,1)S(1)} %collective-permute-done.1.rest_1_), custom_call_target="tpu_custom_call" | custom-call | flops 100000000 | bytes 1000000 | tf_op jit(solution)/shard_map/low/pallas_call | solution.py:81
  10.8 0.4 collective-permute-start.2
  11.2 4.4 %collective-permute-done.2 = f32[32,128]{1,0:T(8,128)S(1)} collective-permute-done((f32[32,128]{1,0:T(8,128)S(1)}, f32[32,128]{1,0:T(8,128)S(1)}, u32[]{:S(2)}, u32[]{:S(2)}) %collective-permute-start.2) | collective-permute-done | bytes 16416 | tf_op jit(solution)/shard_map/ppermute | solution.py:306
  15.6 0.0 collective-permute-start.9
  15.6 0.0 collective-permute-done.rest_1_
  15.6 0.5 collective-permute-start.3
  16.1 0.0 collective-permute-done.6.rest_2_
  16.1 0.6 %collective-permute-start.7 = (bf16[64,1024]{1,0:T(8,128)(2,1)S(1)}, bf16[64,1024]{1,0:T(8,128)(2,1)S(1)}, u32[]{:S(2)}, u32[]{:S(2)}) collective-permute-start(bf16[64,1024]{1,0:T(8,128)(2,1)S(1)} %pad_maximum_fusion), channel_id=1, source_target_pairs={{0,1},{1,0},{2,3},{3,2},{4,5},{5,4},{6,7},{7,6},{8,9},{9,8},{10,11... | collective-permute-start | bytes 393224 | tf_op jit(solution)/shard_map/ppermute | solution.py:306
  16.7 3.7 %collective-permute-done.3.rest_1_ = bf16[32,1152]{1,0:T(8,128)(2,1)S(1)} collective-permute-done((bf16[32,1152]{1,0:T(8,128)(2,1)S(1)}, bf16[32,1152]{1,0:T(8,128)(2,1)S(1)}, u32[]{:S(2)}, u32[]{:S(2)}) %collective-permute-start.3) | collective-permute-done | bytes 73760 | tf_op jit(solution)/shard_map/ppermute | solution.py:306
  20.4 0.6 %collective-permute-start.4 = (bf16[32,1152]{1,0:T(8,128)(2,1)S(1)}, bf16[32,1152]{1,0:T(8,128)(2,1)S(1)}, u32[]{:S(2)}, u32[]{:S(2)}) collective-permute-start(bf16[32,1152]{1,0:T(8,128)(2,1)S(1)} %pad_maximum_fusion.2), channel_id=1, source_target_pairs={{0,1},{1,0},{2,3},{3,2},{4,5},{5,4},{6,7},{7,6},{8,9},{9,8},{10,11... | collective-permute-start | bytes 221192 | tf_op jit(solution)/shard_map/ppermute | solution.py:306
  21.0 0.7 %fusion.1.refs_13_ = f32[32,1024]{1,0:T(8,128)S(1)} fusion(s32[32]{0:T(128)} %param.23, s32[1024]{0:T(1024)S(1)} %get-tuple-element.34, s32[1024]{0:T(1024)S(1)} %get-tuple-element.35, s32[1024]{0:T(1024)S(1)} %get-tuple-element.33, s32[1024]{0:T(1024)S(1)} %get-tuple-element.36, pred[1024]{0:T(1024)(128)(4,1)S(1)} %get-tuple-element.37, ...), kind=kLoop, calls=%fused_computation.7 | loop fusion | flops 196608 | bytes 149632 | tf_op jit(solution)/shard_map/convert_element_type | solution.py:328
  21.7 0.0 copy-start
  21.7 0.0 copy-start.1
  21.7 3.2 %shard_map.118.rest_4_ = f32[32,1024]{1,0:T(8,128)S(1)} custom-call(s32[1]{0:T(128)} %bitcast.tensor_ref.refs_0_, bf16[32,1024]{1,0:T(8,128)(2,1)S(1)} %get-tuple-element.17.rest_0_, bf16[32,1024]{1,0:T(8,128)(2,1)S(1)} %collective-permute-done.rest_1_, bf16[32,1024]{1,0:T(8,128)(2,1)S(1)} %collective-permute-done.6.rest_2_, bf16[8192,1024]{1,0:T(8,128)(2,1)} %refs_2_.1), custom_call_target="tpu_custom_call" | custom-call | flops 201326592 | bytes 6291456 | tf_op jit(solution)/shard_map/pallas_call | solution.py:152
  25.0 0.0 collective-permute-done.5.rest_0_
  25.0 0.0 collective-permute-done.7.rest_2_
  25.0 3.8 %shard_map.119.refs_4_ = f32[32,1024]{1,0:T(8,128)S(1)} custom-call(s32[1]{0:T(128)} %bitcast.tensor_ref.refs_0_, bf16[32,1024]{1,0:T(8,128)(2,1)S(1)} %collective-permute-done.5.rest_0_, bf16[32,1152]{1,0:T(8,128)(2,1)S(1)} %collective-permute-done.3.rest_1_, bf16[64,1024]{1,0:T(8,128)(2,1)S(1)} %collective-permute-done.7.rest_2_, ...), custom_call_target="tpu_custom_call" | custom-call | flops 268435456 | bytes 8388608 | tf_op jit(solution)/shard_map/pallas_call | solution.py:152
  28.8 0.0 collective-permute-done.4.refs_1_
  28.8 0.0 collective-permute-done.8.refs_8_
  28.8 0.0 collective-permute-done.9.refs_10_
  28.8 0.0 copy-done
  28.8 0.0 copy-done.1
  28.9 5.3 %mix.1 = (f32[32,128]{1,0:T(8,128)S(1)}, bf16[32,1024]{1,0:T(8,128)(2,1)S(1)}, bf16[32,1152]{1,0:T(8,128)(2,1)S(1)}, bf16[32,1024]{1,0:T(8,128)(2,1)S(1)}) custom-call(s32[1]{0:T(128)} %bitcast.tensor_ref.refs_0_, bf16[32,1152]{1,0:T(8,128)(2,1)S(1)} %collective-permute-done.4.refs_1_, bf16[8192,1024]{1,0:T(8,128)(2,1)} %refs_2_.1, ...), custom_call_target="tpu_custom_call" | custom-call | flops 1000000000 | bytes 6291456 | tf_op jit(solution)/shard_map/mix/pallas_call | solution.py:380
  34.1 0.0 copy-start.2
  34.2 1.6 %collective-permute-start.11 = (bf16[32,1152]{1,0:T(8,128)(2,1)S(1)}, bf16[32,1152]{1,0:T(8,128)(2,1)S(1)}, u32[]{:S(2)}, u32[]{:S(2)}) collective-permute-start(bf16[32,1152]{1,0:T(8,128)(2,1)S(1)} %get-tuple-element.19), channel_id=1, source_target_pairs={{0,1},{1,0},{2,3},{3,2},{4,5},{5,4},{6,7},{7,6},{8,9},{9,8},{10,11... | collective-permute-start | bytes 221192 | tf_op jit(solution)/shard_map/ppermute | solution.py:306
  35.7 3.3 %shard_map.120 = (f32[32,1024]{1,0:T(8,128)S(1)}, bf16[32,1024]{1,0:T(8,128)(2,1)S(1)}, f32[32,1024]{1,0:T(8,128)S(1)}) custom-call(s32[1]{0:T(128)} %bitcast.tensor_ref.refs_0_, bf16[32,1024]{1,0:T(8,128)(2,1)S(1)} %get-tuple-element.20.x_ref, bf16[1024,8192]{1,0:T(8,128)(2,1)} %weight.5), custom_call_target="tpu_custom_call" | custom-call | flops 201326592 | bytes 6291456 | tf_op jit(solution)/shard_map/pallas_call | solution.py:245
  39.1 0.0 collective-permute-done.11.rest_2_
  39.1 0.5 collective-permute-start.12
  39.6 1.0 %collective-permute-start.13 = (bf16[32,1024]{1,0:T(8,128)(2,1)S(1)}, bf16[32,1024]{1,0:T(8,128)(2,1)S(1)}, u32[]{:S(2)}, u32[]{:S(2)}) collective-permute-start(bf16[32,1024]{1,0:T(8,128)(2,1)S(1)} %get-tuple-element.23), channel_id=1, source_target_pairs={{0,1},{1,0},{2,3},{3,2},{4,5},{5,4},{6,7},{7,6},{8,9},{9,8},{10,11... | collective-permute-start | bytes 196616 | tf_op jit(solution)/shard_map/ppermute | solution.py:306
  40.6 0.0 copy-done.2
  40.6 0.0 collective-permute-start.10
  40.6 2.7 %shard_map.122 = (f32[32,1024]{1,0:T(8,128)S(1)}, bf16[32,1024]{1,0:T(8,128)(2,1)S(1)}) custom-call(s32[1]{0:T(128)} %bitcast.tensor_ref.refs_0_, bf16[32,1024]{1,0:T(8,128)(2,1)S(1)} %get-tuple-element.20.x_ref, bf16[1024,8192]{1,0:T(8,128)(2,1)} %weight.5), custom_call_target="tpu_custom_call" | custom-call | flops 134217728 | bytes 4194304 | tf_op jit(solution)/shard_map/pallas_call | solution.py:245
  43.3 1.1 %collective-permute-start.15 = (bf16[32,1024]{1,0:T(8,128)(2,1)S(1)}, bf16[32,1024]{1,0:T(8,128)(2,1)S(1)}, u32[]{:S(2)}, u32[]{:S(2)}) collective-permute-start(bf16[32,1024]{1,0:T(8,128)(2,1)S(1)} %get-tuple-element.24), channel_id=1, source_target_pairs={{0,1},{1,0},{2,3},{3,2},{4,5},{5,4},{6,7},{7,6},{8,9},{9,8},{10,11... | collective-permute-start | bytes 196616 | tf_op jit(solution)/shard_map/ppermute | solution.py:306
  44.4 1.0 %collective-permute-start.16 = (bf16[32,1024]{1,0:T(8,128)(2,1)S(1)}, bf16[32,1024]{1,0:T(8,128)(2,1)S(1)}, u32[]{:S(2)}, u32[]{:S(2)}) collective-permute-start(bf16[32,1024]{1,0:T(8,128)(2,1)S(1)} %get-tuple-element.26), channel_id=1, source_target_pairs={{0,1},{1,0},{2,3},{3,2},{4,5},{5,4},{6,7},{7,6},{8,9},{9,8},{10,11... | collective-permute-start | bytes 196616 | tf_op jit(solution)/shard_map/ppermute | solution.py:306
  45.4 0.0 collective-permute-done.13
  45.4 0.0 collective-permute-done.12.rest_3_
  45.5 0.4 collective-permute-start.14
  45.9 3.4 %collective-permute-done.16 = bf16[32,1024]{1,0:T(8,128)(2,1)S(1)} collective-permute-done((bf16[32,1024]{1,0:T(8,128)(2,1)S(1)}, bf16[32,1024]{1,0:T(8,128)(2,1)S(1)}, u32[]{:S(2)}, u32[]{:S(2)}) %collective-permute-start.16) | collective-permute-done | bytes 65568 | tf_op jit(solution)/shard_map/ppermute | solution.py:306
  49.3 1.7 %collective-permute-start.17 = (bf16[32,1024]{1,0:T(8,128)(2,1)S(1)}, bf16[32,1024]{1,0:T(8,128)(2,1)S(1)}, u32[]{:S(2)}, u32[]{:S(2)}) collective-permute-start(bf16[32,1024]{1,0:T(8,128)(2,1)S(1)} %add_convert_fusion), channel_id=1, source_target_pairs={{0,2},{1,3},{2,0},{3,1},{4,6},{5,7},{6,4},{7,5},{8,10},{9,11},{10,... | collective-permute-start | bytes 196616 | tf_op jit(solution)/shard_map/ppermute | solution.py:306
  51.0 2.0 %shard_map.121.rest_5_ = f32[32,1024]{1,0:T(8,128)S(1)} custom-call(s32[1]{0:T(128)} %bitcast.tensor_ref.refs_0_, bf16[32,1024]{1,0:T(8,128)(2,1)S(1)} %get-tuple-element.20.x_ref, bf16[1024,8192]{1,0:T(8,128)(2,1)} %weight.5), custom_call_target="tpu_custom_call" | custom-call | flops 67108864 | bytes 2097152 | tf_op jit(solution)/shard_map/pallas_call | solution.py:245
  53.0 0.0 collective-permute-done.10.rest_1_
  53.0 0.0 collective-permute-done.15.rest_6_
  53.1 0.6 %collective-permute-done.17.rest_7_ = bf16[32,1024]{1,0:T(8,128)(2,1)S(1)} collective-permute-done((bf16[32,1024]{1,0:T(8,128)(2,1)S(1)}, bf16[32,1024]{1,0:T(8,128)(2,1)S(1)}, u32[]{:S(2)}, u32[]{:S(2)}) %collective-permute-start.17) | collective-permute-done | bytes 65568 | tf_op jit(solution)/shard_map/ppermute | solution.py:306
  53.6 0.0 collective-permute-done.14.rest_4_
  53.6 0.9 %final.1 = bf16[32,1024]{1,0:T(8,128)(2,1)} custom-call(f32[32,512]{1,0:T(8,128)S(1)} %add_convert_fusion.3.picks_ref.refs_6_, f32[32,128]{1,0:T(8,128)S(1)} %get-tuple-element.18.low_ref, bf16[256,1024]{1,0:T(8,128)(2,1)S(1)} %bitcast.10, bf16[256,1024]{1,0:T(8,128)(2,1)S(1)} %collective-permute-done.10.rest_1_, ...), custom_call_target="tpu_custom_call" | custom-call | flops 100000000 | bytes 1000000 | tf_op jit(solution)/shard_map/final/pallas_call | solution.py:449
  (19 shorter events, 0.2 us)
Async XLA Ops:
  0.0 15.6 %collective-permute-start = (bf16[32,1024]{1,0:T(8,128)(2,1)}, bf16[32,1024]{1,0:T(8,128)(2,1)S(1)}, u32[]{:S(2)}, u32[]{:S(2)}) collective-permute-start(bf16[32,1024]{1,0:T(8,128)(2,1)} %x_hbm.1), channel_id=1, source_target_pairs={{0,4},{1,5},{2,6},{3,7},{4,0},{5,1},{6,2},{7,3},{8,12},{9,13},{10,... | collective-permute-start | bytes 196616 | tf_op jit(solution)/shard_map/ppermute | solution.py:306
  4.1 12.0 %collective-permute-start.6 = (bf16[32,1024]{1,0:T(8,128)(2,1)}, bf16[32,1024]{1,0:T(8,128)(2,1)S(1)}, u32[]{:S(2)}, u32[]{:S(2)}) collective-permute-start(bf16[32,1024]{1,0:T(8,128)(2,1)} %x_hbm.1), channel_id=1, source_target_pairs={{0,2},{1,3},{2,0},{3,1},{4,6},{5,7},{6,4},{7,5},{8,10},{9,11},{10,... | collective-permute-start | bytes 196616 | tf_op jit(solution)/shard_map/ppermute | solution.py:306
  5.6 19.3 %collective-permute-start.5 = (bf16[32,1024]{1,0:T(8,128)(2,1)}, bf16[32,1024]{1,0:T(8,128)(2,1)S(1)}, u32[]{:S(2)}, u32[]{:S(2)}) collective-permute-start(bf16[32,1024]{1,0:T(8,128)(2,1)} %x_hbm.1), channel_id=1, source_target_pairs={{0,1},{1,0},{2,3},{3,2},{4,5},{5,4},{6,7},{7,6},{8,9},{9,8},{10,11... | collective-permute-start | bytes 196616 | tf_op jit(solution)/shard_map/ppermute | solution.py:306
  7.2 2.1 %collective-permute-start.1 = (bf16[256,1024]{1,0:T(8,128)(2,1)}, bf16[256,1024]{1,0:T(8,128)(2,1)S(1)}, u32[]{:S(2)}, u32[]{:S(2)}) collective-permute-start(bf16[256,1024]{1,0:T(8,128)(2,1)} %bitcast.11), channel_id=1, source_target_pairs={{0,8},{8,0},{1,9},{9,1},{2,10},{10,2},{3,11},{11,3},{4,12},{12,4},... | collective-permute-start | bytes 1572872 | tf_op jit(solution)/shard_map/ppermute | solution.py:311
  7.2 21.6 %collective-permute-start.8 = (bf16[256,1024]{1,0:T(8,128)(2,1)}, bf16[256,1024]{1,0:T(8,128)(2,1)S(1)}, u32[]{:S(2)}, u32[]{:S(2)}) collective-permute-start(bf16[256,1024]{1,0:T(8,128)(2,1)} %bitcast.5), channel_id=1, source_target_pairs={{0,8},{8,0},{1,9},{9,1},{2,10},{10,2},{3,11},{11,3},{4,12},{12,4},... | collective-permute-start | bytes 1572872 | tf_op jit(solution)/shard_map/ppermute | solution.py:311
  10.8 4.8 %collective-permute-start.2 = (f32[32,128]{1,0:T(8,128)S(1)}, f32[32,128]{1,0:T(8,128)S(1)}, u32[]{:S(2)}, u32[]{:S(2)}) collective-permute-start(f32[32,128]{1,0:T(8,128)S(1)} %get-tuple-element.16), channel_id=1, source_target_pairs={{0,4},{1,5},{2,6},{3,7},{4,0},{5,1},{6,2},{7,3},{8,12},{9,13},{10,... | collective-permute-start | bytes 49160 | tf_op jit(solution)/shard_map/ppermute | solution.py:306
  15.6 13.2 %collective-permute-start.9 = (bf16[256,1024]{1,0:T(8,128)(2,1)}, bf16[256,1024]{1,0:T(8,128)(2,1)S(1)}, u32[]{:S(2)}, u32[]{:S(2)}) collective-permute-start(bf16[256,1024]{1,0:T(8,128)(2,1)} %bitcast.7), channel_id=1, source_target_pairs={{0,8},{8,0},{1,9},{9,1},{2,10},{10,2},{3,11},{11,3},{4,12},{12,4},... | collective-permute-start | bytes 1572872 | tf_op jit(solution)/shard_map/ppermute | solution.py:311
  15.6 4.7 %collective-permute-start.3 = (bf16[32,1152]{1,0:T(8,128)(2,1)S(1)}, bf16[32,1152]{1,0:T(8,128)(2,1)S(1)}, u32[]{:S(2)}, u32[]{:S(2)}) collective-permute-start(bf16[32,1152]{1,0:T(8,128)(2,1)S(1)} %pad_maximum_fusion.1), channel_id=1, source_target_pairs={{0,2},{1,3},{2,0},{3,1},{4,6},{5,7},{6,4},{7,5},{8,10},{9,11},{10,... | collective-permute-start | bytes 221192 | tf_op jit(solution)/shard_map/ppermute | solution.py:306
  16.1 8.9 %collective-permute-start.7 = (bf16[64,1024]{1,0:T(8,128)(2,1)S(1)}, bf16[64,1024]{1,0:T(8,128)(2,1)S(1)}, u32[]{:S(2)}, u32[]{:S(2)}) collective-permute-start(bf16[64,1024]{1,0:T(8,128)(2,1)S(1)} %pad_maximum_fusion), channel_id=1, source_target_pairs={{0,1},{1,0},{2,3},{3,2},{4,5},{5,4},{6,7},{7,6},{8,9},{9,8},{10,11... | collective-permute-start | bytes 393224 | tf_op jit(solution)/shard_map/ppermute | solution.py:306
  20.4 8.4 %collective-permute-start.4 = (bf16[32,1152]{1,0:T(8,128)(2,1)S(1)}, bf16[32,1152]{1,0:T(8,128)(2,1)S(1)}, u32[]{:S(2)}, u32[]{:S(2)}) collective-permute-start(bf16[32,1152]{1,0:T(8,128)(2,1)S(1)} %pad_maximum_fusion.2), channel_id=1, source_target_pairs={{0,1},{1,0},{2,3},{3,2},{4,5},{5,4},{6,7},{7,6},{8,9},{9,8},{10,11... | collective-permute-start | bytes 221192 | tf_op jit(solution)/shard_map/ppermute | solution.py:306
  21.7 7.1 %copy-start = (bf16[4,64,1024]{2,1,0:T(8,128)(2,1)S(1)}, bf16[4,64,1024]{2,1,0:T(8,128)(2,1)}, u32[]{:S(2)}) copy-start(bf16[4,64,1024]{2,1,0:T(8,128)(2,1)} %param.18) | copy-start | bytes 1572868
  21.7 7.1 %copy-start.1 = (bf16[4,64,1024]{2,1,0:T(8,128)(2,1)S(1)}, bf16[4,64,1024]{2,1,0:T(8,128)(2,1)}, u32[]{:S(2)}) copy-start(bf16[4,64,1024]{2,1,0:T(8,128)(2,1)} %param.19) | copy-start | bytes 1572868
  34.1 6.5 %copy-start.2 = (bf16[4,64,1024]{2,1,0:T(8,128)(2,1)S(1)}, bf16[4,64,1024]{2,1,0:T(8,128)(2,1)}, u32[]{:S(2)}) copy-start(bf16[4,64,1024]{2,1,0:T(8,128)(2,1)} %param.20) | copy-start | bytes 1572868
  34.2 4.9 %collective-permute-start.11 = (bf16[32,1152]{1,0:T(8,128)(2,1)S(1)}, bf16[32,1152]{1,0:T(8,128)(2,1)S(1)}, u32[]{:S(2)}, u32[]{:S(2)}) collective-permute-start(bf16[32,1152]{1,0:T(8,128)(2,1)S(1)} %get-tuple-element.19), channel_id=1, source_target_pairs={{0,1},{1,0},{2,3},{3,2},{4,5},{5,4},{6,7},{7,6},{8,9},{9,8},{10,11... | collective-permute-start | bytes 221192 | tf_op jit(solution)/shard_map/ppermute | solution.py:306
  39.1 6.2 %collective-permute-start.12 = (bf16[32,1152]{1,0:T(8,128)(2,1)S(1)}, bf16[32,1152]{1,0:T(8,128)(2,1)S(1)}, u32[]{:S(2)}, u32[]{:S(2)}) collective-permute-start(bf16[32,1152]{1,0:T(8,128)(2,1)S(1)} %pad_maximum_fusion.3), channel_id=1, source_target_pairs={{0,2},{1,3},{2,0},{3,1},{4,6},{5,7},{6,4},{7,5},{8,10},{9,11},{10,... | collective-permute-start | bytes 221192 | tf_op jit(solution)/shard_map/ppermute | solution.py:306
  39.6 5.8 %collective-permute-start.13 = (bf16[32,1024]{1,0:T(8,128)(2,1)S(1)}, bf16[32,1024]{1,0:T(8,128)(2,1)S(1)}, u32[]{:S(2)}, u32[]{:S(2)}) collective-permute-start(bf16[32,1024]{1,0:T(8,128)(2,1)S(1)} %get-tuple-element.23), channel_id=1, source_target_pairs={{0,1},{1,0},{2,3},{3,2},{4,5},{5,4},{6,7},{7,6},{8,9},{9,8},{10,11... | collective-permute-start | bytes 196616 | tf_op jit(solution)/shard_map/ppermute | solution.py:306
  40.6 12.4 %collective-permute-start.10 = (bf16[256,1024]{1,0:T(8,128)(2,1)S(1)}, bf16[256,1024]{1,0:T(8,128)(2,1)S(1)}, u32[]{:S(2)}, u32[]{:S(2)}) collective-permute-start(bf16[256,1024]{1,0:T(8,128)(2,1)S(1)} %bitcast.9), channel_id=1, source_target_pairs={{0,8},{8,0},{1,9},{9,1},{2,10},{10,2},{3,11},{11,3},{4,12},{12,4},... | collective-permute-start | bytes 1572872 | tf_op jit(solution)/shard_map/ppermute | solution.py:311
  43.3 9.8 %collective-permute-start.15 = (bf16[32,1024]{1,0:T(8,128)(2,1)S(1)}, bf16[32,1024]{1,0:T(8,128)(2,1)S(1)}, u32[]{:S(2)}, u32[]{:S(2)}) collective-permute-start(bf16[32,1024]{1,0:T(8,128)(2,1)S(1)} %get-tuple-element.24), channel_id=1, source_target_pairs={{0,1},{1,0},{2,3},{3,2},{4,5},{5,4},{6,7},{7,6},{8,9},{9,8},{10,11... | collective-permute-start | bytes 196616 | tf_op jit(solution)/shard_map/ppermute | solution.py:306
  44.4 4.9 %collective-permute-start.16 = (bf16[32,1024]{1,0:T(8,128)(2,1)S(1)}, bf16[32,1024]{1,0:T(8,128)(2,1)S(1)}, u32[]{:S(2)}, u32[]{:S(2)}) collective-permute-start(bf16[32,1024]{1,0:T(8,128)(2,1)S(1)} %get-tuple-element.26), channel_id=1, source_target_pairs={{0,1},{1,0},{2,3},{3,2},{4,5},{5,4},{6,7},{7,6},{8,9},{9,8},{10,11... | collective-permute-start | bytes 196616 | tf_op jit(solution)/shard_map/ppermute | solution.py:306
  45.5 8.2 %collective-permute-start.14 = (bf16[32,1152]{1,0:T(8,128)(2,1)S(1)}, bf16[32,1152]{1,0:T(8,128)(2,1)S(1)}, u32[]{:S(2)}, u32[]{:S(2)}) collective-permute-start(bf16[32,1152]{1,0:T(8,128)(2,1)S(1)} %pad_maximum_fusion.4), channel_id=1, source_target_pairs={{0,4},{1,5},{2,6},{3,7},{4,0},{5,1},{6,2},{7,3},{8,12},{9,13},{10,... | collective-permute-start | bytes 221192 | tf_op jit(solution)/shard_map/ppermute | solution.py:306
  49.3 4.3 %collective-permute-start.17 = (bf16[32,1024]{1,0:T(8,128)(2,1)S(1)}, bf16[32,1024]{1,0:T(8,128)(2,1)S(1)}, u32[]{:S(2)}, u32[]{:S(2)}) collective-permute-start(bf16[32,1024]{1,0:T(8,128)(2,1)S(1)} %add_convert_fusion), channel_id=1, source_target_pairs={{0,2},{1,3},{2,0},{3,1},{4,6},{5,7},{6,4},{7,5},{8,10},{9,11},{10,... | collective-permute-start | bytes 196616 | tf_op jit(solution)/shard_map/ppermute | solution.py:306

commit v3 on v1

--- a/solution.py
+++ b/solution.py
@@ -14,8 +14,10 @@
 SMEM = pl.BlockSpec(memory_space=pltpu.SMEM)
 HBM = pl.BlockSpec(memory_space=pltpu.HBM)
 LANES = 128
-PIECES = 2
+PIECES = 4
 GRANT = 24 << 20
+SOON = 2
+BAND = 32
 
 
 def dot(a, b):
@@ -118,50 +120,123 @@
     return total
 
 
-def project_kernel(ks, spans, first, tensor_ref, *rest):
-    given = len(set(i for i, _ in spans))
-    chunks, rest = rest[:given], rest[given:]
-    weight, rest = rest[0], rest[1:]
-    if first:
-        total = 0.0
-    else:
-        total, rest = rest[0][...], rest[1:]
+def project_kernel(ks, held_count, spans, given, tensor_ref, *rest):
+    arrays, rest = rest[:given], rest[given:]
+    weight, before, rest = rest[0], rest[1], rest[2:]
+    if held_count:
+        held, rest = rest[0], rest[1:]
     out_ref, buf, sems = rest
     rows = out_ref.shape[0]
-    copies = [weight_copies(weight, buf, sems, j, tensor_ref[0] ^ k, 0) for j, k in enumerate(ks)]
-    for pieces in copies:
-        for c in pieces:
-            c.start()
+    width = buf.shape[1]
+    later = ks[held_count:]
+    copies = [weight_copies(weight, buf, sems, j, tensor_ref[0] ^ k, 0) for j, k in enumerate(later)]
+    for c in sum(copies, []):
+        c.start()
+    total = before[...]
     for j, (i, r) in enumerate(spans):
-        total = block_dot(
-            lambda a, n, i=i, r=r: chunks[i][r : r + rows, a : a + n], buf, j, copies[j], total
-        )
+        if j < held_count:
+            total = total + dot(arrays[i][r : r + rows, :width], held[j])
+        else:
+            total = block_dot(
+                lambda a, n, i=i, r=r: arrays[i][r : r + rows, a : a + n],
+                buf,
+                j - held_count,
+                copies[j - held_count],
+                total,
+            )
     out_ref[...] = total
 
 
-def project_call(where, ks, tensor_at, weight, before, rows, width):
-    wide = weight.shape[1]
-    count = len(ks)
+def project_call(where, ks, tensor_at, weight, before, width, held=None):
+    rows, wide = before.shape
     arrays, spans = [], []
     for k in ks:
         array, r = where[k]
         if not any(a is array for a in arrays):
             arrays.append(array)
         spans.append(([a is array for a in arrays].index(True), r))
-    extra = [] if before is None else [before]
+    extra = [] if held is None else [held]
+    held_count = 0 if held is None else held.shape[0]
+    count = len(ks) - held_count
     return pl.pallas_call(
-        functools.partial(project_kernel, ks, spans, before is None),
-        in_specs=[SMEM] + [VMEM] * len(arrays) + [HBM] + [VMEM] * len(extra),
+        functools.partial(project_kernel, ks, held_count, spans, len(arrays)),
+        in_specs=[SMEM] + [VMEM] * len(arrays) + [HBM] + [VMEM] * (1 + len(extra)),
         out_specs=VMEM,
         out_shape=jax.ShapeDtypeStruct((rows, wide), jnp.float32),
         scratch_shapes=[
             pltpu.VMEM((count, width, wide), weight.dtype),
             pltpu.SemaphoreType.DMA((count, PIECES)),
         ],
-        **params(
-            (2 * count * rows * width * wide, 2 * count * width * wide),
-        ),
-    )(tensor_at, *arrays, in_hbm(weight), *extra)
+        **params((2 * len(ks) * rows * width * wide, 2 * count * width * wide)),
+    )(tensor_at, *arrays, in_hbm(weight), before, *extra)
+
+
+def lead_kernel(k, ahead, tensor_ref, chunk, weight, out_ref, ahead_ref, buf, sems, ahead_sems):
+    copies = weight_copies(weight, buf, sems, 0, tensor_ref[0] ^ k, 0)
+    later = [
+        weight_copies(weight, ahead_ref, ahead_sems, j, tensor_ref[0] ^ a, 0)
+        for j, a in enumerate(ahead)
+    ]
+    for c in copies + sum(later, []):
+        c.start()
+    out_ref[...] = block_dot(lambda a, n: chunk[:, a : a + n], buf, 0, copies, 0.0)
+    for c in sum(later, []):
+        c.wait()
+
+
+def lead_call(chunk, k, ahead, tensor_at, weight):
+    rows, width = chunk.shape
+    wide = weight.shape[1]
+    return pl.pallas_call(
+        functools.partial(lead_kernel, k, ahead),
+        in_specs=[SMEM, VMEM, HBM],
+        out_specs=[VMEM] * 2,
+        out_shape=[
+            jax.ShapeDtypeStruct((rows, wide), jnp.float32),
+            jax.ShapeDtypeStruct((len(ahead), width, wide), weight.dtype),
+        ],
+        scratch_shapes=[
+            pltpu.VMEM((1, width, wide), weight.dtype),
+            pltpu.SemaphoreType.DMA((1, PIECES)),
+            pltpu.SemaphoreType.DMA((len(ahead), PIECES)),
+        ],
+        name="lead",
+        **params((2 * rows * width * wide, 2 * (1 + len(ahead)) * width * wide)),
+    )(tensor_at, chunk, in_hbm(weight))
+
+
+def held_kernel(count, ahead, tensor_ref, *refs):
+    chunks, refs = refs[:count], refs[count:]
+    held, before, weight, out_ref, ahead_ref, ahead_sems = refs
+    later = [
+        weight_copies(weight, ahead_ref, ahead_sems, j, tensor_ref[0] ^ a, 0)
+        for j, a in enumerate(ahead)
+    ]
+    for c in sum(later, []):
+        c.start()
+    rows, width = out_ref.shape[0], held.shape[1]
+    total = before[...]
+    for j in range(count):
+        total = total + dot(chunks[j][:rows, :width], held[j])
+    out_ref[...] = total
+    for c in sum(later, []):
+        c.wait()
+
+
+def held_call(chunks, held, before, ahead, tensor_at, weight):
+    _, width, wide = held.shape
+    return pl.pallas_call(
+        functools.partial(held_kernel, len(chunks), ahead),
+        in_specs=[SMEM] + [VMEM] * (len(chunks) + 2) + [HBM],
+        out_specs=[VMEM] * 2,
+        out_shape=[
+            jax.ShapeDtypeStruct(before.shape, before.dtype),
+            jax.ShapeDtypeStruct((len(ahead), width, wide), weight.dtype),
+        ],
+        scratch_shapes=[pltpu.SemaphoreType.DMA((len(ahead), PIECES))],
+        name="held",
+        **params((2 * before.size * width * len(chunks), 2 * len(ahead) * width * wide), 8 << 20),
+    )(tensor_at, *chunks, held, before, in_hbm(weight))
 
 
 def mix_kernel(sizes, *refs):
@@ -196,28 +271,27 @@
         c.wait()
     total = before[...] + 0.5 * lora_of(low[...], [up_buf.at[i] for i in range(maps)], picked)
     total = block_dot(lambda a, n: chunk[:, a : a + n], buf_in, 0, copies_in, total)
-    query = total.astype(jnp.bfloat16)
     for c in kv_copies:
         c.wait()
     length = k_buf.shape[2]
-    heads = [None] * (kv_count * group)
-    alive = jnp.concatenate([live[...]] * group, axis=0) > 0
-    for kvh in range(kv_count):
-        flat_k = k_buf[:, kvh].reshape(rows * length, head)
-        flat_v = v_buf[:, kvh].reshape(rows * length, head)
-        q = jnp.concatenate(
-            [query[:, (kvh * group + g) * head : (kvh * group + g + 1) * head] for g in range(group)],
-            axis=0,
-        )
-        scores = dot_t(q, flat_k) / math.sqrt(head)
-        scores = jnp.where(alive, scores, -1e30)
-        top = jnp.max(scores, axis=1, keepdims=True)
-        weights = jnp.exp(scores - top)
-        probs = (weights / jnp.sum(weights, axis=1, keepdims=True)).astype(jnp.bfloat16)
-        got = dot(probs, flat_v).astype(jnp.bfloat16)
-        for g in range(group):
-            heads[kvh * group + g] = got[g * rows : (g + 1) * rows]
-    mixed = jnp.concatenate(heads, axis=1)
+    bands = []
+    for r in range(0, rows, BAND):
+        alive = jnp.concatenate([live[r : r + BAND, :]] * group, axis=0) > 0
+        heads = []
+        for kvh in range(kv_count):
+            flat_k = k_buf[r : r + BAND, kvh].reshape(BAND * length, head)
+            flat_v = v_buf[r : r + BAND, kvh].reshape(BAND * length, head)
+            at = [slice((kvh * group + g) * head, (kvh * group + g + 1) * head) for g in range(group)]
+            q = jnp.concatenate([total[r : r + BAND, span] for span in at], axis=0)
+            scores = dot_t(q.astype(jnp.bfloat16), flat_k) * (1.0 / math.sqrt(head))
+            scores = jnp.where(alive, scores, -1e30)
+            top = jnp.max(scores, axis=1, keepdims=True)
+            weights = jnp.exp(scores - top)
+            probs = weights * (1.0 / jnp.sum(weights, axis=1, keepdims=True))
+            got = dot(probs.astype(jnp.bfloat16), flat_v)
+            heads += [got[g * BAND : (g + 1) * BAND] for g in range(group)]
+        bands.append(jnp.concatenate(heads, axis=1))
+    mixed = jnp.concatenate(bands, axis=0).astype(jnp.bfloat16)
     mixed_out[...] = mixed
     for c in down_copies:
         c.wait()
@@ -266,8 +340,7 @@
     ups, rest = rest[:maps], rest[maps:]
     lows, rest = rest[: count[0]], rest[count[0] :]
     terms, rest = rest[: count[1]], rest[count[1] :]
-    out_ref, up_buf, sems = rest
-    copies = load_all([(u, up_buf.at[i]) for i, u in enumerate(ups)], sems)
+    (out_ref,) = rest
     low = low_ref[...]
     total = 0.0
     for ref in lows:
@@ -275,9 +348,7 @@
     total = lows[-1][:, :wide].astype(jnp.float32)
     for t in terms:
         total = total + t[:, :wide].astype(jnp.float32)
-    for c in copies:
-        c.wait()
-    total = total + 0.5 * lora_of(low, [up_buf.at[i] for i in range(maps)], picks_ref[...])
+    total = total + 0.5 * lora_of(low, ups, picks_ref[...])
     out_ref[...] = total.astype(out_ref.dtype)
 
 
@@ -333,9 +404,10 @@
         ],
         axis=1,
     )
-    column = lax.broadcasted_iota(jnp.int32, (rows, rows * length), 1)
-    row = lax.broadcasted_iota(jnp.int32, (rows, rows * length), 0)
-    live = ((column // length == row) & (column % length < kv_lengths[:, None])).astype(jnp.float32)
+    column = lax.broadcasted_iota(jnp.int32, (rows, BAND * length), 1)
+    row = lax.broadcasted_iota(jnp.int32, (rows, BAND * length), 0)
+    live = (column // length == row % BAND) & (column % length < kv_lengths[:, None])
+    live = live.astype(jnp.float32)
 
     query_down = with_swapped(query_down_maps)
     query_up = with_swapped(query_up_maps)
@@ -346,15 +418,15 @@
     where = {0: (near, 0)}
     chain = 0
     for bit in reversed(bits):
-        rest = [k for k in where if k not in (0, chain)]
-        where[bit] = (across(hidden, bit), 0)
-        if chain:
+        rest = [k for k in where if k != chain]
+        if chain == 0:
+            where[bit] = (across(hidden, bit), 0)
+            low = low + across(low, bit)
+        else:
             joined = jnp.concatenate([where[chain][0][:, :width], low.astype(jnp.bfloat16)], axis=1)
             got = across(joined, bit)
             where[chain | bit] = (got, 0)
             low = low + got[:, width:].astype(jnp.float32)
-        else:
-            low = low + across(low, bit)
         if rest and bit == 1:
             got = jnp.concatenate([where[k][0][:, :width] for k in rest], axis=0)
             got = across(got, 1)
@@ -362,18 +434,17 @@
                 where[k | 1] = (got, i * rows)
         else:
             for k in rest:
-                where[k | bit] = (across(where[k][0][:, :width], bit), 0)
+                array = hidden if k == 0 else where[k][0][:, :width]
+                where[k | bit] = (across(array, bit), 0)
         chain |= bit
 
-    top = bits[-1] if bits else 0
-    order = sorted(where, key=lambda k: (bin(k).count("1"), -k))
-    last = order[-1]
-    early = order[:-1]
-    first = [k for k in early if k in (0, top >> 1, top)]
-    others = [k for k in early if k not in first]
-    query = project_call(where, first, tensor_at, w_query, None, rows, width)
-    for i in range(0, len(others), 6):
-        query = project_call(where, others[i : i + 6], tensor_at, w_query, query, rows, width)
+    last = chain
+    ahead = [k for k in where if k and not k & 1 and k != last ^ 1]
+    second = [last ^ 1] + [k for k in where if k & 1 and k != last]
+    query, held = lead_call(near, 0, ahead, tensor_at, w_query)
+    chunks = [where[k][0] for k in ahead]
+    query, held = held_call(chunks, held, query, second[:SOON], tensor_at, w_query)
+    query = project_call(where, second, tensor_at, w_query, query, width, held)
 
     wide = w_query.shape[1]
     local_heads = wide // head
@@ -464,13 +535,9 @@
     terms = [parts[0]] + [came[1 << i] for i in range(len(bits) - 1)]
     return pl.pallas_call(
         functools.partial(final_kernel, out_width, (len(lows), len(terms)), replicas),
-        in_specs=[VMEM, VMEM] + [HBM] * replicas + [VMEM] * (len(lows) + len(terms)),
+        in_specs=[VMEM] * (2 + replicas + len(lows) + len(terms)),
         out_specs=VMEM,
         out_shape=jax.ShapeDtypeStruct((rows, out_width), jnp.bfloat16),
-        scratch_shapes=[
-            pltpu.VMEM((replicas,) + map_in, keys.dtype),
-            pltpu.SemaphoreType.DMA((replicas,)),
-        ],
         name="final",
         **params((10**8, 10**6)),
     )(picks, low2, *output_up, *lows, *terms)

time: 50.8 us -> 50.9 us (level)
  starting transfers between devices: 15.2 us -> 14.3 us
  waiting for transfers between devices: 11.3 us -> 11.9 us
    pallas_call x2 -> x3, Pallas kernels: 7.01 us -> 8.24 us  [the longest x1 2.93 us: lead_call(): pl.pallas_call(functools.partial(lead_kernel, k, ahead), in_specs=[SMEM,...]
    ppermute x13 -> x12, starting transfers between devices: 14.7 us -> 13.8 us  [across(): return lax.ppermute(x, 'tensor', [(i, i ^ bit) for i in range(shards)])]
    pallas_call x3, Pallas kernels: 8.07 us -> 7.34 us  [out_call(): pl.pallas_call(functools.partial(out_kernel, ks, spans), in_specs=[SMEM,...]
    ppermute x13 -> x12, waiting for transfers between devices: 10.6 us -> 11.3 us  [across(): return lax.ppermute(x, 'tensor', [(i, i ^ bit) for i in range(shards)])]
  transfers between devices with their start and end apart: 17 -> 16, of which waited for: 6 -> 9; matrix products, arithmetic and copies ran while one was open for 4% -> 4% of each run, Pallas kernels for 33% -> 34%
where the time goes in v3:
time: 50.9 us; the launch traced here: 50.6 us
  Pallas kernels  22.3 us (44%)
  starting transfers between devices  14.3 us (28%)
  waiting for transfers between devices  11.9 us (23%)
  other arithmetic  1.75 us (3%)
    ppermute x12, starting transfers between devices, across(): return lax.ppermute(x, 'tensor', [(i, i ^ bit) for i in range(shards)])  13.8 us
    ppermute x12, waiting for transfers between devices, across(): return lax.ppermute(x, 'tensor', [(i, i ^ bit) for i in range(shards)])  11.3 us
    pallas_call x3, Pallas kernels, out_call(): pl.pallas_call(functools.partial(out_kernel, ks, spans), in_specs=[SMEM,...  7.34 us
    pallas_call x1, Pallas kernels, per_device(): pl.pallas_call(functools.partial(mix_kernel, sizes), in_specs=[SMEM, VMEM...  4.29 us
    pallas_call x1, Pallas kernels, lead_call(): pl.pallas_call(functools.partial(lead_kernel, k, ahead), in_specs=[SMEM,...  2.93 us
    pallas_call x1, Pallas kernels, held_call(): pl.pallas_call(functools.partial(held_kernel, len(chunks), ahead), in_spe...  2.68 us
    pallas_call x1, Pallas kernels, project_call(): pl.pallas_call(functools.partial(project_kernel, ks, held_count, spans, l...  2.63 us
    pallas_call x1, Pallas kernels, low_call(): pl.pallas_call(functools.partial(low_kernel, len(downs)), in_specs=[HBM,...  1.53 us
  transfers between devices with their start and end apart: 16, of which 9 were waited for; matrix products, arithmetic and copies ran while one was open for 4% of the time, Pallas kernels for 34%

profile of v3, /device:TPU:0, one launch (start us, length us, event | category | flops | bytes accessed | tf_op | source)
XLA Modules:
  0.0 50.6 jit_solution(18046093407996463611)
XLA Ops:
  0.0 4.1 %collective-permute-start = (bf16[32,1024]{1,0:T(8,128)(2,1)}, bf16[32,1024]{1,0:T(8,128)(2,1)S(1)}, u32[]{:S(2)}, u32[]{:S(2)}) collective-permute-start(bf16[32,1024]{1,0:T(8,128)(2,1)} %x_hbm.1), channel_id=1, source_target_pairs={{0,4},{1,5},{2,6},{3,7},{4,0},{5,1},{6,2},{7,3},{8,12},{9,13},{10,... | collective-permute-start | bytes 196616 | tf_op jit(solution)/shard_map/ppermute | solution.py:387
  4.1 1.6 %collective-permute-start.5 = (bf16[32,1024]{1,0:T(8,128)(2,1)}, bf16[32,1024]{1,0:T(8,128)(2,1)S(1)}, u32[]{:S(2)}, u32[]{:S(2)}) collective-permute-start(bf16[32,1024]{1,0:T(8,128)(2,1)} %x_hbm.1), channel_id=1, source_target_pairs={{0,2},{1,3},{2,0},{3,1},{4,6},{5,7},{6,4},{7,5},{8,10},{9,11},{10,... | collective-permute-start | bytes 196616 | tf_op jit(solution)/shard_map/ppermute | solution.py:387
  5.6 0.0 collective-permute-start.1
  5.6 0.5 %collective-permute-start.7 = (bf16[256,1024]{1,0:T(8,128)(2,1)}, bf16[256,1024]{1,0:T(8,128)(2,1)S(1)}, u32[]{:S(2)}, u32[]{:S(2)}) collective-permute-start(bf16[256,1024]{1,0:T(8,128)(2,1)} %bitcast.5), channel_id=1, source_target_pairs={{0,8},{8,0},{1,9},{9,1},{2,10},{10,2},{3,11},{11,3},{4,12},{12,4},... | collective-permute-start | bytes 1572872 | tf_op jit(solution)/shard_map/ppermute | solution.py:392
  6.2 0.0 collective-permute-start.8
  6.2 0.8 %select_reduce_fusion = s32[64]{0:T(128)S(1)} fusion(s32[8]{0:T(128)} %param.22, s32[64]{0:T(128)} %param.21), kind=kLoop, calls=%fused_computation.30 | loop fusion | flops 1472 | bytes 544 | tf_op jit(solution)/shard_map/reduce_sum | solution.py:397
  7.0 0.1 dynamic_slice.3
  7.0 0.1 broadcast_compare_fusion.1
  7.1 0.6 %collective-permute-done.1.rest_1_ = bf16[256,1024]{1,0:T(8,128)(2,1)S(1)} collective-permute-done((bf16[256,1024]{1,0:T(8,128)(2,1)}, bf16[256,1024]{1,0:T(8,128)(2,1)S(1)}, u32[]{:S(2)}, u32[]{:S(2)}) %collective-permute-start.1) | collective-permute-done | bytes 524320 | tf_op jit(solution)/shard_map/ppermute | solution.py:392
  7.8 1.5 %low.1 = (f32[32,128]{1,0:T(8,128)S(1)}, bf16[32,1024]{1,0:T(8,128)(2,1)S(1)}) custom-call(bf16[32,1024]{1,0:T(8,128)(2,1)} %x_hbm.1, f32[32,512]{1,0:T(8,128)S(1)} %add_convert_fusion.3.picks_ref.refs_6_, bf16[256,1024]{1,0:T(8,128)(2,1)} %bitcast.12, bf16[256,1024]{1,0:T(8,128)(2,1)S(1)} %collective-permute-done.1.rest_1_), custom_call_target="tpu_custom_call" | custom-call | flops 100000000 | bytes 1000000 | tf_op jit(solution)/shard_map/low/pallas_call | solution.py:83
  9.3 0.4 collective-permute-start.2
  9.7 4.4 %collective-permute-done.2 = f32[32,128]{1,0:T(8,128)S(1)} collective-permute-done((f32[32,128]{1,0:T(8,128)S(1)}, f32[32,128]{1,0:T(8,128)S(1)}, u32[]{:S(2)}, u32[]{:S(2)}) %collective-permute-start.2) | collective-permute-done | bytes 16416 | tf_op jit(solution)/shard_map/ppermute | solution.py:387
  14.1 0.0 collective-permute-done.refs_0_
  14.1 0.5 collective-permute-start.3
  14.6 0.7 %fusion.1.refs_13_ = f32[32,1024]{1,0:T(8,128)S(1)} fusion(s32[32]{0:T(128)} %param.23, s32[1024]{0:T(1024)S(1)} %get-tuple-element.40, s32[1024]{0:T(1024)S(1)} %get-tuple-element.41, s32[32]{0:T(128)S(1)} %get-tuple-element.45, s32[32]{0:T(128)S(1)} %get-tuple-element.46, s32[1024]{0:T(1024)S(1)} %get-tuple-element.39, s32[1024]{0:T(1024)S(1)} %get-tuple-element.42, ...), kind=kLoop, calls=%fused_computation.7 | loop fusion | flops 229376 | bytes 149920 | tf_op jit(solution)/shard_map/convert_element_type | solution.py:410
  15.3 3.2 %collective-permute-done.3.rest_0_ = bf16[32,1152]{1,0:T(8,128)(2,1)S(1)} collective-permute-done((bf16[32,1152]{1,0:T(8,128)(2,1)S(1)}, bf16[32,1152]{1,0:T(8,128)(2,1)S(1)}, u32[]{:S(2)}, u32[]{:S(2)}) %collective-permute-start.3) | collective-permute-done | bytes 73760 | tf_op jit(solution)/shard_map/ppermute | solution.py:387
  18.5 1.6 %collective-permute-start.4 = (bf16[32,1152]{1,0:T(8,128)(2,1)S(1)}, bf16[32,1152]{1,0:T(8,128)(2,1)S(1)}, u32[]{:S(2)}, u32[]{:S(2)}) collective-permute-start(bf16[32,1152]{1,0:T(8,128)(2,1)S(1)} %pad_maximum_fusion.2), channel_id=1, source_target_pairs={{0,1},{1,0},{2,3},{3,2},{4,5},{5,4},{6,7},{7,6},{8,9},{9,8},{10,11... | collective-permute-start | bytes 221192 | tf_op jit(solution)/shard_map/ppermute | solution.py:387
  20.1 0.0 collective-permute-done.5.refs_1_
  20.2 0.6 %collective-permute-start.6 = (bf16[96,1024]{1,0:T(8,128)(2,1)S(1)}, bf16[96,1024]{1,0:T(8,128)(2,1)S(1)}, u32[]{:S(2)}, u32[]{:S(2)}) collective-permute-start(bf16[96,1024]{1,0:T(8,128)(2,1)S(1)} %pad_maximum_fusion), channel_id=1, source_target_pairs={{0,1},{1,0},{2,3},{3,2},{4,5},{5,4},{6,7},{7,6},{8,9},{9,8},{10,11... | collective-permute-start | bytes 589832 | tf_op jit(solution)/shard_map/ppermute | solution.py:387
  20.7 2.9 %lead.1 = (f32[32,1024]{1,0:T(8,128)S(1)}, bf16[2,1024,1024]{2,1,0:T(8,128)(2,1)S(1)}) custom-call(s32[1]{0:T(128)} %bitcast.tensor_ref.refs_0_, bf16[32,1024]{1,0:T(8,128)(2,1)S(1)} %get-tuple-element.19.chunk, bf16[8192,1024]{1,0:T(8,128)(2,1)} %refs_2_.1), custom_call_target="tpu_custom_call" | custom-call | flops 67108864 | bytes 6291456 | tf_op jit(solution)/shard_map/lead/pallas_call | solution.py:190
  23.7 2.7 %held.1 = (f32[32,1024]{1,0:T(8,128)S(1)}, bf16[2,1024,1024]{2,1,0:T(8,128)(2,1)S(1)}) custom-call(s32[1]{0:T(128)} %bitcast.tensor_ref.refs_0_, bf16[32,1024]{1,0:T(8,128)(2,1)S(1)} %collective-permute-done.refs_0_, bf16[32,1024]{1,0:T(8,128)(2,1)S(1)} %collective-permute-done.5.refs_1_, bf16[2,1024,1024]{2,1,0:T(8,128)(2,1)S(1)} %get-tuple-element.20.refs_2_, ...), custom_call_target="tpu_custom_call" | custom-call | flops 134217728 | bytes 4194304 | tf_op jit(solution)/shard_map/held/pallas_call | solution.py:228
  26.4 0.0 collective-permute-done.4.refs_1_
  26.4 0.0 collective-permute-done.6.rest_1_
  26.4 0.0 copy-start
  26.4 0.0 copy-start.1
  26.4 2.6 %shard_map.118.refs_4_ = f32[32,1024]{1,0:T(8,128)S(1)} custom-call(s32[1]{0:T(128)} %bitcast.tensor_ref.refs_0_, bf16[32,1152]{1,0:T(8,128)(2,1)S(1)} %collective-permute-done.3.rest_0_, bf16[96,1024]{1,0:T(8,128)(2,1)S(1)} %collective-permute-done.6.rest_1_, bf16[8192,1024]{1,0:T(8,128)(2,1)} %refs_2_.1, f32[32,1024]{1,0:T(8,128)S(1)} %get-tuple-element.22.rest_3_, ...), custom_call_target="tpu_custom_call" | custom-call | flops 268435456 | bytes 4194304 | tf_op jit(solution)/shard_map/pallas_call | solution.py:161
  29.1 0.0 collective-permute-done.7.refs_8_
  29.1 0.0 collective-permute-done.8.refs_10_
  29.1 0.0 copy-done
  29.1 0.0 copy-done.1
  29.1 4.3 %mix.1 = (f32[32,128]{1,0:T(8,128)S(1)}, bf16[32,1024]{1,0:T(8,128)(2,1)S(1)}, bf16[32,1152]{1,0:T(8,128)(2,1)S(1)}, f32[32,1024]{1,0:T(8,128)S(1)}) custom-call(s32[1]{0:T(128)} %bitcast.tensor_ref.refs_0_, bf16[32,1152]{1,0:T(8,128)(2,1)S(1)} %collective-permute-done.4.refs_1_, bf16[8192,1024]{1,0:T(8,128)(2,1)} %refs_2_.1, bf16[1024,8192]{1,0:T(8,128)(2,1)} %weight.7, ...), custom_call_target="tpu_custom_call" | custom-call | flops 1000000000 | bytes 6291456 | tf_op jit(solution)/shard_map/mix/pallas_call | solution.py:461
  33.4 1.6 %collective-permute-start.10 = (bf16[32,1152]{1,0:T(8,128)(2,1)S(1)}, bf16[32,1152]{1,0:T(8,128)(2,1)S(1)}, u32[]{:S(2)}, u32[]{:S(2)}) collective-permute-start(bf16[32,1152]{1,0:T(8,128)(2,1)S(1)} %get-tuple-element.25), channel_id=1, source_target_pairs={{0,1},{1,0},{2,3},{3,2},{4,5},{5,4},{6,7},{7,6},{8,9},{9,8},{10,11... | collective-permute-start | bytes 221192 | tf_op jit(solution)/shard_map/ppermute | solution.py:387
  35.0 0.0 copy-start.2
  35.0 2.5 %shard_map.120 = bf16[64,1024]{1,0:T(8,128)(2,1)S(1)} custom-call(s32[1]{0:T(128)} %bitcast.tensor_ref.refs_0_, bf16[32,1024]{1,0:T(8,128)(2,1)S(1)} %get-tuple-element.27.x_ref, bf16[1024,8192]{1,0:T(8,128)(2,1)} %weight.7), custom_call_target="tpu_custom_call" | custom-call | flops 134217728 | bytes 4194304 | tf_op jit(solution)/shard_map/pallas_call | solution.py:326
  37.5 0.6 %collective-permute-start.12 = (bf16[64,1024]{1,0:T(8,128)(2,1)S(1)}, bf16[64,1024]{1,0:T(8,128)(2,1)S(1)}, u32[]{:S(2)}, u32[]{:S(2)}) collective-permute-start(bf16[64,1024]{1,0:T(8,128)(2,1)S(1)} %shard_map.120), channel_id=1, source_target_pairs={{0,1},{1,0},{2,3},{3,2},{4,5},{5,4},{6,7},{7,6},{8,9},{9,8},{10,11... | collective-permute-start | bytes 393224 | tf_op jit(solution)/shard_map/ppermute | solution.py:387
  38.0 0.4 collective-permute-done.10.rest_2_
  38.5 0.5 collective-permute-start.11
  39.0 0.0 copy-done.2
  39.0 0.0 collective-permute-start.9
  39.0 3.1 %shard_map.119 = (f32[32,1024]{1,0:T(8,128)S(1)}, f32[32,1024]{1,0:T(8,128)S(1)}, bf16[32,1024]{1,0:T(8,128)(2,1)S(1)}) custom-call(s32[1]{0:T(128)} %bitcast.tensor_ref.refs_0_, bf16[32,1024]{1,0:T(8,128)(2,1)S(1)} %get-tuple-element.27.x_ref, bf16[1024,8192]{1,0:T(8,128)(2,1)} %weight.7), custom_call_target="tpu_custom_call" | custom-call | flops 201326592 | bytes 6291456 | tf_op jit(solution)/shard_map/pallas_call | solution.py:326
  42.1 0.4 collective-permute-done.12
  42.5 0.4 collective-permute-done.11.rest_3_
  43.0 0.3 collective-permute-start.13
  43.4 1.4 %collective-permute-start.14 = (bf16[32,1024]{1,0:T(8,128)(2,1)S(1)}, bf16[32,1024]{1,0:T(8,128)(2,1)S(1)}, u32[]{:S(2)}, u32[]{:S(2)}) collective-permute-start(bf16[32,1024]{1,0:T(8,128)(2,1)S(1)} %get-tuple-element.29), channel_id=1, source_target_pairs={{0,1},{1,0},{2,3},{3,2},{4,5},{5,4},{6,7},{7,6},{8,9},{9,8},{10,11... | collective-permute-start | bytes 196616 | tf_op jit(solution)/shard_map/ppermute | solution.py:387
  44.7 0.8 %collective-permute-start.15 = (bf16[32,1024]{1,0:T(8,128)(2,1)S(1)}, bf16[32,1024]{1,0:T(8,128)(2,1)S(1)}, u32[]{:S(2)}, u32[]{:S(2)}) collective-permute-start(bf16[32,1024]{1,0:T(8,128)(2,1)S(1)} %get-tuple-element.33), channel_id=1, source_target_pairs={{0,2},{1,3},{2,0},{3,1},{4,6},{5,7},{6,4},{7,5},{8,10},{9,11},{10,... | collective-permute-start | bytes 196616 | tf_op jit(solution)/shard_map/ppermute | solution.py:387
  45.5 1.8 %shard_map.121.rest_5_ = f32[32,1024]{1,0:T(8,128)S(1)} custom-call(s32[1]{0:T(128)} %bitcast.tensor_ref.refs_0_, bf16[32,1024]{1,0:T(8,128)(2,1)S(1)} %get-tuple-element.27.x_ref, bf16[1024,8192]{1,0:T(8,128)(2,1)} %weight.7), custom_call_target="tpu_custom_call" | custom-call | flops 67108864 | bytes 2097152 | tf_op jit(solution)/shard_map/pallas_call | solution.py:326
  47.3 0.0 collective-permute-done.9.rest_1_
  47.3 0.3 collective-permute-done.14.rest_6_
  47.6 1.7 %collective-permute-done.15.rest_7_ = bf16[32,1024]{1,0:T(8,128)(2,1)S(1)} collective-permute-done((bf16[32,1024]{1,0:T(8,128)(2,1)S(1)}, bf16[32,1024]{1,0:T(8,128)(2,1)S(1)}, u32[]{:S(2)}, u32[]{:S(2)}) %collective-permute-start.15) | collective-permute-done | bytes 65568 | tf_op jit(solution)/shard_map/ppermute | solution.py:387
  49.3 0.4 collective-permute-done.13.rest_4_
  49.7 0.9 %final.1 = bf16[32,1024]{1,0:T(8,128)(2,1)} custom-call(f32[32,512]{1,0:T(8,128)S(1)} %add_convert_fusion.3.picks_ref.refs_6_, f32[32,128]{1,0:T(8,128)S(1)} %get-tuple-element.24.low_ref, bf16[256,1024]{1,0:T(8,128)(2,1)S(1)} %bitcast.10, bf16[256,1024]{1,0:T(8,128)(2,1)S(1)} %collective-permute-done.9.rest_1_, ...), custom_call_target="tpu_custom_call" | custom-call | flops 100000000 | bytes 1000000 | tf_op jit(solution)/shard_map/final/pallas_call | solution.py:536
  (20 shorter events, 0.2 us)
Async XLA Ops:
  0.0 14.1 %collective-permute-start = (bf16[32,1024]{1,0:T(8,128)(2,1)}, bf16[32,1024]{1,0:T(8,128)(2,1)S(1)}, u32[]{:S(2)}, u32[]{:S(2)}) collective-permute-start(bf16[32,1024]{1,0:T(8,128)(2,1)} %x_hbm.1), channel_id=1, source_target_pairs={{0,4},{1,5},{2,6},{3,7},{4,0},{5,1},{6,2},{7,3},{8,12},{9,13},{10,... | collective-permute-start | bytes 196616 | tf_op jit(solution)/shard_map/ppermute | solution.py:387
  4.1 16.1 %collective-permute-start.5 = (bf16[32,1024]{1,0:T(8,128)(2,1)}, bf16[32,1024]{1,0:T(8,128)(2,1)S(1)}, u32[]{:S(2)}, u32[]{:S(2)}) collective-permute-start(bf16[32,1024]{1,0:T(8,128)(2,1)} %x_hbm.1), channel_id=1, source_target_pairs={{0,2},{1,3},{2,0},{3,1},{4,6},{5,7},{6,4},{7,5},{8,10},{9,11},{10,... | collective-permute-start | bytes 196616 | tf_op jit(solution)/shard_map/ppermute | solution.py:387
  5.6 2.1 %collective-permute-start.1 = (bf16[256,1024]{1,0:T(8,128)(2,1)}, bf16[256,1024]{1,0:T(8,128)(2,1)S(1)}, u32[]{:S(2)}, u32[]{:S(2)}) collective-permute-start(bf16[256,1024]{1,0:T(8,128)(2,1)} %bitcast.11), channel_id=1, source_target_pairs={{0,8},{8,0},{1,9},{9,1},{2,10},{10,2},{3,11},{11,3},{4,12},{12,4},... | collective-permute-start | bytes 1572872 | tf_op jit(solution)/shard_map/ppermute | solution.py:392
  5.6 23.4 %collective-permute-start.7 = (bf16[256,1024]{1,0:T(8,128)(2,1)}, bf16[256,1024]{1,0:T(8,128)(2,1)S(1)}, u32[]{:S(2)}, u32[]{:S(2)}) collective-permute-start(bf16[256,1024]{1,0:T(8,128)(2,1)} %bitcast.5), channel_id=1, source_target_pairs={{0,8},{8,0},{1,9},{9,1},{2,10},{10,2},{3,11},{11,3},{4,12},{12,4},... | collective-permute-start | bytes 1572872 | tf_op jit(solution)/shard_map/ppermute | solution.py:392
  6.2 22.9 %collective-permute-start.8 = (bf16[256,1024]{1,0:T(8,128)(2,1)}, bf16[256,1024]{1,0:T(8,128)(2,1)S(1)}, u32[]{:S(2)}, u32[]{:S(2)}) collective-permute-start(bf16[256,1024]{1,0:T(8,128)(2,1)} %bitcast.7), channel_id=1, source_target_pairs={{0,8},{8,0},{1,9},{9,1},{2,10},{10,2},{3,11},{11,3},{4,12},{12,4},... | collective-permute-start | bytes 1572872 | tf_op jit(solution)/shard_map/ppermute | solution.py:392
  9.3 4.8 %collective-permute-start.2 = (f32[32,128]{1,0:T(8,128)S(1)}, f32[32,128]{1,0:T(8,128)S(1)}, u32[]{:S(2)}, u32[]{:S(2)}) collective-permute-start(f32[32,128]{1,0:T(8,128)S(1)} %get-tuple-element.18), channel_id=1, source_target_pairs={{0,4},{1,5},{2,6},{3,7},{4,0},{5,1},{6,2},{7,3},{8,12},{9,13},{10,... | collective-permute-start | bytes 49160 | tf_op jit(solution)/shard_map/ppermute | solution.py:387
  14.1 4.4 %collective-permute-start.3 = (bf16[32,1152]{1,0:T(8,128)(2,1)S(1)}, bf16[32,1152]{1,0:T(8,128)(2,1)S(1)}, u32[]{:S(2)}, u32[]{:S(2)}) collective-permute-start(bf16[32,1152]{1,0:T(8,128)(2,1)S(1)} %pad_maximum_fusion.1), channel_id=1, source_target_pairs={{0,2},{1,3},{2,0},{3,1},{4,6},{5,7},{6,4},{7,5},{8,10},{9,11},{10,... | collective-permute-start | bytes 221192 | tf_op jit(solution)/shard_map/ppermute | solution.py:387
  18.5 7.8 %collective-permute-start.4 = (bf16[32,1152]{1,0:T(8,128)(2,1)S(1)}, bf16[32,1152]{1,0:T(8,128)(2,1)S(1)}, u32[]{:S(2)}, u32[]{:S(2)}) collective-permute-start(bf16[32,1152]{1,0:T(8,128)(2,1)S(1)} %pad_maximum_fusion.2), channel_id=1, source_target_pairs={{0,1},{1,0},{2,3},{3,2},{4,5},{5,4},{6,7},{7,6},{8,9},{9,8},{10,11... | collective-permute-start | bytes 221192 | tf_op jit(solution)/shard_map/ppermute | solution.py:387
  20.2 6.2 %collective-permute-start.6 = (bf16[96,1024]{1,0:T(8,128)(2,1)S(1)}, bf16[96,1024]{1,0:T(8,128)(2,1)S(1)}, u32[]{:S(2)}, u32[]{:S(2)}) collective-permute-start(bf16[96,1024]{1,0:T(8,128)(2,1)S(1)} %pad_maximum_fusion), channel_id=1, source_target_pairs={{0,1},{1,0},{2,3},{3,2},{4,5},{5,4},{6,7},{7,6},{8,9},{9,8},{10,11... | collective-permute-start | bytes 589832 | tf_op jit(solution)/shard_map/ppermute | solution.py:387
  26.4 2.7 %copy-start = (bf16[4,64,1024]{2,1,0:T(8,128)(2,1)S(1)}, bf16[4,64,1024]{2,1,0:T(8,128)(2,1)}, u32[]{:S(2)}) copy-start(bf16[4,64,1024]{2,1,0:T(8,128)(2,1)} %param.18) | copy-start | bytes 1572868
  26.4 2.7 %copy-start.1 = (bf16[4,64,1024]{2,1,0:T(8,128)(2,1)S(1)}, bf16[4,64,1024]{2,1,0:T(8,128)(2,1)}, u32[]{:S(2)}) copy-start(bf16[4,64,1024]{2,1,0:T(8,128)(2,1)} %param.19) | copy-start | bytes 1572868
  33.4 5.1 %collective-permute-start.10 = (bf16[32,1152]{1,0:T(8,128)(2,1)S(1)}, bf16[32,1152]{1,0:T(8,128)(2,1)S(1)}, u32[]{:S(2)}, u32[]{:S(2)}) collective-permute-start(bf16[32,1152]{1,0:T(8,128)(2,1)S(1)} %get-tuple-element.25), channel_id=1, source_target_pairs={{0,1},{1,0},{2,3},{3,2},{4,5},{5,4},{6,7},{7,6},{8,9},{9,8},{10,11... | collective-permute-start | bytes 221192 | tf_op jit(solution)/shard_map/ppermute | solution.py:387
  35.0 4.0 %copy-start.2 = (bf16[4,64,1024]{2,1,0:T(8,128)(2,1)S(1)}, bf16[4,64,1024]{2,1,0:T(8,128)(2,1)}, u32[]{:S(2)}) copy-start(bf16[4,64,1024]{2,1,0:T(8,128)(2,1)} %param.20) | copy-start | bytes 1572868
  37.5 5.0 %collective-permute-start.12 = (bf16[64,1024]{1,0:T(8,128)(2,1)S(1)}, bf16[64,1024]{1,0:T(8,128)(2,1)S(1)}, u32[]{:S(2)}, u32[]{:S(2)}) collective-permute-start(bf16[64,1024]{1,0:T(8,128)(2,1)S(1)} %shard_map.120), channel_id=1, source_target_pairs={{0,1},{1,0},{2,3},{3,2},{4,5},{5,4},{6,7},{7,6},{8,9},{9,8},{10,11... | collective-permute-start | bytes 393224 | tf_op jit(solution)/shard_map/ppermute | solution.py:387
  38.5 4.4 %collective-permute-start.11 = (bf16[32,1152]{1,0:T(8,128)(2,1)S(1)}, bf16[32,1152]{1,0:T(8,128)(2,1)S(1)}, u32[]{:S(2)}, u32[]{:S(2)}) collective-permute-start(bf16[32,1152]{1,0:T(8,128)(2,1)S(1)} %pad_maximum_fusion.3), channel_id=1, source_target_pairs={{0,2},{1,3},{2,0},{3,1},{4,6},{5,7},{6,4},{7,5},{8,10},{9,11},{10,... | collective-permute-start | bytes 221192 | tf_op jit(solution)/shard_map/ppermute | solution.py:387
  39.0 8.3 %collective-permute-start.9 = (bf16[256,1024]{1,0:T(8,128)(2,1)S(1)}, bf16[256,1024]{1,0:T(8,128)(2,1)S(1)}, u32[]{:S(2)}, u32[]{:S(2)}) collective-permute-start(bf16[256,1024]{1,0:T(8,128)(2,1)S(1)} %bitcast.9), channel_id=1, source_target_pairs={{0,8},{8,0},{1,9},{9,1},{2,10},{10,2},{3,11},{11,3},{4,12},{12,4},... | collective-permute-start | bytes 1572872 | tf_op jit(solution)/shard_map/ppermute | solution.py:392
  43.0 6.7 %collective-permute-start.13 = (bf16[32,1152]{1,0:T(8,128)(2,1)S(1)}, bf16[32,1152]{1,0:T(8,128)(2,1)S(1)}, u32[]{:S(2)}, u32[]{:S(2)}) collective-permute-start(bf16[32,1152]{1,0:T(8,128)(2,1)S(1)} %pad_maximum_fusion.4), channel_id=1, source_target_pairs={{0,4},{1,5},{2,6},{3,7},{4,0},{5,1},{6,2},{7,3},{8,12},{9,13},{10,... | collective-permute-start | bytes 221192 | tf_op jit(solution)/shard_map/ppermute | solution.py:387
  43.4 4.3 %collective-permute-start.14 = (bf16[32,1024]{1,0:T(8,128)(2,1)S(1)}, bf16[32,1024]{1,0:T(8,128)(2,1)S(1)}, u32[]{:S(2)}, u32[]{:S(2)}) collective-permute-start(bf16[32,1024]{1,0:T(8,128)(2,1)S(1)} %get-tuple-element.29), channel_id=1, source_target_pairs={{0,1},{1,0},{2,3},{3,2},{4,5},{5,4},{6,7},{7,6},{8,9},{9,8},{10,11... | collective-permute-start | bytes 196616 | tf_op jit(solution)/shard_map/ppermute | solution.py:387
  44.7 4.6 %collective-permute-start.15 = (bf16[32,1024]{1,0:T(8,128)(2,1)S(1)}, bf16[32,1024]{1,0:T(8,128)(2,1)S(1)}, u32[]{:S(2)}, u32[]{:S(2)}) collective-permute-start(bf16[32,1024]{1,0:T(8,128)(2,1)S(1)} %get-tuple-element.33), channel_id=1, source_target_pairs={{0,2},{1,3},{2,0},{3,1},{4,6},{5,7},{6,4},{7,5},{8,10},{9,11},{10,... | collective-permute-start | bytes 196616 | tf_op jit(solution)/shard_map/ppermute | solution.py:387

commit v4 on v3

--- a/solution.py
+++ b/solution.py
@@ -15,8 +15,7 @@
 HBM = pl.BlockSpec(memory_space=pltpu.HBM)
 LANES = 128
 PIECES = 4
-GRANT = 24 << 20
-SOON = 2
+GRANT = 12 << 20
 BAND = 32
 
 
@@ -72,17 +71,18 @@
     return copies
 
 
-def low_kernel(count, x_hbm, picks_ref, *rest):
+def low_kernel(count, hints, x_hbm, picks_ref, *rest):
+    rest = rest[hints:]
     downs, (out_ref, x_ref), bufs, sems = rest[:count], rest[count : count + 2], rest[count + 2 : -1], rest[-1]
     for c in load_all([(x_hbm, x_ref)] + list(zip(downs, bufs)), sems):
         c.wait()
     out_ref[...] = low_of(x_ref[...], bufs, picks_ref[...])
 
 
-def low_call(x, picks, downs):
+def low_call(x, picks, downs, hints):
     return pl.pallas_call(
-        functools.partial(low_kernel, len(downs)),
-        in_specs=[HBM, VMEM] + [HBM] * len(downs),
+        functools.partial(low_kernel, len(downs), len(hints)),
+        in_specs=[HBM, VMEM] + [HBM] * (len(hints) + len(downs)),
         out_specs=[VMEM] * 2,
         out_shape=[
             jax.ShapeDtypeStruct((x.shape[0], LANES), jnp.float32),
@@ -92,155 +92,75 @@
         + [pltpu.SemaphoreType.DMA((1 + len(downs),))],
         name="low",
         **params((10**8, 10**6)),
-    )(in_hbm(x), picks, in_hbm(downs[0]), *downs[1:])
-
-
-def weight_copies(weight, buf, sems, j, block, along):
-    depth, wide = buf.shape[1], buf.shape[2]
-    piece = depth // PIECES
+    )(in_hbm(x), picks, *[in_hbm(h) for h in hints], in_hbm(downs[0]), *downs[1:])
+
+
+def lead_kernel(tensor_ref, chunk, weight, out_ref, buf, sems):
+    width = buf.shape[0]
+    piece = width // PIECES
     copies = []
     for p in range(PIECES):
-        if along == 0:
-            src = weight.at[pl.ds(pl.multiple_of(block * depth + p * piece, piece), piece), :]
-        else:
-            src = weight.at[p * piece : (p + 1) * piece, pl.ds(pl.multiple_of(block * wide, LANES), wide)]
-        copies.append(
-            pltpu.make_async_copy(src, buf.at[j, p * piece : (p + 1) * piece, :], sems.at[j, p])
-        )
-    return copies
-
-
-def block_dot(x_ref_read, buf, j, copies, total):
-    piece = buf.shape[1] // PIECES
-    for p in range(PIECES):
-        copies[p].wait()
-        total = total + dot(
-            x_ref_read(p * piece, piece), buf[j, p * piece : (p + 1) * piece, :]
-        )
-    return total
-
-
-def project_kernel(ks, held_count, spans, given, tensor_ref, *rest):
+        at = pl.multiple_of(tensor_ref[0] * width + p * piece, piece)
+        spot = pl.ds(p * piece, piece)
+        copies.append(pltpu.make_async_copy(weight.at[pl.ds(at, piece), :], buf.at[spot, :], sems.at[p]))
+    for c in copies:
+        c.start()
+    total = 0.0
+    for p, c in enumerate(copies):
+        c.wait()
+        span = slice(p * piece, (p + 1) * piece)
+        total = total + dot(chunk[:, span], buf[span, :])
+    out_ref[...] = total
+
+
+def lead_call(chunk, tensor_at, weight):
+    rows, width = chunk.shape
+    wide = weight.shape[1]
+    return pl.pallas_call(
+        lead_kernel,
+        in_specs=[SMEM, VMEM, HBM],
+        out_specs=VMEM,
+        out_shape=jax.ShapeDtypeStruct((rows, wide), jnp.float32),
+        scratch_shapes=[
+            pltpu.VMEM((width, wide), weight.dtype),
+            pltpu.SemaphoreType.DMA((PIECES,)),
+        ],
+        name="lead",
+        **params((2 * rows * width * wide, 2 * width * wide)),
+    )(tensor_at, chunk, in_hbm(weight))
+
+
+def dense_kernel(shards, ks, spans, given, first, tensor_ref, weight, *rest):
     arrays, rest = rest[:given], rest[given:]
-    weight, before, rest = rest[0], rest[1], rest[2:]
-    if held_count:
-        held, rest = rest[0], rest[1:]
-    out_ref, buf, sems = rest
-    rows = out_ref.shape[0]
-    width = buf.shape[1]
-    later = ks[held_count:]
-    copies = [weight_copies(weight, buf, sems, j, tensor_ref[0] ^ k, 0) for j, k in enumerate(later)]
-    for c in sum(copies, []):
-        c.start()
-    total = before[...]
-    for j, (i, r) in enumerate(spans):
-        if j < held_count:
-            total = total + dot(arrays[i][r : r + rows, :width], held[j])
-        else:
-            total = block_dot(
-                lambda a, n, i=i, r=r: arrays[i][r : r + rows, a : a + n],
-                buf,
-                j - held_count,
-                copies[j - held_count],
-                total,
-            )
+    out_ref = rest[-1]
+    rows, width = out_ref.shape[0], weight.shape[0] // shards
+    total = 0.0 if first else rest[0][...]
+    for k, (i, r) in zip(ks, spans):
+        at = pl.multiple_of((tensor_ref[0] ^ k) * width, width)
+        total = total + dot(arrays[i][r : r + rows, :width], weight[pl.ds(at, width), :])
     out_ref[...] = total
 
 
-def project_call(where, ks, tensor_at, weight, before, width, held=None):
-    rows, wide = before.shape
+def dense_call(shards, where, ks, tensor_at, weight, before, rows, hints):
+    wide = weight.shape[1]
     arrays, spans = [], []
     for k in ks:
         array, r = where[k]
         if not any(a is array for a in arrays):
             arrays.append(array)
         spans.append(([a is array for a in arrays].index(True), r))
-    extra = [] if held is None else [held]
-    held_count = 0 if held is None else held.shape[0]
-    count = len(ks) - held_count
+    extra = [] if before is None else [before]
     return pl.pallas_call(
-        functools.partial(project_kernel, ks, held_count, spans, len(arrays)),
-        in_specs=[SMEM] + [VMEM] * len(arrays) + [HBM] + [VMEM] * (1 + len(extra)),
+        functools.partial(dense_kernel, shards, ks, spans, len(arrays), before is None),
+        in_specs=[SMEM, VMEM] + [VMEM] * (len(arrays) + len(extra)) + [HBM] * len(hints),
         out_specs=VMEM,
         out_shape=jax.ShapeDtypeStruct((rows, wide), jnp.float32),
-        scratch_shapes=[
-            pltpu.VMEM((count, width, wide), weight.dtype),
-            pltpu.SemaphoreType.DMA((count, PIECES)),
-        ],
-        **params((2 * len(ks) * rows * width * wide, 2 * count * width * wide)),
-    )(tensor_at, *arrays, in_hbm(weight), before, *extra)
-
-
-def lead_kernel(k, ahead, tensor_ref, chunk, weight, out_ref, ahead_ref, buf, sems, ahead_sems):
-    copies = weight_copies(weight, buf, sems, 0, tensor_ref[0] ^ k, 0)
-    later = [
-        weight_copies(weight, ahead_ref, ahead_sems, j, tensor_ref[0] ^ a, 0)
-        for j, a in enumerate(ahead)
-    ]
-    for c in copies + sum(later, []):
-        c.start()
-    out_ref[...] = block_dot(lambda a, n: chunk[:, a : a + n], buf, 0, copies, 0.0)
-    for c in sum(later, []):
-        c.wait()
-
-
-def lead_call(chunk, k, ahead, tensor_at, weight):
-    rows, width = chunk.shape
-    wide = weight.shape[1]
-    return pl.pallas_call(
-        functools.partial(lead_kernel, k, ahead),
-        in_specs=[SMEM, VMEM, HBM],
-        out_specs=[VMEM] * 2,
-        out_shape=[
-            jax.ShapeDtypeStruct((rows, wide), jnp.float32),
-            jax.ShapeDtypeStruct((len(ahead), width, wide), weight.dtype),
-        ],
-        scratch_shapes=[
-            pltpu.VMEM((1, width, wide), weight.dtype),
-            pltpu.SemaphoreType.DMA((1, PIECES)),
-            pltpu.SemaphoreType.DMA((len(ahead), PIECES)),
-        ],
-        name="lead",
-        **params((2 * rows * width * wide, 2 * (1 + len(ahead)) * width * wide)),
-    )(tensor_at, chunk, in_hbm(weight))
-
-
-def held_kernel(count, ahead, tensor_ref, *refs):
-    chunks, refs = refs[:count], refs[count:]
-    held, before, weight, out_ref, ahead_ref, ahead_sems = refs
-    later = [
-        weight_copies(weight, ahead_ref, ahead_sems, j, tensor_ref[0] ^ a, 0)
-        for j, a in enumerate(ahead)
-    ]
-    for c in sum(later, []):
-        c.start()
-    rows, width = out_ref.shape[0], held.shape[1]
-    total = before[...]
-    for j in range(count):
-        total = total + dot(chunks[j][:rows, :width], held[j])
-    out_ref[...] = total
-    for c in sum(later, []):
-        c.wait()
-
-
-def held_call(chunks, held, before, ahead, tensor_at, weight):
-    _, width, wide = held.shape
-    return pl.pallas_call(
-        functools.partial(held_kernel, len(chunks), ahead),
-        in_specs=[SMEM] + [VMEM] * (len(chunks) + 2) + [HBM],
-        out_specs=[VMEM] * 2,
-        out_shape=[
-            jax.ShapeDtypeStruct(before.shape, before.dtype),
-            jax.ShapeDtypeStruct((len(ahead), width, wide), weight.dtype),
-        ],
-        scratch_shapes=[pltpu.SemaphoreType.DMA((len(ahead), PIECES))],
-        name="held",
-        **params((2 * before.size * width * len(chunks), 2 * len(ahead) * width * wide), 8 << 20),
-    )(tensor_at, *chunks, held, before, in_hbm(weight))
+        **params((2 * len(ks) * rows * weight.size // shards, 10**6), 6 << 20),
+    )(tensor_at, weight, *arrays, *extra, *[in_hbm(h) for h in hints])
 
 
 def mix_kernel(sizes, *refs):
-    k_in, k_outs, maps, kv_count, group, head, local_heads, group_all, _ = sizes
+    k_in, k_outs, maps, kv_count, group, head, local_heads, group_all, width = sizes
     refs = list(refs)
     tensor_ref, chunk, w_in, w_out, before, low, picks = [refs.pop(0) for _ in range(7)]
     ups = [refs.pop(0) for _ in range(maps)]
@@ -248,29 +168,21 @@
     keys, values, live = [refs.pop(0) for _ in range(3)]
     low_out, mixed_out, block_out = [refs.pop(0) for _ in range(3)]
     more_outs = [refs.pop(0) for _ in k_outs[1:]]
-    buf_in, sem_in, buf_out, sem_out, k_buf, v_buf, up_buf, down_buf, sems = refs
+    k_buf, v_buf, up_buf, down_buf, sems = refs
 
     tensor_at = tensor_ref[0]
-    copies_in = weight_copies(w_in, buf_in, sem_in, 0, tensor_at ^ k_in, 0)
-    copies_out = [
-        weight_copies(w_out, buf_out, sem_out, j, tensor_at ^ k, 1) for j, k in enumerate(k_outs)
-    ]
     kv = pl.ds(tensor_at * local_heads // group_all, kv_count)
     up_copies = load_all([(u, up_buf.at[i]) for i, u in enumerate(ups)], sems.at[0])
-    for c in copies_in:
-        c.start()
     kv_copies = load_all([(keys.at[:, kv], k_buf), (values.at[:, kv], v_buf)], sems.at[1])
     down_copies = load_all([(d, down_buf.at[i]) for i, d in enumerate(downs)], sems.at[2])
-    for pieces in copies_out:
-        for c in pieces:
-            c.start()
 
     rows = before.shape[0]
     picked = picks[...]
     for c in up_copies:
         c.wait()
     total = before[...] + 0.5 * lora_of(low[...], [up_buf.at[i] for i in range(maps)], picked)
-    total = block_dot(lambda a, n: chunk[:, a : a + n], buf_in, 0, copies_in, total)
+    at = pl.multiple_of((tensor_at ^ k_in) * width, width)
+    total = total + dot(chunk[:, :width], w_in[pl.ds(at, width), :])
     for c in kv_copies:
         c.wait()
     length = k_buf.shape[2]
@@ -297,43 +209,39 @@
         c.wait()
     low_part = low_of(mixed, [down_buf.at[i] for i in range(maps)], picked)
     low_out[...] = low_part
-    block = block_dot(lambda a, n: mixed[:, a : a + n], buf_out, 0, copies_out[0], 0.0)
-    wide = block.shape[1]
-    block_out[:, :wide] = block.astype(block_out.dtype)
+    wide = block_out.shape[1] - LANES
     block_out[:, wide:] = low_part.astype(block_out.dtype)
-    for j, ref in enumerate(more_outs):
-        ref[...] = block_dot(
-            lambda a, n: mixed[:, a : a + n], buf_out, j + 1, copies_out[j + 1], 0.0
-        )
-
-
-def out_kernel(ks, spans, tensor_ref, x_ref, weight, *rest):
-    outs, (buf, sems) = rest[:-2], rest[-2:]
+    for j, k in enumerate(k_outs):
+        at = pl.multiple_of((tensor_at ^ k) * wide, LANES)
+        block = dot(mixed, w_out[:, pl.ds(at, wide)])
+        if j == 0:
+            block_out[:, :wide] = block.astype(block_out.dtype)
+        else:
+            more_outs[j - 1][...] = block
+
+
+def resident_kernel(ks, spans, tensor_ref, x_ref, weight, *outs):
     rows = x_ref.shape[0]
-    copies = [weight_copies(weight, buf, sems, j, tensor_ref[0] ^ k, 1) for j, k in enumerate(ks)]
-    for pieces in copies:
-        for c in pieces:
-            c.start()
-    for j, (i, r) in enumerate(spans):
-        block = block_dot(lambda a, n: x_ref[:, a : a + n], buf, j, copies[j], 0.0)
+    wide = outs[0].shape[1]
+    for k, (i, r) in zip(ks, spans):
+        at = pl.multiple_of((tensor_ref[0] ^ k) * wide, LANES)
+        block = dot(x_ref[...], weight[:, pl.ds(at, wide)])
         outs[i][r : r + rows, :] = block.astype(outs[i].dtype)
 
 
-def out_call(groups, tensor_at, mixed, weight, out_width):
-    rows, depth = mixed.shape
+def resident_call(groups, tensor_at, mixed, weight, out_width):
+    rows, _ = mixed.shape
     ks = [k for group, _ in groups for k in group]
     spans = [(i, r * rows) for i, (group, _) in enumerate(groups) for r in range(len(group))]
     return pl.pallas_call(
-        functools.partial(out_kernel, ks, spans),
-        in_specs=[SMEM, VMEM, HBM],
+        functools.partial(resident_kernel, ks, spans),
+        in_specs=[SMEM, VMEM, VMEM],
         out_specs=[VMEM] * len(groups),
-        out_shape=[jax.ShapeDtypeStruct((rows * len(group), out_width), kind) for group, kind in groups],
-        scratch_shapes=[
-            pltpu.VMEM((len(ks), depth, out_width), weight.dtype),
-            pltpu.SemaphoreType.DMA((len(ks), PIECES)),
+        out_shape=[
+            jax.ShapeDtypeStruct((rows * len(group), out_width), kind) for group, kind in groups
         ],
-        **params((2 * len(ks) * rows * depth * out_width, 2 * len(ks) * depth * out_width)),
-    )(tensor_at, mixed, in_hbm(weight))
+        compiler_params=pltpu.CompilerParams(vmem_limit_bytes=6 << 20),
+    )(tensor_at, mixed, weight)
 
 
 def final_kernel(wide, count, maps, picks_ref, low_ref, *rest):
@@ -414,7 +322,7 @@
     output_down = with_swapped(output_down_maps)
     output_up = with_swapped(output_up_maps)
 
-    low, near = low_call(hidden, picks, query_down)
+    low, near = low_call(hidden, picks, query_down, [])
     where = {0: (near, 0)}
     chain = 0
     for bit in reversed(bits):
@@ -441,10 +349,9 @@
     last = chain
     ahead = [k for k in where if k and not k & 1 and k != last ^ 1]
     second = [last ^ 1] + [k for k in where if k & 1 and k != last]
-    query, held = lead_call(near, 0, ahead, tensor_at, w_query)
-    chunks = [where[k][0] for k in ahead]
-    query, held = held_call(chunks, held, query, second[:SOON], tensor_at, w_query)
-    query = project_call(where, second, tensor_at, w_query, query, width, held)
+    query = lead_call(near, tensor_at, w_query)
+    for ks, hints in ((ahead, [output_weight]), (second, [])):
+        query = dense_call(shards, where, ks, tensor_at, w_query, query, rows, hints)
 
     wide = w_query.shape[1]
     local_heads = wide // head
@@ -460,7 +367,7 @@
     map_in, map_out = (stored * rank, wide), (stored * rank, depth)
     low2, mixed, payload, *blocks = pl.pallas_call(
         functools.partial(mix_kernel, sizes),
-        in_specs=[SMEM, VMEM, HBM, HBM, VMEM, VMEM, VMEM] + [HBM] * (2 * replicas) + [HBM, HBM, VMEM],
+        in_specs=[SMEM, VMEM, VMEM, VMEM, VMEM, VMEM, VMEM] + [HBM] * (2 * replicas) + [HBM, HBM, VMEM],
         out_specs=[VMEM] * (2 + len(k_outs)),
         out_shape=[
             jax.ShapeDtypeStruct((rows, LANES), jnp.float32),
@@ -469,10 +376,6 @@
         ]
         + [jax.ShapeDtypeStruct((rows, out_width), jnp.float32)] * (len(k_outs) - 1),
         scratch_shapes=[
-            pltpu.VMEM((1, width, wide), w_query.dtype),
-            pltpu.SemaphoreType.DMA((1, PIECES)),
-            pltpu.VMEM((len(k_outs), depth, out_width), output_weight.dtype),
-            pltpu.SemaphoreType.DMA((len(k_outs), PIECES)),
             pltpu.VMEM((rows, kv_count, length, head), keys.dtype),
             pltpu.VMEM((rows, kv_count, length, head), values.dtype),
             pltpu.VMEM((replicas,) + map_in, keys.dtype),
@@ -484,8 +387,8 @@
     )(
         tensor_at,
         where[last][0],
-        in_hbm(w_query),
-        in_hbm(output_weight),
+        w_query,
+        output_weight,
         query,
         low,
         picks,
@@ -506,12 +409,11 @@
     even = [k for k in even if k not in parts]
     plan = [
         [(odd, bf16)] * bool(odd),
-        [([k], f32) for k in even[:-1]] + [([1], bf16)] * (whole > 1),
-        [([k], f32) for k in even[-1:]],
+        [([k], f32) for k in even[:-1]] + [([1], bf16)] * (whole > 1) + [([k], f32) for k in even[-1:]],
     ]
     plan = [groups for groups in plan if groups]
     for groups in plan:
-        arrays = out_call(groups, tensor_at, mixed, output_weight, out_width)
+        arrays = resident_call(groups, tensor_at, mixed, output_weight, out_width)
         for (g, kind), array in zip(groups, arrays):
             if kind == bf16:
                 got = across(array, 1)

time: 50.9 us -> 52 us (1.022)
  Pallas kernels: 22.3 us -> 14.5 us
  waiting for transfers between devices: 11.9 us -> 15.9 us
  other arithmetic: 1.75 us -> 4.76 us
  local copies, waits for them, and re-layouts: 0.1 us -> 1.72 us
    pallas_call x7 -> x6, Pallas kernels: 17.1 us -> 10.5 us  [the longest x2 4.89 us: dense_call(): pl.pallas_call(functools.partial(dense_kernel, shards, ks, spans, len(arr...]
    ppermute x12, waiting for transfers between devices: 11.3 us -> 15.3 us  [across(): return lax.ppermute(x, 'tensor', [(i, i ^ bit) for i in range(shards)])]
    slice x1, local copies, waits for them, and re-layouts: 0.01 us -> 1.59 us  [per_device(): where[chain][0][:, :width]]
    add x1, other arithmetic: 0.01 us -> 1.47 us  [per_device(): low = low + got[:, width:].astype(jnp.float32)]
    pallas_call x1, Pallas kernels: 4.29 us -> 3.08 us  [per_device(): pl.pallas_call(functools.partial(mix_kernel, sizes), in_specs=[SMEM, VMEM...]
    concatenate x1, other arithmetic: 0.01 us -> 0.85 us  [per_device(): got = jnp.concatenate([where[k][0][:, :width] for k in rest], axis=0)]
    convert_element_type x2, other arithmetic: 0.01 us -> 0.71 us  [per_device(): low.astype(jnp.bfloat16)]
  transfers between devices with their start and end apart: 16 -> 16, of which waited for: 9 -> 8; matrix products, arithmetic and copies ran while one was open for 4% -> 12% of each run, Pallas kernels for 34% -> 20%
where the time goes in v4:
time: 52 us; the launch traced here: 51.7 us
  waiting for transfers between devices  15.9 us (31%)
  starting transfers between devices  14.5 us (28%)
  Pallas kernels  14.5 us (28%)
  other arithmetic  4.76 us (9%)
  local copies, waits for them, and re-layouts  1.72 us (3%)
    ppermute x12, waiting for transfers between devices, across(): return lax.ppermute(x, 'tensor', [(i, i ^ bit) for i in range(shards)])  15.3 us
    ppermute x12, starting transfers between devices, across(): return lax.ppermute(x, 'tensor', [(i, i ^ bit) for i in range(shards)])  14 us
    pallas_call x2, Pallas kernels, dense_call(): pl.pallas_call(functools.partial(dense_kernel, shards, ks, spans, len(arr...  4.89 us
    pallas_call x1, Pallas kernels, per_device(): pl.pallas_call(functools.partial(mix_kernel, sizes), in_specs=[SMEM, VMEM...  3.08 us
    pallas_call x2, Pallas kernels, resident_call(): pl.pallas_call(functools.partial(resident_kernel, ks, spans), in_specs=[S...  2.37 us
    pallas_call x1, Pallas kernels, lead_call(): pl.pallas_call(lead_kernel, in_specs=[SMEM, VMEM, HBM], out_specs=VMEM, o...  1.75 us
    slice x1, local copies, waits for them, and re-layouts, per_device(): where[chain][0][:, :width]  1.59 us
    pallas_call x1, Pallas kernels, low_call(): pl.pallas_call(functools.partial(low_kernel, len(downs), len(hints)), in_...  1.53 us
  transfers between devices with their start and end apart: 16, of which 8 were waited for; matrix products, arithmetic and copies ran while one was open for 12% of the time, Pallas kernels for 20%

profile of v4, /device:TPU:0, one launch (start us, length us, event | category | flops | bytes accessed | tf_op | source)
XLA Modules:
  0.0 51.7 jit_solution(14467385723825402179)
XLA Ops:
  0.0 4.1 %collective-permute-start = (bf16[32,1024]{1,0:T(8,128)(2,1)}, bf16[32,1024]{1,0:T(8,128)(2,1)S(1)}, u32[]{:S(2)}, u32[]{:S(2)}) collective-permute-start(bf16[32,1024]{1,0:T(8,128)(2,1)} %x_hbm.1), channel_id=1, source_target_pairs={{0,4},{1,5},{2,6},{3,7},{4,0},{5,1},{6,2},{7,3},{8,12},{9,13},{10,... | collective-permute-start | bytes 196616 | tf_op jit(solution)/shard_map/ppermute | solution.py:295
  4.1 1.6 %collective-permute-start.5 = (bf16[32,1024]{1,0:T(8,128)(2,1)}, bf16[32,1024]{1,0:T(8,128)(2,1)}, u32[]{:S(2)}, u32[]{:S(2)}) collective-permute-start(bf16[32,1024]{1,0:T(8,128)(2,1)} %x_hbm.1), channel_id=1, source_target_pairs={{0,2},{1,3},{2,0},{3,1},{4,6},{5,7},{6,4},{7,5},{8,10},{9,11},{10,... | collective-permute-start | bytes 196616 | tf_op jit(solution)/shard_map/ppermute | solution.py:295
  5.6 0.0 collective-permute-start.1
  5.6 0.5 collective-permute-start.7
  6.2 0.0 collective-permute-start.8
  6.2 0.8 %select_reduce_fusion = s32[64]{0:T(128)S(1)} fusion(s32[8]{0:T(128)} %param.22, s32[64]{0:T(128)} %param.21), kind=kLoop, calls=%fused_computation.30 | loop fusion | flops 1472 | bytes 544 | tf_op jit(solution)/shard_map/reduce_sum | solution.py:305
  7.0 0.1 dynamic_slice.3
  7.0 0.1 broadcast_compare_fusion.1
  7.1 0.6 %collective-permute-done.1.rest_1_ = bf16[256,1024]{1,0:T(8,128)(2,1)S(1)} collective-permute-done((bf16[256,1024]{1,0:T(8,128)(2,1)}, bf16[256,1024]{1,0:T(8,128)(2,1)S(1)}, u32[]{:S(2)}, u32[]{:S(2)}) %collective-permute-start.1) | collective-permute-done | bytes 524320 | tf_op jit(solution)/shard_map/ppermute | solution.py:300
  7.8 1.5 %low.1 = (f32[32,128]{1,0:T(8,128)S(1)}, bf16[32,1024]{1,0:T(8,128)(2,1)S(1)}) custom-call(bf16[32,1024]{1,0:T(8,128)(2,1)} %x_hbm.1, f32[32,512]{1,0:T(8,128)S(1)} %add_convert_fusion.3.picks_ref.refs_6_, bf16[256,1024]{1,0:T(8,128)(2,1)} %bitcast.14, bf16[256,1024]{1,0:T(8,128)(2,1)S(1)} %collective-permute-done.1.rest_1_), custom_call_target="tpu_custom_call" | custom-call | flops 100000000 | bytes 1000000 | tf_op jit(solution)/shard_map/low/pallas_call | solution.py:83
  9.3 0.4 collective-permute-start.2
  9.7 4.4 %collective-permute-done.2 = f32[32,128]{1,0:T(8,128)S(1)} collective-permute-done((f32[32,128]{1,0:T(8,128)S(1)}, f32[32,128]{1,0:T(8,128)S(1)}, u32[]{:S(2)}, u32[]{:S(2)}) %collective-permute-start.2) | collective-permute-done | bytes 16416 | tf_op jit(solution)/shard_map/ppermute | solution.py:295
  14.1 0.0 collective-permute-done.rest_0_
  14.1 0.5 collective-permute-start.3
  14.6 0.7 %fusion.1.refs_13_ = f32[32,1024]{1,0:T(8,128)S(1)} fusion(s32[32]{0:T(128)} %param.23, s32[1024]{0:T(1024)S(1)} %get-tuple-element.34, s32[1024]{0:T(1024)S(1)} %get-tuple-element.35, s32[32]{0:T(128)S(1)} %get-tuple-element.39, s32[32]{0:T(128)S(1)} %get-tuple-element.40, s32[1024]{0:T(1024)S(1)} %get-tuple-element.33, s32[1024]{0:T(1024)S(1)} %get-tuple-element.36, ...), kind=kLoop, calls=%fused_computation.7 | loop fusion | flops 229376 | bytes 149920 | tf_op jit(solution)/shard_map/convert_element_type | solution.py:318
  15.3 0.0 copy-start
  15.3 3.3 %collective-permute-done.3.rest_0_ = bf16[32,1152]{1,0:T(8,128)(2,1)} collective-permute-done((bf16[32,1152]{1,0:T(8,128)(2,1)S(1)}, bf16[32,1152]{1,0:T(8,128)(2,1)}, u32[]{:S(2)}, u32[]{:S(2)}) %collective-permute-start.3) | collective-permute-done | bytes 73760 | tf_op jit(solution)/shard_map/ppermute | solution.py:295
  18.6 1.6 %slice.37 = bf16[32,1024]{1,0:T(8,128)(2,1)S(1)} slice(bf16[32,1152]{1,0:T(8,128)(2,1)} %collective-permute-done.3.rest_0_), slice={[0:32], [0:1024]} | slice | bytes 131072 | tf_op jit(solution)/shard_map/slice | solution.py:334
  20.2 0.7 %fusion.2 = bf16[32,128]{1,0:T(8,128)(2,1)S(1)} fusion(f32[32,128]{1,0:T(8,128)S(1)} %get-tuple-element.26, bf16[32,1152]{1,0:T(8,128)(2,1)} %collective-permute-done.3.rest_0_), kind=kLoop, calls=%fused_computation.19 | loop fusion | flops 12288 | bytes 32768 | tf_op jit(solution)/shard_map/convert_element_type | solution.py:334
  20.9 1.6 %collective-permute-start.4 = (bf16[32,1152]{1,0:T(8,128)(2,1)S(1)}, bf16[32,1152]{1,0:T(8,128)(2,1)S(1)}, u32[]{:S(2)}, u32[]{:S(2)}) collective-permute-start(bf16[32,1152]{1,0:T(8,128)(2,1)S(1)} %pad_maximum_fusion.2), channel_id=1, source_target_pairs={{0,1},{1,0},{2,3},{3,2},{4,5},{5,4},{6,7},{7,6},{8,9},{9,8},{10,11... | collective-permute-start | bytes 221192 | tf_op jit(solution)/shard_map/ppermute | solution.py:295
  22.5 0.0 collective-permute-done.5.rest_1_
  22.5 0.9 %pad_maximum_fusion = bf16[96,1024]{1,0:T(8,128)(2,1)S(1)} fusion(bf16[32,1024]{1,0:T(8,128)(2,1)} %collective-permute-done.5.rest_1_, bf16[32,1024]{1,0:T(8,128)(2,1)S(1)} %collective-permute-done.rest_0_, bf16[32,1024]{1,0:T(8,128)(2,1)S(1)} %get-tuple-element.16.chunk), kind=kLoop, calls=%fused_computation | loop fusion | flops 589824 | bytes 393216 | tf_op jit(solution)/shard_map/concatenate | solution.py:339
  23.4 0.6 %collective-permute-start.6 = (bf16[96,1024]{1,0:T(8,128)(2,1)S(1)}, bf16[96,1024]{1,0:T(8,128)(2,1)S(1)}, u32[]{:S(2)}, u32[]{:S(2)}) collective-permute-start(bf16[96,1024]{1,0:T(8,128)(2,1)S(1)} %pad_maximum_fusion), channel_id=1, source_target_pairs={{0,1},{1,0},{2,3},{3,2},{4,5},{5,4},{6,7},{7,6},{8,9},{9,8},{10,11... | collective-permute-start | bytes 589832 | tf_op jit(solution)/shard_map/ppermute | solution.py:295
  23.9 1.7 %lead.1.rest_2_ = f32[32,1024]{1,0:T(8,128)S(1)} custom-call(s32[1]{0:T(128)} %bitcast.tensor_ref.refs_0_, bf16[32,1024]{1,0:T(8,128)(2,1)S(1)} %get-tuple-element.16.chunk, bf16[8192,1024]{1,0:T(8,128)(2,1)} %refs_2_.1), custom_call_target="tpu_custom_call" | custom-call | flops 67108864 | bytes 2097152 | tf_op jit(solution)/shard_map/lead/pallas_call | solution.py:119
  25.7 0.0 copy-done
  25.7 0.0 slice-start
  25.7 0.0 slice-start.1
  25.7 0.0 slice-start.2
  25.7 1.8 %shard_map.118.rest_2_ = f32[32,1024]{1,0:T(8,128)S(1)} custom-call(s32[1]{0:T(128)} %bitcast.tensor_ref.refs_0_, bf16[8192,1024]{1,0:T(8,128)(2,1)S(1)} %copy-done, bf16[32,1024]{1,0:T(8,128)(2,1)S(1)} %collective-permute-done.rest_0_, bf16[32,1024]{1,0:T(8,128)(2,1)} %collective-permute-done.5.rest_1_, f32[32,1024]{1,0:T(8,128)S(1)} %lead.1.rest_2_, ...), custom_call_target="tpu_custom_call" | custom-call | flops 134217728 | bytes 1000000 | tf_op jit(solution)/shard_map/pallas_call | solution.py:153
  27.6 0.0 copy-start.1
  27.6 0.0 copy-start.2
  27.6 0.0 collective-permute-done.4.refs_1_
  27.6 1.5 %convert_add_fusion.1.refs_5_ = f32[32,128]{1,0:T(8,128)S(1)} fusion(f32[32,128]{1,0:T(8,128)S(1)} %get-tuple-element.26, bf16[32,1152]{1,0:T(8,128)(2,1)S(1)} %collective-permute-done.4.refs_1_, bf16[32,1152]{1,0:T(8,128)(2,1)} %collective-permute-done.3.rest_0_), kind=kLoop, calls=%fused_computation.15 | loop fusion | flops 16384 | bytes 49152 | tf_op jit(solution)/shard_map/add | solution.py:337
  29.1 0.0 slice-start.3
  29.1 0.0 collective-permute-done.6.rest_1_
  29.1 3.1 %shard_map.119.refs_4_ = f32[32,1024]{1,0:T(8,128)S(1)} custom-call(s32[1]{0:T(128)} %bitcast.tensor_ref.refs_0_, bf16[8192,1024]{1,0:T(8,128)(2,1)S(1)} %copy-done, bf16[32,1152]{1,0:T(8,128)(2,1)} %collective-permute-done.3.rest_0_, bf16[96,1024]{1,0:T(8,128)(2,1)S(1)} %collective-permute-done.6.rest_1_, f32[32,1024]{1,0:T(8,128)S(1)} %shard_map.118.rest_2_), custom_call_target="tpu_custom_call" | custom-call | flops 268435456 | bytes 1000000 | tf_op jit(solution)/shard_map/pallas_call | solution.py:153
  32.2 0.0 collective-permute-done.7.refs_8_
  32.2 0.0 collective-permute-done.8.refs_10_
  32.2 0.0 slice-done
  32.2 0.0 slice-done.1
  32.2 0.0 slice-done.2
  32.2 0.0 copy-done.1
  32.3 0.0 copy-done.2
  32.3 0.0 slice-done.3
  32.3 3.1 %mix.1 = (f32[32,128]{1,0:T(8,128)S(1)}, bf16[32,1024]{1,0:T(8,128)(2,1)S(1)}, bf16[32,1152]{1,0:T(8,128)(2,1)S(1)}, f32[32,1024]{1,0:T(8,128)S(1)}) custom-call(s32[1]{0:T(128)} %bitcast.tensor_ref.refs_0_, bf16[32,1152]{1,0:T(8,128)(2,1)S(1)} %collective-permute-done.4.refs_1_, bf16[8192,1024]{1,0:T(8,128)(2,1)S(1)} %copy-done, ...), custom_call_target="tpu_custom_call" | custom-call | flops 1000000000 | bytes 6291456 | tf_op jit(solution)/shard_map/mix/pallas_call | solution.py:368
  35.4 0.0 copy-start.3
  35.4 1.5 %collective-permute-start.10 = (bf16[32,1152]{1,0:T(8,128)(2,1)S(1)}, bf16[32,1152]{1,0:T(8,128)(2,1)S(1)}, u32[]{:S(2)}, u32[]{:S(2)}) collective-permute-start(bf16[32,1152]{1,0:T(8,128)(2,1)S(1)} %get-tuple-element.18), channel_id=1, source_target_pairs={{0,1},{1,0},{2,3},{3,2},{4,5},{5,4},{6,7},{7,6},{8,9},{9,8},{10,11... | collective-permute-start | bytes 221192 | tf_op jit(solution)/shard_map/ppermute | solution.py:295
  36.9 0.8 %shard_map.121 = bf16[64,1024]{1,0:T(8,128)(2,1)S(1)} custom-call(s32[1]{0:T(128)} %bitcast.tensor_ref.refs_0_, bf16[32,1024]{1,0:T(8,128)(2,1)S(1)} %get-tuple-element.20.x_ref, bf16[1024,8192]{1,0:T(8,128)(2,1)S(1)} %bitcast.6), custom_call_target="tpu_custom_call" | custom-call | tf_op jit(solution)/shard_map/pallas_call | solution.py:236
  37.8 0.6 %collective-permute-start.12 = (bf16[64,1024]{1,0:T(8,128)(2,1)S(1)}, bf16[64,1024]{1,0:T(8,128)(2,1)S(1)}, u32[]{:S(2)}, u32[]{:S(2)}) collective-permute-start(bf16[64,1024]{1,0:T(8,128)(2,1)S(1)} %shard_map.121), channel_id=1, source_target_pairs={{0,1},{1,0},{2,3},{3,2},{4,5},{5,4},{6,7},{7,6},{8,9},{9,8},{10,11... | collective-permute-start | bytes 393224 | tf_op jit(solution)/shard_map/ppermute | solution.py:295
  38.3 1.6 %collective-permute-done.10.rest_2_ = bf16[32,1152]{1,0:T(8,128)(2,1)S(1)} collective-permute-done((bf16[32,1152]{1,0:T(8,128)(2,1)S(1)}, bf16[32,1152]{1,0:T(8,128)(2,1)S(1)}, u32[]{:S(2)}, u32[]{:S(2)}) %collective-permute-start.10) | collective-permute-done | bytes 73760 | tf_op jit(solution)/shard_map/ppermute | solution.py:295
  39.9 0.7 %collective-permute-start.11 = (bf16[32,1152]{1,0:T(8,128)(2,1)S(1)}, bf16[32,1152]{1,0:T(8,128)(2,1)S(1)}, u32[]{:S(2)}, u32[]{:S(2)}) collective-permute-start(bf16[32,1152]{1,0:T(8,128)(2,1)S(1)} %pad_maximum_fusion.3), channel_id=1, source_target_pairs={{0,2},{1,3},{2,0},{3,1},{4,6},{5,7},{6,4},{7,5},{8,10},{9,11},{10,... | collective-permute-start | bytes 221192 | tf_op jit(solution)/shard_map/ppermute | solution.py:295
  40.6 0.0 copy-done.3
  40.6 0.0 collective-permute-start.9
  40.6 1.5 %shard_map.120 = (f32[32,1024]{1,0:T(8,128)S(1)}, f32[32,1024]{1,0:T(8,128)S(1)}, bf16[32,1024]{1,0:T(8,128)(2,1)S(1)}, f32[32,1024]{1,0:T(8,128)S(1)}) custom-call(s32[1]{0:T(128)} %bitcast.tensor_ref.refs_0_, bf16[32,1024]{1,0:T(8,128)(2,1)S(1)} %get-tuple-element.20.x_ref, bf16[1024,8192]{1,0:T(8,128)(2,1)S(1)} %bitcast.6), custom_call_target="tpu_custom_call" | custom-call | tf_op jit(solution)/shard_map/pallas_call | solution.py:236
  42.2 0.5 %collective-permute-done.12 = bf16[64,1024]{1,0:T(8,128)(2,1)S(1)} collective-permute-done((bf16[64,1024]{1,0:T(8,128)(2,1)S(1)}, bf16[64,1024]{1,0:T(8,128)(2,1)S(1)}, u32[]{:S(2)}, u32[]{:S(2)}) %collective-permute-start.12) | collective-permute-done | bytes 131104 | tf_op jit(solution)/shard_map/ppermute | solution.py:295
  42.7 1.6 %collective-permute-done.11.rest_3_ = bf16[32,1152]{1,0:T(8,128)(2,1)S(1)} collective-permute-done((bf16[32,1152]{1,0:T(8,128)(2,1)S(1)}, bf16[32,1152]{1,0:T(8,128)(2,1)S(1)}, u32[]{:S(2)}, u32[]{:S(2)}) %collective-permute-start.11) | collective-permute-done | bytes 73760 | tf_op jit(solution)/shard_map/ppermute | solution.py:295
  44.4 0.3 collective-permute-start.13
  44.8 1.4 %collective-permute-start.14 = (bf16[32,1024]{1,0:T(8,128)(2,1)S(1)}, bf16[32,1024]{1,0:T(8,128)(2,1)S(1)}, u32[]{:S(2)}, u32[]{:S(2)}) collective-permute-start(bf16[32,1024]{1,0:T(8,128)(2,1)S(1)} %get-tuple-element.23), channel_id=1, source_target_pairs={{0,1},{1,0},{2,3},{3,2},{4,5},{5,4},{6,7},{7,6},{8,9},{9,8},{10,11... | collective-permute-start | bytes 196616 | tf_op jit(solution)/shard_map/ppermute | solution.py:295
  46.2 0.8 %collective-permute-start.15 = (bf16[32,1024]{1,0:T(8,128)(2,1)S(1)}, bf16[32,1024]{1,0:T(8,128)(2,1)S(1)}, u32[]{:S(2)}, u32[]{:S(2)}) collective-permute-start(bf16[32,1024]{1,0:T(8,128)(2,1)S(1)} %get-tuple-element.27), channel_id=1, source_target_pairs={{0,2},{1,3},{2,0},{3,1},{4,6},{5,7},{6,4},{7,5},{8,10},{9,11},{10,... | collective-permute-start | bytes 196616 | tf_op jit(solution)/shard_map/ppermute | solution.py:295
  46.9 0.0 collective-permute-done.9.rest_1_
  47.0 2.1 %collective-permute-done.14.rest_6_ = bf16[32,1024]{1,0:T(8,128)(2,1)S(1)} collective-permute-done((bf16[32,1024]{1,0:T(8,128)(2,1)S(1)}, bf16[32,1024]{1,0:T(8,128)(2,1)S(1)}, u32[]{:S(2)}, u32[]{:S(2)}) %collective-permute-start.14) | collective-permute-done | bytes 65568 | tf_op jit(solution)/shard_map/ppermute | solution.py:295
  49.0 1.8 %collective-permute-done.15.rest_7_ = bf16[32,1024]{1,0:T(8,128)(2,1)S(1)} collective-permute-done((bf16[32,1024]{1,0:T(8,128)(2,1)S(1)}, bf16[32,1024]{1,0:T(8,128)(2,1)S(1)}, u32[]{:S(2)}, u32[]{:S(2)}) %collective-permute-start.15) | collective-permute-done | bytes 65568 | tf_op jit(solution)/shard_map/ppermute | solution.py:295
  50.8 0.0 collective-permute-done.13.rest_4_
  50.8 0.9 %final.1 = bf16[32,1024]{1,0:T(8,128)(2,1)} custom-call(f32[32,512]{1,0:T(8,128)S(1)} %add_convert_fusion.3.picks_ref.refs_6_, f32[32,128]{1,0:T(8,128)S(1)} %get-tuple-element.17.low_ref, bf16[256,1024]{1,0:T(8,128)(2,1)S(1)} %bitcast.12, bf16[256,1024]{1,0:T(8,128)(2,1)S(1)} %collective-permute-done.9.rest_1_, ...), custom_call_target="tpu_custom_call" | custom-call | flops 100000000 | bytes 1000000 | tf_op jit(solution)/shard_map/final/pallas_call | solution.py:438
  (17 shorter events, 0.1 us)
Async XLA Ops:
  0.0 14.1 %collective-permute-start = (bf16[32,1024]{1,0:T(8,128)(2,1)}, bf16[32,1024]{1,0:T(8,128)(2,1)S(1)}, u32[]{:S(2)}, u32[]{:S(2)}) collective-permute-start(bf16[32,1024]{1,0:T(8,128)(2,1)} %x_hbm.1), channel_id=1, source_target_pairs={{0,4},{1,5},{2,6},{3,7},{4,0},{5,1},{6,2},{7,3},{8,12},{9,13},{10,... | collective-permute-start | bytes 196616 | tf_op jit(solution)/shard_map/ppermute | solution.py:295
  4.1 18.4 %collective-permute-start.5 = (bf16[32,1024]{1,0:T(8,128)(2,1)}, bf16[32,1024]{1,0:T(8,128)(2,1)}, u32[]{:S(2)}, u32[]{:S(2)}) collective-permute-start(bf16[32,1024]{1,0:T(8,128)(2,1)} %x_hbm.1), channel_id=1, source_target_pairs={{0,2},{1,3},{2,0},{3,1},{4,6},{5,7},{6,4},{7,5},{8,10},{9,11},{10,... | collective-permute-start | bytes 196616 | tf_op jit(solution)/shard_map/ppermute | solution.py:295
  5.6 2.1 %collective-permute-start.1 = (bf16[256,1024]{1,0:T(8,128)(2,1)}, bf16[256,1024]{1,0:T(8,128)(2,1)S(1)}, u32[]{:S(2)}, u32[]{:S(2)}) collective-permute-start(bf16[256,1024]{1,0:T(8,128)(2,1)} %bitcast.13), channel_id=1, source_target_pairs={{0,8},{8,0},{1,9},{9,1},{2,10},{10,2},{3,11},{11,3},{4,12},{12,4},... | collective-permute-start | bytes 1572872 | tf_op jit(solution)/shard_map/ppermute | solution.py:300
  5.6 26.6 %collective-permute-start.7 = (bf16[256,1024]{1,0:T(8,128)(2,1)}, bf16[256,1024]{1,0:T(8,128)(2,1)S(1)}, u32[]{:S(2)}, u32[]{:S(2)}) collective-permute-start(bf16[256,1024]{1,0:T(8,128)(2,1)} %bitcast.7), channel_id=1, source_target_pairs={{0,8},{8,0},{1,9},{9,1},{2,10},{10,2},{3,11},{11,3},{4,12},{12,4},... | collective-permute-start | bytes 1572872 | tf_op jit(solution)/shard_map/ppermute | solution.py:300
  6.2 26.1 %collective-permute-start.8 = (bf16[256,1024]{1,0:T(8,128)(2,1)}, bf16[256,1024]{1,0:T(8,128)(2,1)S(1)}, u32[]{:S(2)}, u32[]{:S(2)}) collective-permute-start(bf16[256,1024]{1,0:T(8,128)(2,1)} %bitcast.9), channel_id=1, source_target_pairs={{0,8},{8,0},{1,9},{9,1},{2,10},{10,2},{3,11},{11,3},{4,12},{12,4},... | collective-permute-start | bytes 1572872 | tf_op jit(solution)/shard_map/ppermute | solution.py:300
  9.3 4.8 %collective-permute-start.2 = (f32[32,128]{1,0:T(8,128)S(1)}, f32[32,128]{1,0:T(8,128)S(1)}, u32[]{:S(2)}, u32[]{:S(2)}) collective-permute-start(f32[32,128]{1,0:T(8,128)S(1)} %get-tuple-element.15), channel_id=1, source_target_pairs={{0,4},{1,5},{2,6},{3,7},{4,0},{5,1},{6,2},{7,3},{8,12},{9,13},{10,... | collective-permute-start | bytes 49160 | tf_op jit(solution)/shard_map/ppermute | solution.py:295
  14.1 4.5 %collective-permute-start.3 = (bf16[32,1152]{1,0:T(8,128)(2,1)S(1)}, bf16[32,1152]{1,0:T(8,128)(2,1)}, u32[]{:S(2)}, u32[]{:S(2)}) collective-permute-start(bf16[32,1152]{1,0:T(8,128)(2,1)S(1)} %pad_maximum_fusion.1), channel_id=1, source_target_pairs={{0,2},{1,3},{2,0},{3,1},{4,6},{5,7},{6,4},{7,5},{8,10},{9,11},{10,... | collective-permute-start | bytes 221192 | tf_op jit(solution)/shard_map/ppermute | solution.py:295
  15.3 10.4 %copy-start = (bf16[8192,1024]{1,0:T(8,128)(2,1)S(1)}, bf16[8192,1024]{1,0:T(8,128)(2,1)}, u32[]{:S(2)}) copy-start(bf16[8192,1024]{1,0:T(8,128)(2,1)} %refs_2_.1) | copy-start | bytes 50331652
  20.9 6.7 %collective-permute-start.4 = (bf16[32,1152]{1,0:T(8,128)(2,1)S(1)}, bf16[32,1152]{1,0:T(8,128)(2,1)S(1)}, u32[]{:S(2)}, u32[]{:S(2)}) collective-permute-start(bf16[32,1152]{1,0:T(8,128)(2,1)S(1)} %pad_maximum_fusion.2), channel_id=1, source_target_pairs={{0,1},{1,0},{2,3},{3,2},{4,5},{5,4},{6,7},{7,6},{8,9},{9,8},{10,11... | collective-permute-start | bytes 221192 | tf_op jit(solution)/shard_map/ppermute | solution.py:295
  23.4 5.7 %collective-permute-start.6 = (bf16[96,1024]{1,0:T(8,128)(2,1)S(1)}, bf16[96,1024]{1,0:T(8,128)(2,1)S(1)}, u32[]{:S(2)}, u32[]{:S(2)}) collective-permute-start(bf16[96,1024]{1,0:T(8,128)(2,1)S(1)} %pad_maximum_fusion), channel_id=1, source_target_pairs={{0,1},{1,0},{2,3},{3,2},{4,5},{5,4},{6,7},{7,6},{8,9},{9,8},{10,11... | collective-permute-start | bytes 589832 | tf_op jit(solution)/shard_map/ppermute | solution.py:295
  25.7 6.5 %slice-start = ((s8[16777216]{0:T(1024)(128)(4,1)}), s8[4194304]{0:T(1024)(128)(4,1)S(1)}, s32[]{:S(2)}) async-start(s8[16777216]{0:T(1024)(128)(4,1)} %bitcast.5), calls=%async_computation | async-start | bytes 8388608
  25.7 6.5 %slice-start.1 = ((s8[16777216]{0:T(1024)(128)(4,1)}), s8[4194304]{0:T(1024)(128)(4,1)S(1)}, s32[]{:S(2)}) async-start(s8[16777216]{0:T(1024)(128)(4,1)} %bitcast.5), calls=%async_computation.1 | async-start | bytes 8388608
  25.7 6.5 %slice-start.2 = ((s8[16777216]{0:T(1024)(128)(4,1)}), s8[4194304]{0:T(1024)(128)(4,1)S(1)}, s32[]{:S(2)}) async-start(s8[16777216]{0:T(1024)(128)(4,1)} %bitcast.5), calls=%async_computation.2 | async-start | bytes 8388608
  27.6 4.7 %copy-start.1 = (bf16[4,64,1024]{2,1,0:T(8,128)(2,1)S(1)}, bf16[4,64,1024]{2,1,0:T(8,128)(2,1)}, u32[]{:S(2)}) copy-start(bf16[4,64,1024]{2,1,0:T(8,128)(2,1)} %param.18) | copy-start | bytes 1572868
  27.6 4.7 %copy-start.2 = (bf16[4,64,1024]{2,1,0:T(8,128)(2,1)S(1)}, bf16[4,64,1024]{2,1,0:T(8,128)(2,1)}, u32[]{:S(2)}) copy-start(bf16[4,64,1024]{2,1,0:T(8,128)(2,1)} %param.19) | copy-start | bytes 1572868
  29.1 3.2 %slice-start.3 = ((s8[16777216]{0:T(1024)(128)(4,1)}), s8[4194304]{0:T(1024)(128)(4,1)S(1)}, s32[]{:S(2)}) async-start(s8[16777216]{0:T(1024)(128)(4,1)} %bitcast.5), calls=%async_computation.3 | async-start | bytes 8388608
  35.4 5.3 %copy-start.3 = (bf16[4,64,1024]{2,1,0:T(8,128)(2,1)S(1)}, bf16[4,64,1024]{2,1,0:T(8,128)(2,1)}, u32[]{:S(2)}) copy-start(bf16[4,64,1024]{2,1,0:T(8,128)(2,1)} %param.20) | copy-start | bytes 1572868
  35.4 4.5 %collective-permute-start.10 = (bf16[32,1152]{1,0:T(8,128)(2,1)S(1)}, bf16[32,1152]{1,0:T(8,128)(2,1)S(1)}, u32[]{:S(2)}, u32[]{:S(2)}) collective-permute-start(bf16[32,1152]{1,0:T(8,128)(2,1)S(1)} %get-tuple-element.18), channel_id=1, source_target_pairs={{0,1},{1,0},{2,3},{3,2},{4,5},{5,4},{6,7},{7,6},{8,9},{9,8},{10,11... | collective-permute-start | bytes 221192 | tf_op jit(solution)/shard_map/ppermute | solution.py:295
  37.8 5.0 %collective-permute-start.12 = (bf16[64,1024]{1,0:T(8,128)(2,1)S(1)}, bf16[64,1024]{1,0:T(8,128)(2,1)S(1)}, u32[]{:S(2)}, u32[]{:S(2)}) collective-permute-start(bf16[64,1024]{1,0:T(8,128)(2,1)S(1)} %shard_map.121), channel_id=1, source_target_pairs={{0,1},{1,0},{2,3},{3,2},{4,5},{5,4},{6,7},{7,6},{8,9},{9,8},{10,11... | collective-permute-start | bytes 393224 | tf_op jit(solution)/shard_map/ppermute | solution.py:295
  39.9 4.4 %collective-permute-start.11 = (bf16[32,1152]{1,0:T(8,128)(2,1)S(1)}, bf16[32,1152]{1,0:T(8,128)(2,1)S(1)}, u32[]{:S(2)}, u32[]{:S(2)}) collective-permute-start(bf16[32,1152]{1,0:T(8,128)(2,1)S(1)} %pad_maximum_fusion.3), channel_id=1, source_target_pairs={{0,2},{1,3},{2,0},{3,1},{4,6},{5,7},{6,4},{7,5},{8,10},{9,11},{10,... | collective-permute-start | bytes 221192 | tf_op jit(solution)/shard_map/ppermute | solution.py:295
  40.6 6.3 %collective-permute-start.9 = (bf16[256,1024]{1,0:T(8,128)(2,1)S(1)}, bf16[256,1024]{1,0:T(8,128)(2,1)S(1)}, u32[]{:S(2)}, u32[]{:S(2)}) collective-permute-start(bf16[256,1024]{1,0:T(8,128)(2,1)S(1)} %bitcast.11), channel_id=1, source_target_pairs={{0,8},{8,0},{1,9},{9,1},{2,10},{10,2},{3,11},{11,3},{4,12},{12,4},... | collective-permute-start | bytes 1572872 | tf_op jit(solution)/shard_map/ppermute | solution.py:300
  44.4 6.4 %collective-permute-start.13 = (bf16[32,1152]{1,0:T(8,128)(2,1)S(1)}, bf16[32,1152]{1,0:T(8,128)(2,1)S(1)}, u32[]{:S(2)}, u32[]{:S(2)}) collective-permute-start(bf16[32,1152]{1,0:T(8,128)(2,1)S(1)} %pad_maximum_fusion.4), channel_id=1, source_target_pairs={{0,4},{1,5},{2,6},{3,7},{4,0},{5,1},{6,2},{7,3},{8,12},{9,13},{10,... | collective-permute-start | bytes 221192 | tf_op jit(solution)/shard_map/ppermute | solution.py:295
  44.8 4.3 %collective-permute-start.14 = (bf16[32,1024]{1,0:T(8,128)(2,1)S(1)}, bf16[32,1024]{1,0:T(8,128)(2,1)S(1)}, u32[]{:S(2)}, u32[]{:S(2)}) collective-permute-start(bf16[32,1024]{1,0:T(8,128)(2,1)S(1)} %get-tuple-element.23), channel_id=1, source_target_pairs={{0,1},{1,0},{2,3},{3,2},{4,5},{5,4},{6,7},{7,6},{8,9},{9,8},{10,11... | collective-permute-start | bytes 196616 | tf_op jit(solution)/shard_map/ppermute | solution.py:295
  46.2 4.6 %collective-permute-start.15 = (bf16[32,1024]{1,0:T(8,128)(2,1)S(1)}, bf16[32,1024]{1,0:T(8,128)(2,1)S(1)}, u32[]{:S(2)}, u32[]{:S(2)}) collective-permute-start(bf16[32,1024]{1,0:T(8,128)(2,1)S(1)} %get-tuple-element.27), channel_id=1, source_target_pairs={{0,2},{1,3},{2,0},{3,1},{4,6},{5,7},{6,4},{7,5},{8,10},{9,11},{10,... | collective-permute-start | bytes 196616 | tf_op jit(solution)/shard_map/ppermute | solution.py:295

commit v5 on v4

--- a/solution.py
+++ b/solution.py
@@ -14,7 +14,6 @@
 SMEM = pl.BlockSpec(memory_space=pltpu.SMEM)
 HBM = pl.BlockSpec(memory_space=pltpu.HBM)
 LANES = 128
-PIECES = 4
 GRANT = 12 << 20
 BAND = 32
 
@@ -95,39 +94,20 @@
     )(in_hbm(x), picks, *[in_hbm(h) for h in hints], in_hbm(downs[0]), *downs[1:])
 
 
-def lead_kernel(tensor_ref, chunk, weight, out_ref, buf, sems):
-    width = buf.shape[0]
-    piece = width // PIECES
-    copies = []
-    for p in range(PIECES):
-        at = pl.multiple_of(tensor_ref[0] * width + p * piece, piece)
-        spot = pl.ds(p * piece, piece)
-        copies.append(pltpu.make_async_copy(weight.at[pl.ds(at, piece), :], buf.at[spot, :], sems.at[p]))
-    for c in copies:
-        c.start()
-    total = 0.0
-    for p, c in enumerate(copies):
-        c.wait()
-        span = slice(p * piece, (p + 1) * piece)
-        total = total + dot(chunk[:, span], buf[span, :])
-    out_ref[...] = total
-
-
-def lead_call(chunk, tensor_at, weight):
-    rows, width = chunk.shape
-    wide = weight.shape[1]
+def begin_kernel(tensor_ref, weight, out_ref):
+    out_ref[0] = tensor_ref[0]
+
+
+def begin_call(tensor_at, weight):
     return pl.pallas_call(
-        lead_kernel,
-        in_specs=[SMEM, VMEM, HBM],
-        out_specs=VMEM,
-        out_shape=jax.ShapeDtypeStruct((rows, wide), jnp.float32),
-        scratch_shapes=[
-            pltpu.VMEM((width, wide), weight.dtype),
-            pltpu.SemaphoreType.DMA((PIECES,)),
-        ],
-        name="lead",
-        **params((2 * rows * width * wide, 2 * width * wide)),
-    )(tensor_at, chunk, in_hbm(weight))
+        begin_kernel,
+        in_specs=[SMEM, HBM],
+        out_specs=SMEM,
+        out_shape=jax.ShapeDtypeStruct(tensor_at.shape, tensor_at.dtype),
+        name="begin",
+        compiler_params=pltpu.CompilerParams(vmem_limit_bytes=4 << 20, has_side_effects=True),
+        cost_estimate=pl.CostEstimate(flops=1000, bytes_accessed=1000, transcendentals=0),
+    )(tensor_at, in_hbm(weight))
 
 
 def dense_kernel(shards, ks, spans, given, first, tensor_ref, weight, *rest):
@@ -326,31 +306,35 @@
     where = {0: (near, 0)}
     chain = 0
     for bit in reversed(bits):
-        rest = [k for k in where if k != chain]
-        if chain == 0:
+        rest = [k for k in where if k not in (0, chain)]
+        if bit != 1 or not chain:
             where[bit] = (across(hidden, bit), 0)
-            low = low + across(low, bit)
-        else:
+        if chain:
             joined = jnp.concatenate([where[chain][0][:, :width], low.astype(jnp.bfloat16)], axis=1)
             got = across(joined, bit)
             where[chain | bit] = (got, 0)
             low = low + got[:, width:].astype(jnp.float32)
-        if rest and bit == 1:
-            got = jnp.concatenate([where[k][0][:, :width] for k in rest], axis=0)
-            got = across(got, 1)
-            for i, k in enumerate(rest):
-                where[k | 1] = (got, i * rows)
+        else:
+            low = low + across(low, bit)
+        if chain and bit == 1:
+            for ks in ([0, bits[-1]], rest):
+                ks = [k for k in ks if k != chain and k | 1 not in where]
+                if ks:
+                    got = jnp.concatenate([where[k][0][:, :width] for k in ks], axis=0)
+                    got = across(got, 1)
+                    for i, k in enumerate(ks):
+                        where[k | 1] = (got, i * rows)
         else:
             for k in rest:
-                array = hidden if k == 0 else where[k][0][:, :width]
-                where[k | bit] = (across(array, bit), 0)
+                where[k | bit] = (across(where[k][0][:, :width], bit), 0)
         chain |= bit
 
     last = chain
-    ahead = [k for k in where if k and not k & 1 and k != last ^ 1]
+    first = [k for k in where if not k & 1 and k != last ^ 1]
     second = [last ^ 1] + [k for k in where if k & 1 and k != last]
-    query = lead_call(near, tensor_at, w_query)
-    for ks, hints in ((ahead, [output_weight]), (second, [])):
+    begin_call(tensor_at, w_query)
+    query = None
+    for ks, hints in ((first, [output_weight]), (second, [])):
         query = dense_call(shards, where, ks, tensor_at, w_query, query, rows, hints)
 
     wide = w_query.shape[1]
@@ -362,7 +346,7 @@
     depth = output_weight.shape[0]
     whole = shards - 1
     even = [k for k in sorted(where, reverse=True) if not k & 1]
-    k_outs = [whole] + even[:-1][:1]
+    k_outs = [whole]
     sizes = (last, k_outs, replicas, kv_count, group, head, local_heads, group_all, width)
     map_in, map_out = (stored * rank, wide), (stored * rank, depth)
     low2, mixed, payload, *blocks = pl.pallas_call(
@@ -408,8 +392,8 @@
     parts = dict(zip(k_outs[1:], blocks))
     even = [k for k in even if k not in parts]
     plan = [
-        [(odd, bf16)] * bool(odd),
-        [([k], f32) for k in even[:-1]] + [([1], bf16)] * (whole > 1) + [([k], f32) for k in even[-1:]],
+        [([k], f32) for k in even[:1]] + [(odd, bf16)] * bool(odd) + [([1], bf16)] * (whole > 1),
+        [([k], f32) for k in even[1:]],
     ]
     plan = [groups for groups in plan if groups]
     for groups in plan:
@@ -425,7 +409,10 @@
         main = parts[k]
         bit = 1
         while bit < low_bit(k):
-            main = main + came[k | bit][:, :out_width].astype(jnp.float32)
+            term = came[k | bit][:, :out_width]
+            if k not in chain:
+                term = lax.optimization_barrier(term)
+            main = main + term.astype(jnp.float32)
             bit *= 2
         if k in chain:
             carried = low2

time: 52 us -> 58.1 us (1.12)
  local copies, waits for them, and re-layouts: 1.72 us -> 9.97 us
  waiting for transfers between devices: 15.9 us -> 11.9 us
  starting transfers between devices: 14.5 us -> 16.4 us
    unnamed x16 -> x28, local copies, waits for them, and re-layouts: 0.05 us -> 9.89 us
    ppermute x12 -> x13, waiting for transfers between devices: 15.3 us -> 11.3 us  [across(): return lax.ppermute(x, 'tensor', [(i, i ^ bit) for i in range(shards)])]
    ppermute x12 -> x13, starting transfers between devices: 14 us -> 15.9 us  [across(): return lax.ppermute(x, 'tensor', [(i, i ^ bit) for i in range(shards)])]
    slice x1, local copies, waits for them, and re-layouts: 1.59 us -> 0.01 us  [per_device(): where[chain][0][:, :width]]
    pallas_call x1, Pallas kernels: 1.75 us -> 0.52 us  [begin_call(): pl.pallas_call(begin_kernel, in_specs=[SMEM, HBM], out_specs=SMEM, out_sh...]
    convert_element_type x2, other arithmetic: 0.71 us -> 0.01 us  [per_device(): low.astype(jnp.bfloat16)]
    concatenate x2, other arithmetic: 0.02 us -> 0.65 us  [per_device(): jnp.concatenate([where[chain][0][:, :width], low.astype(jnp.bfloat16)], a...]
  transfers between devices with their start and end apart: 16 -> 17, of which waited for: 8 -> 8; matrix products, arithmetic and copies ran while one was open for 12% -> 8% of each run, Pallas kernels for 20% -> 17%
where the time goes in v5:
time: 58.1 us; the launch traced here: 57.9 us
  starting transfers between devices  16.4 us (28%)
  Pallas kernels  14.6 us (25%)
  waiting for transfers between devices  11.9 us (20%)
  local copies, waits for them, and re-layouts  9.97 us (17%)
  other arithmetic  4.54 us (8%)
    ppermute x13, starting transfers between devices, across(): return lax.ppermute(x, 'tensor', [(i, i ^ bit) for i in range(shards)])  15.9 us
    ppermute x13, waiting for transfers between devices, across(): return lax.ppermute(x, 'tensor', [(i, i ^ bit) for i in range(shards)])  11.3 us
    unnamed x28, local copies, waits for them, and re-layouts  9.89 us
    pallas_call x2, Pallas kernels, dense_call(): pl.pallas_call(functools.partial(dense_kernel, shards, ks, spans, len(arr...  5.34 us
    pallas_call x1, Pallas kernels, per_device(): pl.pallas_call(functools.partial(mix_kernel, sizes), in_specs=[SMEM, VMEM...  3.59 us
    pallas_call x2, Pallas kernels, resident_call(): pl.pallas_call(functools.partial(resident_kernel, ks, spans), in_specs=[S...  2.73 us
    pallas_call x1, Pallas kernels, low_call(): pl.pallas_call(functools.partial(low_kernel, len(downs), len(hints)), in_...  1.53 us
    add x1, other arithmetic, per_device(): low = low + got[:, width:].astype(jnp.float32)  1.51 us
  transfers between devices with their start and end apart: 17, of which 8 were waited for; matrix products, arithmetic and copies ran while one was open for 8% of the time, Pallas kernels for 17%

profile of v5, /device:TPU:0, one launch (start us, length us, event | category | flops | bytes accessed | tf_op | source)
XLA Modules:
  0.0 57.9 jit_solution(13963384663237463724)
XLA Ops:
  0.0 4.1 %collective-permute-start = (bf16[32,1024]{1,0:T(8,128)(2,1)}, bf16[32,1024]{1,0:T(8,128)(2,1)S(1)}, u32[]{:S(2)}, u32[]{:S(2)}) collective-permute-start(bf16[32,1024]{1,0:T(8,128)(2,1)} %x_hbm.1), channel_id=1, source_target_pairs={{0,4},{1,5},{2,6},{3,7},{4,0},{5,1},{6,2},{7,3},{8,12},{9,13},{10,... | collective-permute-start | bytes 196616 | tf_op jit(solution)/shard_map/ppermute | solution.py:275
  4.1 1.6 %collective-permute-start.6 = (bf16[32,1024]{1,0:T(8,128)(2,1)}, bf16[32,1024]{1,0:T(8,128)(2,1)}, u32[]{:S(2)}, u32[]{:S(2)}) collective-permute-start(bf16[32,1024]{1,0:T(8,128)(2,1)} %x_hbm.1), channel_id=1, source_target_pairs={{0,2},{1,3},{2,0},{3,1},{4,6},{5,7},{6,4},{7,5},{8,10},{9,11},{10,... | collective-permute-start | bytes 196616 | tf_op jit(solution)/shard_map/ppermute | solution.py:275
  5.6 0.0 collective-permute-start.1
  5.6 0.5 collective-permute-start.8
  6.2 0.0 collective-permute-start.9
  6.2 0.8 %select_reduce_fusion = s32[64]{0:T(128)S(1)} fusion(s32[8]{0:T(128)} %param.22, s32[64]{0:T(128)} %param.21), kind=kLoop, calls=%fused_computation.30 | loop fusion | flops 1472 | bytes 544 | tf_op jit(solution)/shard_map/reduce_sum | solution.py:285
  7.0 0.1 dynamic_slice.3
  7.0 0.1 broadcast_compare_fusion.1
  7.1 0.6 %collective-permute-done.1.rest_1_ = bf16[256,1024]{1,0:T(8,128)(2,1)S(1)} collective-permute-done((bf16[256,1024]{1,0:T(8,128)(2,1)}, bf16[256,1024]{1,0:T(8,128)(2,1)S(1)}, u32[]{:S(2)}, u32[]{:S(2)}) %collective-permute-start.1) | collective-permute-done | bytes 524320 | tf_op jit(solution)/shard_map/ppermute | solution.py:280
  7.8 1.5 %low.1 = (f32[32,128]{1,0:T(8,128)S(1)}, bf16[32,1024]{1,0:T(8,128)(2,1)S(1)}) custom-call(bf16[32,1024]{1,0:T(8,128)(2,1)} %x_hbm.1, f32[32,512]{1,0:T(8,128)S(1)} %add_convert_fusion.3.picks_ref.refs_6_, bf16[256,1024]{1,0:T(8,128)(2,1)} %bitcast.16, bf16[256,1024]{1,0:T(8,128)(2,1)S(1)} %collective-permute-done.1.rest_1_), custom_call_target="tpu_custom_call" | custom-call | flops 100000000 | bytes 1000000 | tf_op jit(solution)/shard_map/low/pallas_call | solution.py:82
  9.3 0.4 collective-permute-start.2
  9.7 0.0 collective-permute-done.6.rest_2_
  9.7 1.5 %collective-permute-start.7 = (bf16[32,1024]{1,0:T(8,128)(2,1)}, bf16[32,1024]{1,0:T(8,128)(2,1)}, u32[]{:S(2)}, u32[]{:S(2)}) collective-permute-start(bf16[32,1024]{1,0:T(8,128)(2,1)} %collective-permute-done.6.rest_2_), channel_id=1, source_target_pairs={{0,1},{1,0},{2,3},{3,2},{4,5},{5,4},{6,7},{7,6},{8,9},{9,8},{10,11... | collective-permute-start | bytes 196616 | tf_op jit(solution)/shard_map/ppermute | solution.py:275
  11.2 2.8 %collective-permute-done.2 = f32[32,128]{1,0:T(8,128)S(1)} collective-permute-done((f32[32,128]{1,0:T(8,128)S(1)}, f32[32,128]{1,0:T(8,128)S(1)}, u32[]{:S(2)}, u32[]{:S(2)}) %collective-permute-start.2) | collective-permute-done | bytes 16416 | tf_op jit(solution)/shard_map/ppermute | solution.py:275
  14.1 0.0 collective-permute-done.rest_1_
  14.1 0.5 collective-permute-start.3
  14.6 0.7 %pad_maximum_fusion = bf16[64,1024]{1,0:T(8,128)(2,1)} fusion(bf16[32,1024]{1,0:T(8,128)(2,1)S(1)} %collective-permute-done.rest_1_, bf16[32,1024]{1,0:T(8,128)(2,1)S(1)} %get-tuple-element.17.rest_0_), kind=kLoop, calls=%fused_computation | loop fusion | flops 262144 | bytes 262144 | tf_op jit(solution)/shard_map/concatenate | solution.py:323
  15.2 1.5 %collective-permute-start.5 = (bf16[64,1024]{1,0:T(8,128)(2,1)}, bf16[64,1024]{1,0:T(8,128)(2,1)S(1)}, u32[]{:S(2)}, u32[]{:S(2)}) collective-permute-start(bf16[64,1024]{1,0:T(8,128)(2,1)} %pad_maximum_fusion), channel_id=1, source_target_pairs={{0,1},{1,0},{2,3},{3,2},{4,5},{5,4},{6,7},{7,6},{8,9},{9,8},{10,11... | collective-permute-start | bytes 393224 | tf_op jit(solution)/shard_map/ppermute | solution.py:275
  16.7 1.8 %collective-permute-done.3.rest_0_ = bf16[32,1152]{1,0:T(8,128)(2,1)S(1)} collective-permute-done((bf16[32,1152]{1,0:T(8,128)(2,1)S(1)}, bf16[32,1152]{1,0:T(8,128)(2,1)S(1)}, u32[]{:S(2)}, u32[]{:S(2)}) %collective-permute-start.3) | collective-permute-done | bytes 73760 | tf_op jit(solution)/shard_map/ppermute | solution.py:275
  18.5 0.6 %pad_maximum_fusion.2 = bf16[32,1152]{1,0:T(8,128)(2,1)} fusion(bf16[32,128]{1,0:T(8,128)(2,1)S(1)} %fusion.2, bf16[32,1024]{1,0:T(8,128)(2,1)S(1)} %slice.37), kind=kLoop, calls=%fused_computation.9 | loop fusion | flops 147456 | bytes 147456 | tf_op jit(solution)/shard_map/concatenate | solution.py:313
  19.2 1.5 %collective-permute-start.4 = (bf16[32,1152]{1,0:T(8,128)(2,1)}, bf16[32,1152]{1,0:T(8,128)(2,1)}, u32[]{:S(2)}, u32[]{:S(2)}) collective-permute-start(bf16[32,1152]{1,0:T(8,128)(2,1)} %pad_maximum_fusion.2), channel_id=1, source_target_pairs={{0,1},{1,0},{2,3},{3,2},{4,5},{5,4},{6,7},{7,6},{8,9},{9,8},{10,11... | collective-permute-start | bytes 221192 | tf_op jit(solution)/shard_map/ppermute | solution.py:275
  20.7 0.7 %fusion.1.refs_13_ = f32[32,1024]{1,0:T(8,128)S(1)} fusion(s32[32]{0:T(128)} %param.23, s32[1024]{0:T(1024)S(1)} %get-tuple-element.34, s32[1024]{0:T(1024)S(1)} %get-tuple-element.35, s32[32]{0:T(128)S(1)} %get-tuple-element.39, s32[32]{0:T(128)S(1)} %get-tuple-element.40, s32[1024]{0:T(1024)S(1)} %get-tuple-element.33, s32[1024]{0:T(1024)S(1)} %get-tuple-element.36, ...), kind=kLoop, calls=%fused_computation.7 | loop fusion | flops 229376 | bytes 149920 | tf_op jit(solution)/shard_map/convert_element_type | solution.py:298
  21.5 0.0 copy-start
  21.5 5.8 %copy-done = bf16[8192,1024]{1,0:T(8,128)(2,1)S(1)} copy-done((bf16[8192,1024]{1,0:T(8,128)(2,1)S(1)}, bf16[8192,1024]{1,0:T(8,128)(2,1)}, u32[]{:S(2)}) %copy-start) | copy-done | bytes 16777240
  27.2 0.0 slice-start.5
  27.3 0.0 slice-start.6
  27.3 2.2 %shard_map.118.rest_3_ = f32[32,1024]{1,0:T(8,128)S(1)} custom-call(s32[1]{0:T(128)} %bitcast.tensor_ref.refs_0_, bf16[8192,1024]{1,0:T(8,128)(2,1)S(1)} %copy-done, bf16[32,1024]{1,0:T(8,128)(2,1)S(1)} %get-tuple-element.17.rest_0_, bf16[32,1024]{1,0:T(8,128)(2,1)S(1)} %collective-permute-done.rest_1_, bf16[32,1024]{1,0:T(8,128)(2,1)} %collective-permute-done.6.rest_2_, ...), custom_call_target="tpu_custom_call" | custom-call | flops 201326592 | bytes 1000000 | tf_op jit(solution)/shard_map/pallas_call | solution.py:133
  29.4 0.0 slice-start.3
  29.5 0.0 slice-start.7
  29.5 0.0 copy-start.1
  29.5 0.0 copy-start.2
  29.5 0.0 collective-permute-done.7.rest_2_
  29.5 0.0 collective-permute-done.5.rest_1_
  29.5 3.2 %shard_map.119.refs_4_ = f32[32,1024]{1,0:T(8,128)S(1)} custom-call(s32[1]{0:T(128)} %bitcast.tensor_ref.refs_0_, bf16[8192,1024]{1,0:T(8,128)(2,1)S(1)} %copy-done, bf16[32,1152]{1,0:T(8,128)(2,1)S(1)} %collective-permute-done.3.rest_0_, bf16[64,1024]{1,0:T(8,128)(2,1)S(1)} %collective-permute-done.5.rest_1_, ...), custom_call_target="tpu_custom_call" | custom-call | flops 268435456 | bytes 1000000 | tf_op jit(solution)/shard_map/pallas_call | solution.py:133
  32.7 0.0 collective-permute-done.4.refs_1_
  32.7 1.5 %convert_add_fusion.1.refs_5_ = f32[32,128]{1,0:T(8,128)S(1)} fusion(f32[32,128]{1,0:T(8,128)S(1)} %copy-done.5, bf16[32,1152]{1,0:T(8,128)(2,1)} %collective-permute-done.4.refs_1_, bf16[32,1152]{1,0:T(8,128)(2,1)S(1)} %collective-permute-done.3.rest_0_), kind=kLoop, calls=%fused_computation.15 | loop fusion | flops 16384 | bytes 49152 | tf_op jit(solution)/shard_map/add | solution.py:316
  34.2 0.0 collective-permute-done.8.refs_8_
  34.2 0.0 collective-permute-done.9.refs_10_
  34.3 0.1 slice-done.5
  34.4 1.2 %slice-done.6 = s8[4194304]{0:T(1024)(128)(4,1)S(1)} async-done(((s8[16777216]{0:T(1024)(128)(4,1)}), s8[4194304]{0:T(1024)(128)(4,1)S(1)}, s32[]{:S(2)}) %slice-start.6) | async-done | bytes 4194328
  35.6 1.4 %slice-done.3 = s8[4194304]{0:T(1024)(128)(4,1)S(1)} async-done(((s8[16777216]{0:T(1024)(128)(4,1)}), s8[4194304]{0:T(1024)(128)(4,1)S(1)}, s32[]{:S(2)}) %slice-start.3) | async-done | bytes 4194328
  37.0 1.2 %slice-done.7 = s8[4194304]{0:T(1024)(128)(4,1)S(1)} async-done(((s8[16777216]{0:T(1024)(128)(4,1)}), s8[4194304]{0:T(1024)(128)(4,1)S(1)}, s32[]{:S(2)}) %slice-start.7) | async-done | bytes 4194328
  38.2 0.0 copy-done.1
  38.2 0.2 copy-done.2
  38.3 3.6 %mix.1 = (f32[32,128]{1,0:T(8,128)S(1)}, bf16[32,1024]{1,0:T(8,128)(2,1)S(1)}, bf16[32,1152]{1,0:T(8,128)(2,1)S(1)}) custom-call(s32[1]{0:T(128)} %bitcast.tensor_ref.refs_0_, bf16[32,1152]{1,0:T(8,128)(2,1)} %collective-permute-done.4.refs_1_, bf16[8192,1024]{1,0:T(8,128)(2,1)S(1)} %bitcast.8, bf16[1024,8192]{1,0:T(8,128)(2,1)S(1)} %bitcast.6, ...), custom_call_target="tpu_custom_call" | custom-call | flops 1000000000 | bytes 6291456 | tf_op jit(solution)/shard_map/mix/pallas_call | solution.py:352
  41.9 0.0 copy-start.3
  42.0 0.6 collective-permute-start.11
  42.5 1.5 %shard_map.120 = (f32[32,1024]{1,0:T(8,128)S(1)}, bf16[64,1024]{1,0:T(8,128)(2,1)S(1)}, bf16[32,1024]{1,0:T(8,128)(2,1)S(1)}) custom-call(s32[1]{0:T(128)} %bitcast.tensor_ref.refs_0_, bf16[32,1024]{1,0:T(8,128)(2,1)S(1)} %get-tuple-element.20.x_ref, bf16[1024,8192]{1,0:T(8,128)(2,1)S(1)} %bitcast.6), custom_call_target="tpu_custom_call" | custom-call | tf_op jit(solution)/shard_map/pallas_call | solution.py:216
  44.1 1.5 %collective-permute-start.13 = (bf16[64,1024]{1,0:T(8,128)(2,1)S(1)}, bf16[64,1024]{1,0:T(8,128)(2,1)S(1)}, u32[]{:S(2)}, u32[]{:S(2)}) collective-permute-start(bf16[64,1024]{1,0:T(8,128)(2,1)S(1)} %get-tuple-element.23), channel_id=1, source_target_pairs={{0,1},{1,0},{2,3},{3,2},{4,5},{5,4},{6,7},{7,6},{8,9},{9,8},{10,11... | collective-permute-start | bytes 393224 | tf_op jit(solution)/shard_map/ppermute | solution.py:275
  45.6 0.8 %collective-permute-done.11.rest_2_ = bf16[32,1152]{1,0:T(8,128)(2,1)S(1)} collective-permute-done((bf16[32,1152]{1,0:T(8,128)(2,1)S(1)}, bf16[32,1152]{1,0:T(8,128)(2,1)S(1)}, u32[]{:S(2)}, u32[]{:S(2)}) %collective-permute-start.11) | collective-permute-done | bytes 73760 | tf_op jit(solution)/shard_map/ppermute | solution.py:275
  46.4 0.5 collective-permute-start.12
  46.9 0.0 collective-permute-start.10
  46.9 1.2 %shard_map.121 = (f32[32,1024]{1,0:T(8,128)S(1)}, f32[32,1024]{1,0:T(8,128)S(1)}, f32[32,1024]{1,0:T(8,128)S(1)}) custom-call(s32[1]{0:T(128)} %bitcast.tensor_ref.refs_0_, bf16[32,1024]{1,0:T(8,128)(2,1)S(1)} %get-tuple-element.20.x_ref, bf16[1024,8192]{1,0:T(8,128)(2,1)S(1)} %bitcast.6), custom_call_target="tpu_custom_call" | custom-call | tf_op jit(solution)/shard_map/pallas_call | solution.py:216
  48.1 1.3 %collective-permute-start.15 = (bf16[32,1024]{1,0:T(8,128)(2,1)S(1)}, bf16[32,1024]{1,0:T(8,128)(2,1)S(1)}, u32[]{:S(2)}, u32[]{:S(2)}) collective-permute-start(bf16[32,1024]{1,0:T(8,128)(2,1)S(1)} %get-tuple-element.25), channel_id=1, source_target_pairs={{0,1},{1,0},{2,3},{3,2},{4,5},{5,4},{6,7},{7,6},{8,9},{9,8},{10,11... | collective-permute-start | bytes 196616 | tf_op jit(solution)/shard_map/ppermute | solution.py:275
  49.4 0.0 collective-permute-done.13
  49.4 1.4 %collective-permute-done.12.rest_3_ = bf16[32,1152]{1,0:T(8,128)(2,1)S(1)} collective-permute-done((bf16[32,1152]{1,0:T(8,128)(2,1)S(1)}, bf16[32,1152]{1,0:T(8,128)(2,1)S(1)}, u32[]{:S(2)}, u32[]{:S(2)}) %collective-permute-start.12) | collective-permute-done | bytes 73760 | tf_op jit(solution)/shard_map/ppermute | solution.py:275
  50.9 0.5 collective-permute-start.14
  51.4 0.5 collective-permute-start.16
  51.9 0.5 begin.1
  52.4 0.0 collective-permute-done.10.rest_1_
  52.5 0.1 collective-permute-done.15.rest_6_
  52.6 3.4 %collective-permute-done.16.rest_7_ = bf16[32,1024]{1,0:T(8,128)(2,1)S(1)} collective-permute-done((bf16[32,1024]{1,0:T(8,128)(2,1)S(1)}, bf16[32,1024]{1,0:T(8,128)(2,1)S(1)}, u32[]{:S(2)}, u32[]{:S(2)}) %collective-permute-start.16) | collective-permute-done | bytes 65568 | tf_op jit(solution)/shard_map/ppermute | solution.py:275
  56.0 0.9 %collective-permute-done.14.rest_4_ = bf16[32,1152]{1,0:T(8,128)(2,1)S(1)} collective-permute-done((bf16[32,1152]{1,0:T(8,128)(2,1)S(1)}, bf16[32,1152]{1,0:T(8,128)(2,1)S(1)}, u32[]{:S(2)}, u32[]{:S(2)}) %collective-permute-start.14) | collective-permute-done | bytes 73760 | tf_op jit(solution)/shard_map/ppermute | solution.py:275
  56.9 0.9 %final.1 = bf16[32,1024]{1,0:T(8,128)(2,1)} custom-call(f32[32,512]{1,0:T(8,128)S(1)} %add_convert_fusion.3.picks_ref.refs_6_, f32[32,128]{1,0:T(8,128)S(1)} %get-tuple-element.18.low_ref, bf16[256,1024]{1,0:T(8,128)(2,1)S(1)} %bitcast.14, bf16[256,1024]{1,0:T(8,128)(2,1)S(1)} %collective-permute-done.10.rest_1_, ...), custom_call_target="tpu_custom_call" | custom-call | flops 100000000 | bytes 1000000 | tf_op jit(solution)/shard_map/final/pallas_call | solution.py:425
  (34 shorter events, 0.2 us)
Async XLA Ops:
  0.0 14.1 %collective-permute-start = (bf16[32,1024]{1,0:T(8,128)(2,1)}, bf16[32,1024]{1,0:T(8,128)(2,1)S(1)}, u32[]{:S(2)}, u32[]{:S(2)}) collective-permute-start(bf16[32,1024]{1,0:T(8,128)(2,1)} %x_hbm.1), channel_id=1, source_target_pairs={{0,4},{1,5},{2,6},{3,7},{4,0},{5,1},{6,2},{7,3},{8,12},{9,13},{10,... | collective-permute-start | bytes 196616 | tf_op jit(solution)/shard_map/ppermute | solution.py:275
  4.1 5.6 %collective-permute-start.6 = (bf16[32,1024]{1,0:T(8,128)(2,1)}, bf16[32,1024]{1,0:T(8,128)(2,1)}, u32[]{:S(2)}, u32[]{:S(2)}) collective-permute-start(bf16[32,1024]{1,0:T(8,128)(2,1)} %x_hbm.1), channel_id=1, source_target_pairs={{0,2},{1,3},{2,0},{3,1},{4,6},{5,7},{6,4},{7,5},{8,10},{9,11},{10,... | collective-permute-start | bytes 196616 | tf_op jit(solution)/shard_map/ppermute | solution.py:275
  5.6 2.1 %collective-permute-start.1 = (bf16[256,1024]{1,0:T(8,128)(2,1)}, bf16[256,1024]{1,0:T(8,128)(2,1)S(1)}, u32[]{:S(2)}, u32[]{:S(2)}) collective-permute-start(bf16[256,1024]{1,0:T(8,128)(2,1)} %bitcast.15), channel_id=1, source_target_pairs={{0,8},{8,0},{1,9},{9,1},{2,10},{10,2},{3,11},{11,3},{4,12},{12,4},... | collective-permute-start | bytes 1572872 | tf_op jit(solution)/shard_map/ppermute | solution.py:280
  5.6 28.6 %collective-permute-start.8 = (bf16[256,1024]{1,0:T(8,128)(2,1)}, bf16[256,1024]{1,0:T(8,128)(2,1)S(1)}, u32[]{:S(2)}, u32[]{:S(2)}) collective-permute-start(bf16[256,1024]{1,0:T(8,128)(2,1)} %bitcast.9), channel_id=1, source_target_pairs={{0,8},{8,0},{1,9},{9,1},{2,10},{10,2},{3,11},{11,3},{4,12},{12,4},... | collective-permute-start | bytes 1572872 | tf_op jit(solution)/shard_map/ppermute | solution.py:280
  6.2 28.1 %collective-permute-start.9 = (bf16[256,1024]{1,0:T(8,128)(2,1)}, bf16[256,1024]{1,0:T(8,128)(2,1)S(1)}, u32[]{:S(2)}, u32[]{:S(2)}) collective-permute-start(bf16[256,1024]{1,0:T(8,128)(2,1)} %bitcast.11), channel_id=1, source_target_pairs={{0,8},{8,0},{1,9},{9,1},{2,10},{10,2},{3,11},{11,3},{4,12},{12,4},... | collective-permute-start | bytes 1572872 | tf_op jit(solution)/shard_map/ppermute | solution.py:280
  9.3 4.8 %collective-permute-start.2 = (f32[32,128]{1,0:T(8,128)S(1)}, f32[32,128]{1,0:T(8,128)S(1)}, u32[]{:S(2)}, u32[]{:S(2)}) collective-permute-start(f32[32,128]{1,0:T(8,128)S(1)} %get-tuple-element.16), channel_id=1, source_target_pairs={{0,4},{1,5},{2,6},{3,7},{4,0},{5,1},{6,2},{7,3},{8,12},{9,13},{10,... | collective-permute-start | bytes 49160 | tf_op jit(solution)/shard_map/ppermute | solution.py:275
  9.7 19.8 %collective-permute-start.7 = (bf16[32,1024]{1,0:T(8,128)(2,1)}, bf16[32,1024]{1,0:T(8,128)(2,1)}, u32[]{:S(2)}, u32[]{:S(2)}) collective-permute-start(bf16[32,1024]{1,0:T(8,128)(2,1)} %collective-permute-done.6.rest_2_), channel_id=1, source_target_pairs={{0,1},{1,0},{2,3},{3,2},{4,5},{5,4},{6,7},{7,6},{8,9},{9,8},{10,11... | collective-permute-start | bytes 196616 | tf_op jit(solution)/shard_map/ppermute | solution.py:275
  14.1 6.6 %copy-start.4 = (f32[32,128]{1,0:T(8,128)}, f32[32,128]{1,0:T(8,128)S(1)}, u32[]{:S(2)}) copy-start(f32[32,128]{1,0:T(8,128)S(1)} %get-tuple-element.28) | copy-start | bytes 49156
  14.1 4.4 %collective-permute-start.3 = (bf16[32,1152]{1,0:T(8,128)(2,1)S(1)}, bf16[32,1152]{1,0:T(8,128)(2,1)S(1)}, u32[]{:S(2)}, u32[]{:S(2)}) collective-permute-start(bf16[32,1152]{1,0:T(8,128)(2,1)S(1)} %pad_maximum_fusion.1), channel_id=1, source_target_pairs={{0,2},{1,3},{2,0},{3,1},{4,6},{5,7},{6,4},{7,5},{8,10},{9,11},{10,... | collective-permute-start | bytes 221192 | tf_op jit(solution)/shard_map/ppermute | solution.py:275
  15.2 14.3 %collective-permute-start.5 = (bf16[64,1024]{1,0:T(8,128)(2,1)}, bf16[64,1024]{1,0:T(8,128)(2,1)S(1)}, u32[]{:S(2)}, u32[]{:S(2)}) collective-permute-start(bf16[64,1024]{1,0:T(8,128)(2,1)} %pad_maximum_fusion), channel_id=1, source_target_pairs={{0,1},{1,0},{2,3},{3,2},{4,5},{5,4},{6,7},{7,6},{8,9},{9,8},{10,11... | collective-permute-start | bytes 393224 | tf_op jit(solution)/shard_map/ppermute | solution.py:275
  19.2 13.5 %collective-permute-start.4 = (bf16[32,1152]{1,0:T(8,128)(2,1)}, bf16[32,1152]{1,0:T(8,128)(2,1)}, u32[]{:S(2)}, u32[]{:S(2)}) collective-permute-start(bf16[32,1152]{1,0:T(8,128)(2,1)} %pad_maximum_fusion.2), channel_id=1, source_target_pairs={{0,1},{1,0},{2,3},{3,2},{4,5},{5,4},{6,7},{7,6},{8,9},{9,8},{10,11... | collective-permute-start | bytes 221192 | tf_op jit(solution)/shard_map/ppermute | solution.py:275
  21.5 5.8 %copy-start = (bf16[8192,1024]{1,0:T(8,128)(2,1)S(1)}, bf16[8192,1024]{1,0:T(8,128)(2,1)}, u32[]{:S(2)}) copy-start(bf16[8192,1024]{1,0:T(8,128)(2,1)} %refs_2_.1) | copy-start | bytes 50331652
  27.2 7.0 %slice-start = ((s8[16777216]{0:T(1024)(128)(4,1)}), s8[4194304]{0:T(1024)(128)(4,1)S(1)}, s32[]{:S(2)}) async-start(s8[16777216]{0:T(1024)(128)(4,1)} %bitcast.5), calls=%async_computation | async-start | bytes 8388608
  27.2 7.0 %slice-start.1 = ((s8[16777216]{0:T(1024)(128)(4,1)}), s8[4194304]{0:T(1024)(128)(4,1)S(1)}, s32[]{:S(2)}) async-start(s8[16777216]{0:T(1024)(128)(4,1)} %bitcast.5), calls=%async_computation.1 | async-start | bytes 8388608
  27.2 7.0 %slice-start.2 = ((s8[16777216]{0:T(1024)(128)(4,1)}), s8[4194304]{0:T(1024)(128)(4,1)S(1)}, s32[]{:S(2)}) async-start(s8[16777216]{0:T(1024)(128)(4,1)} %bitcast.5), calls=%async_computation.2 | async-start | bytes 8388608
  27.2 7.0 %slice-start.4 = ((s8[16777216]{0:T(1024)(128)(4,1)}), s8[4194304]{0:T(1024)(128)(4,1)S(1)}, s32[]{:S(2)}) async-start(s8[16777216]{0:T(1024)(128)(4,1)} %bitcast.7), calls=%async_computation.4 | async-start | bytes 8388608
  27.2 7.1 %slice-start.5 = ((s8[16777216]{0:T(1024)(128)(4,1)}), s8[4194304]{0:T(1024)(128)(4,1)S(1)}, s32[]{:S(2)}) async-start(s8[16777216]{0:T(1024)(128)(4,1)} %bitcast.7), calls=%async_computation.5 | async-start | bytes 8388608
  27.3 8.3 %slice-start.6 = ((s8[16777216]{0:T(1024)(128)(4,1)}), s8[4194304]{0:T(1024)(128)(4,1)S(1)}, s32[]{:S(2)}) async-start(s8[16777216]{0:T(1024)(128)(4,1)} %bitcast.7), calls=%async_computation.6 | async-start | bytes 8388608
  29.4 3.3 %copy-start.5 = (f32[32,128]{1,0:T(8,128)S(1)}, f32[32,128]{1,0:T(8,128)}, u32[]{:S(2)}) copy-start(f32[32,128]{1,0:T(8,128)} %copy-done.4) | copy-start | bytes 49156
  29.4 7.5 %slice-start.3 = ((s8[16777216]{0:T(1024)(128)(4,1)}), s8[4194304]{0:T(1024)(128)(4,1)S(1)}, s32[]{:S(2)}) async-start(s8[16777216]{0:T(1024)(128)(4,1)} %bitcast.5), calls=%async_computation.3 | async-start | bytes 8388608
  29.5 8.7 %slice-start.7 = ((s8[16777216]{0:T(1024)(128)(4,1)}), s8[4194304]{0:T(1024)(128)(4,1)S(1)}, s32[]{:S(2)}) async-start(s8[16777216]{0:T(1024)(128)(4,1)} %bitcast.7), calls=%async_computation.7 | async-start | bytes 8388608
  29.5 8.7 %copy-start.1 = (bf16[4,64,1024]{2,1,0:T(8,128)(2,1)S(1)}, bf16[4,64,1024]{2,1,0:T(8,128)(2,1)}, u32[]{:S(2)}) copy-start(bf16[4,64,1024]{2,1,0:T(8,128)(2,1)} %param.18) | copy-start | bytes 1572868
  29.5 8.9 %copy-start.2 = (bf16[4,64,1024]{2,1,0:T(8,128)(2,1)S(1)}, bf16[4,64,1024]{2,1,0:T(8,128)(2,1)}, u32[]{:S(2)}) copy-start(bf16[4,64,1024]{2,1,0:T(8,128)(2,1)} %param.19) | copy-start | bytes 1572868
  41.9 4.9 %copy-start.3 = (bf16[4,64,1024]{2,1,0:T(8,128)(2,1)S(1)}, bf16[4,64,1024]{2,1,0:T(8,128)(2,1)}, u32[]{:S(2)}) copy-start(bf16[4,64,1024]{2,1,0:T(8,128)(2,1)} %param.20) | copy-start | bytes 1572868
  42.0 4.4 %collective-permute-start.11 = (bf16[32,1152]{1,0:T(8,128)(2,1)S(1)}, bf16[32,1152]{1,0:T(8,128)(2,1)S(1)}, u32[]{:S(2)}, u32[]{:S(2)}) collective-permute-start(bf16[32,1152]{1,0:T(8,128)(2,1)S(1)} %get-tuple-element.19), channel_id=1, source_target_pairs={{0,1},{1,0},{2,3},{3,2},{4,5},{5,4},{6,7},{7,6},{8,9},{9,8},{10,11... | collective-permute-start | bytes 221192 | tf_op jit(solution)/shard_map/ppermute | solution.py:275
  44.1 5.3 %collective-permute-start.13 = (bf16[64,1024]{1,0:T(8,128)(2,1)S(1)}, bf16[64,1024]{1,0:T(8,128)(2,1)S(1)}, u32[]{:S(2)}, u32[]{:S(2)}) collective-permute-start(bf16[64,1024]{1,0:T(8,128)(2,1)S(1)} %get-tuple-element.23), channel_id=1, source_target_pairs={{0,1},{1,0},{2,3},{3,2},{4,5},{5,4},{6,7},{7,6},{8,9},{9,8},{10,11... | collective-permute-start | bytes 393224 | tf_op jit(solution)/shard_map/ppermute | solution.py:275
  46.4 4.4 %collective-permute-start.12 = (bf16[32,1152]{1,0:T(8,128)(2,1)S(1)}, bf16[32,1152]{1,0:T(8,128)(2,1)S(1)}, u32[]{:S(2)}, u32[]{:S(2)}) collective-permute-start(bf16[32,1152]{1,0:T(8,128)(2,1)S(1)} %pad_maximum_fusion.3), channel_id=1, source_target_pairs={{0,2},{1,3},{2,0},{3,1},{4,6},{5,7},{6,4},{7,5},{8,10},{9,11},{10,... | collective-permute-start | bytes 221192 | tf_op jit(solution)/shard_map/ppermute | solution.py:275
  46.9 5.6 %collective-permute-start.10 = (bf16[256,1024]{1,0:T(8,128)(2,1)S(1)}, bf16[256,1024]{1,0:T(8,128)(2,1)S(1)}, u32[]{:S(2)}, u32[]{:S(2)}) collective-permute-start(bf16[256,1024]{1,0:T(8,128)(2,1)S(1)} %bitcast.13), channel_id=1, source_target_pairs={{0,8},{8,0},{1,9},{9,1},{2,10},{10,2},{3,11},{11,3},{4,12},{12,4},... | collective-permute-start | bytes 1572872 | tf_op jit(solution)/shard_map/ppermute | solution.py:280
  48.1 4.5 %collective-permute-start.15 = (bf16[32,1024]{1,0:T(8,128)(2,1)S(1)}, bf16[32,1024]{1,0:T(8,128)(2,1)S(1)}, u32[]{:S(2)}, u32[]{:S(2)}) collective-permute-start(bf16[32,1024]{1,0:T(8,128)(2,1)S(1)} %get-tuple-element.25), channel_id=1, source_target_pairs={{0,1},{1,0},{2,3},{3,2},{4,5},{5,4},{6,7},{7,6},{8,9},{9,8},{10,11... | collective-permute-start | bytes 196616 | tf_op jit(solution)/shard_map/ppermute | solution.py:275
  50.9 6.0 %collective-permute-start.14 = (bf16[32,1152]{1,0:T(8,128)(2,1)S(1)}, bf16[32,1152]{1,0:T(8,128)(2,1)S(1)}, u32[]{:S(2)}, u32[]{:S(2)}) collective-permute-start(bf16[32,1152]{1,0:T(8,128)(2,1)S(1)} %pad_maximum_fusion.4), channel_id=1, source_target_pairs={{0,4},{1,5},{2,6},{3,7},{4,0},{5,1},{6,2},{7,3},{8,12},{9,13},{10,... | collective-permute-start | bytes 221192 | tf_op jit(solution)/shard_map/ppermute | solution.py:275
  51.4 4.6 %collective-permute-start.16 = (bf16[32,1024]{1,0:T(8,128)(2,1)S(1)}, bf16[32,1024]{1,0:T(8,128)(2,1)S(1)}, u32[]{:S(2)}, u32[]{:S(2)}) collective-permute-start(bf16[32,1024]{1,0:T(8,128)(2,1)S(1)} %add_convert_fusion), channel_id=1, source_target_pairs={{0,2},{1,3},{2,0},{3,1},{4,6},{5,7},{6,4},{7,5},{8,10},{9,11},{10,... | collective-permute-start | bytes 196616 | tf_op jit(solution)/shard_map/ppermute | solution.py:275

commit v6 on v5

--- a/solution.py
+++ b/solution.py
@@ -110,18 +110,26 @@
     )(tensor_at, in_hbm(weight))
 
 
-def dense_kernel(shards, ks, spans, given, first, tensor_ref, weight, *rest):
+def dense_kernel(shards, ks, spans, given, first, kv, tensor_ref, weight, *rest):
     arrays, rest = rest[:given], rest[given:]
-    out_ref = rest[-1]
+    copies = []
+    if kv:
+        keys, values, out_ref, k_out, v_out, sems = rest[-6:]
+        at = pl.ds(tensor_ref[0] * kv[0] // kv[1], kv[2])
+        copies = load_all([(keys.at[:, at], k_out), (values.at[:, at], v_out)], sems)
+    else:
+        out_ref = rest[-1]
     rows, width = out_ref.shape[0], weight.shape[0] // shards
     total = 0.0 if first else rest[0][...]
     for k, (i, r) in zip(ks, spans):
         at = pl.multiple_of((tensor_ref[0] ^ k) * width, width)
         total = total + dot(arrays[i][r : r + rows, :width], weight[pl.ds(at, width), :])
     out_ref[...] = total
-
-
-def dense_call(shards, where, ks, tensor_at, weight, before, rows, hints):
+    for c in copies:
+        c.wait()
+
+
+def dense_call(shards, where, ks, tensor_at, weight, before, rows, hints, kv, caches):
     wide = weight.shape[1]
     arrays, spans = [], []
     for k in ks:
@@ -131,40 +139,33 @@
         spans.append(([a is array for a in arrays].index(True), r))
     extra = [] if before is None else [before]
     return pl.pallas_call(
-        functools.partial(dense_kernel, shards, ks, spans, len(arrays), before is None),
-        in_specs=[SMEM, VMEM] + [VMEM] * (len(arrays) + len(extra)) + [HBM] * len(hints),
-        out_specs=VMEM,
-        out_shape=jax.ShapeDtypeStruct((rows, wide), jnp.float32),
+        functools.partial(dense_kernel, shards, ks, spans, len(arrays), before is None, kv),
+        in_specs=[SMEM, VMEM] + [VMEM] * (len(arrays) + len(extra)) + [HBM] * (len(hints) + len(caches)),
+        out_specs=[VMEM] * (1 + len(caches)),
+        out_shape=[jax.ShapeDtypeStruct((rows, wide), jnp.float32)]
+        + [jax.ShapeDtypeStruct((c.shape[0], kv[2]) + c.shape[2:], c.dtype) for c in caches],
+        scratch_shapes=[pltpu.SemaphoreType.DMA((len(caches),))] * bool(caches),
         **params((2 * len(ks) * rows * weight.size // shards, 10**6), 6 << 20),
-    )(tensor_at, weight, *arrays, *extra, *[in_hbm(h) for h in hints])
+    )(tensor_at, weight, *arrays, *extra, *[in_hbm(h) for h in hints], *[in_hbm(c) for c in caches])
 
 
 def mix_kernel(sizes, *refs):
-    k_in, k_outs, maps, kv_count, group, head, local_heads, group_all, width = sizes
+    k_in, k_outs, maps, kv_count, group, head, _, _, width = sizes
     refs = list(refs)
     tensor_ref, chunk, w_in, w_out, before, low, picks = [refs.pop(0) for _ in range(7)]
     ups = [refs.pop(0) for _ in range(maps)]
     downs = [refs.pop(0) for _ in range(maps)]
-    keys, values, live = [refs.pop(0) for _ in range(3)]
+    k_buf, v_buf, live = [refs.pop(0) for _ in range(3)]
     low_out, mixed_out, block_out = [refs.pop(0) for _ in range(3)]
     more_outs = [refs.pop(0) for _ in k_outs[1:]]
-    k_buf, v_buf, up_buf, down_buf, sems = refs
 
     tensor_at = tensor_ref[0]
-    kv = pl.ds(tensor_at * local_heads // group_all, kv_count)
-    up_copies = load_all([(u, up_buf.at[i]) for i, u in enumerate(ups)], sems.at[0])
-    kv_copies = load_all([(keys.at[:, kv], k_buf), (values.at[:, kv], v_buf)], sems.at[1])
-    down_copies = load_all([(d, down_buf.at[i]) for i, d in enumerate(downs)], sems.at[2])
 
     rows = before.shape[0]
     picked = picks[...]
-    for c in up_copies:
-        c.wait()
-    total = before[...] + 0.5 * lora_of(low[...], [up_buf.at[i] for i in range(maps)], picked)
+    total = before[...] + 0.5 * lora_of(low[...], ups, picked)
     at = pl.multiple_of((tensor_at ^ k_in) * width, width)
     total = total + dot(chunk[:, :width], w_in[pl.ds(at, width), :])
-    for c in kv_copies:
-        c.wait()
     length = k_buf.shape[2]
     bands = []
     for r in range(0, rows, BAND):
@@ -185,9 +186,7 @@
         bands.append(jnp.concatenate(heads, axis=1))
     mixed = jnp.concatenate(bands, axis=0).astype(jnp.bfloat16)
     mixed_out[...] = mixed
-    for c in down_copies:
-        c.wait()
-    low_part = low_of(mixed, [down_buf.at[i] for i in range(maps)], picked)
+    low_part = low_of(mixed, downs, picked)
     low_out[...] = low_part
     wide = block_out.shape[1] - LANES
     block_out[:, wide:] = low_part.astype(block_out.dtype)
@@ -333,15 +332,19 @@
     first = [k for k in where if not k & 1 and k != last ^ 1]
     second = [last ^ 1] + [k for k in where if k & 1 and k != last]
     begin_call(tensor_at, w_query)
-    query = None
-    for ks, hints in ((first, [output_weight]), (second, [])):
-        query = dense_call(shards, where, ks, tensor_at, w_query, query, rows, hints)
-
     wide = w_query.shape[1]
     local_heads = wide // head
     group_all = HEADS // KVS
     kv_count = max(1, local_heads // group_all)
     group = local_heads // kv_count
+    kv = (local_heads, group_all, kv_count)
+    (query,) = dense_call(
+        shards, where, first, tensor_at, w_query, None, rows, [output_weight], None, []
+    )
+    query, near_keys, near_values = dense_call(
+        shards, where, second, tensor_at, w_query, query, rows, [], kv, [keys, values]
+    )
+
     out_width = output_weight.shape[1] // shards
     depth = output_weight.shape[0]
     whole = shards - 1
@@ -351,7 +354,7 @@
     map_in, map_out = (stored * rank, wide), (stored * rank, depth)
     low2, mixed, payload, *blocks = pl.pallas_call(
         functools.partial(mix_kernel, sizes),
-        in_specs=[SMEM, VMEM, VMEM, VMEM, VMEM, VMEM, VMEM] + [HBM] * (2 * replicas) + [HBM, HBM, VMEM],
+        in_specs=[SMEM, VMEM, VMEM, VMEM, VMEM, VMEM, VMEM] + [VMEM] * (2 * replicas) + [VMEM, VMEM, VMEM],
         out_specs=[VMEM] * (2 + len(k_outs)),
         out_shape=[
             jax.ShapeDtypeStruct((rows, LANES), jnp.float32),
@@ -360,8 +363,6 @@
         ]
         + [jax.ShapeDtypeStruct((rows, out_width), jnp.float32)] * (len(k_outs) - 1),
         scratch_shapes=[
-            pltpu.VMEM((rows, kv_count, length, head), keys.dtype),
-            pltpu.VMEM((rows, kv_count, length, head), values.dtype),
             pltpu.VMEM((replicas,) + map_in, keys.dtype),
             pltpu.VMEM((replicas,) + map_out, keys.dtype),
             pltpu.SemaphoreType.DMA((3, max(2, replicas))),
@@ -378,8 +379,8 @@
         picks,
         *query_up,
         *output_down,
-        in_hbm(keys),
-        in_hbm(values),
+        near_keys,
+        near_values,
         live,
     )
 

time: 58.1 us -> 57.8 us (level)
  local copies, waits for them, and re-layouts: 9.97 us -> 8.37 us
  Pallas kernels: 14.6 us -> 16 us
    pallas_call x2, Pallas kernels: 5.34 us -> 7.07 us  [dense_call(): pl.pallas_call(functools.partial(dense_kernel, shards, ks, spans, len(arr...]
    unnamed x28, local copies, waits for them, and re-layouts: 9.89 us -> 8.28 us
  transfers between devices with their start and end apart: 17 -> 17, of which waited for: 8 -> 8; matrix products, arithmetic and copies ran while one was open for 8% -> 8% of each run, Pallas kernels for 17% -> 21%
where the time goes in v6:
time: 57.8 us; the launch traced here: 57.6 us
  starting transfers between devices  16.4 us (28%)
  Pallas kernels  16 us (28%)
  waiting for transfers between devices  11.9 us (21%)
  local copies, waits for them, and re-layouts  8.37 us (14%)
  other arithmetic  4.56 us (8%)
    ppermute x13, starting transfers between devices, across(): return lax.ppermute(x, 'tensor', [(i, i ^ bit) for i in range(shards)])  15.9 us
    ppermute x13, waiting for transfers between devices, across(): return lax.ppermute(x, 'tensor', [(i, i ^ bit) for i in range(shards)])  11.3 us
    unnamed x28, local copies, waits for them, and re-layouts  8.28 us
    pallas_call x2, Pallas kernels, dense_call(): pl.pallas_call(functools.partial(dense_kernel, shards, ks, spans, len(arr...  7.07 us
    pallas_call x1, Pallas kernels, per_device(): pl.pallas_call(functools.partial(mix_kernel, sizes), in_specs=[SMEM, VMEM...  3.19 us
    pallas_call x2, Pallas kernels, resident_call(): pl.pallas_call(functools.partial(resident_kernel, ks, spans), in_specs=[S...  2.73 us
    add x1, other arithmetic, per_device(): low = low + got[:, width:].astype(jnp.float32)  1.53 us
    pallas_call x1, Pallas kernels, low_call(): pl.pallas_call(functools.partial(low_kernel, len(downs), len(hints)), in_...  1.53 us
  transfers between devices with their start and end apart: 17, of which 8 were waited for; matrix products, arithmetic and copies ran while one was open for 8% of the time, Pallas kernels for 21%

profile of v6, /device:TPU:0, one launch (start us, length us, event | category | flops | bytes accessed | tf_op | source)
XLA Modules:
  0.0 57.6 jit_solution(8084799475772674559)
XLA Ops:
  0.0 4.1 %collective-permute-start = (bf16[32,1024]{1,0:T(8,128)(2,1)}, bf16[32,1024]{1,0:T(8,128)(2,1)S(1)}, u32[]{:S(2)}, u32[]{:S(2)}) collective-permute-start(bf16[32,1024]{1,0:T(8,128)(2,1)} %x_hbm.1), channel_id=1, source_target_pairs={{0,4},{1,5},{2,6},{3,7},{4,0},{5,1},{6,2},{7,3},{8,12},{9,13},{10,... | collective-permute-start | bytes 196616 | tf_op jit(solution)/shard_map/ppermute | solution.py:274
  4.1 1.6 %collective-permute-start.6 = (bf16[32,1024]{1,0:T(8,128)(2,1)}, bf16[32,1024]{1,0:T(8,128)(2,1)}, u32[]{:S(2)}, u32[]{:S(2)}) collective-permute-start(bf16[32,1024]{1,0:T(8,128)(2,1)} %x_hbm.1), channel_id=1, source_target_pairs={{0,2},{1,3},{2,0},{3,1},{4,6},{5,7},{6,4},{7,5},{8,10},{9,11},{10,... | collective-permute-start | bytes 196616 | tf_op jit(solution)/shard_map/ppermute | solution.py:274
  5.6 0.0 collective-permute-start.1
  5.6 0.5 collective-permute-start.8
  6.2 0.0 collective-permute-start.9
  6.2 0.8 %select_reduce_fusion = s32[64]{0:T(128)S(1)} fusion(s32[8]{0:T(128)} %param.22, s32[64]{0:T(128)} %param.21), kind=kLoop, calls=%fused_computation.30 | loop fusion | flops 1472 | bytes 544 | tf_op jit(solution)/shard_map/reduce_sum | solution.py:284
  7.0 0.1 dynamic_slice.3
  7.0 0.1 broadcast_compare_fusion.1
  7.1 0.6 %collective-permute-done.1.rest_1_ = bf16[256,1024]{1,0:T(8,128)(2,1)S(1)} collective-permute-done((bf16[256,1024]{1,0:T(8,128)(2,1)}, bf16[256,1024]{1,0:T(8,128)(2,1)S(1)}, u32[]{:S(2)}, u32[]{:S(2)}) %collective-permute-start.1) | collective-permute-done | bytes 524320 | tf_op jit(solution)/shard_map/ppermute | solution.py:279
  7.8 1.5 %low.1 = (f32[32,128]{1,0:T(8,128)S(1)}, bf16[32,1024]{1,0:T(8,128)(2,1)S(1)}) custom-call(bf16[32,1024]{1,0:T(8,128)(2,1)} %x_hbm.1, f32[32,512]{1,0:T(8,128)S(1)} %add_convert_fusion.3.picks_ref.refs_6_, bf16[256,1024]{1,0:T(8,128)(2,1)} %bitcast.16, bf16[256,1024]{1,0:T(8,128)(2,1)S(1)} %collective-permute-done.1.rest_1_), custom_call_target="tpu_custom_call" | custom-call | flops 100000000 | bytes 1000000 | tf_op jit(solution)/shard_map/low/pallas_call | solution.py:82
  9.3 0.4 collective-permute-start.2
  9.7 0.0 collective-permute-done.6.rest_2_
  9.7 1.5 %collective-permute-start.7 = (bf16[32,1024]{1,0:T(8,128)(2,1)}, bf16[32,1024]{1,0:T(8,128)(2,1)}, u32[]{:S(2)}, u32[]{:S(2)}) collective-permute-start(bf16[32,1024]{1,0:T(8,128)(2,1)} %collective-permute-done.6.rest_2_), channel_id=1, source_target_pairs={{0,1},{1,0},{2,3},{3,2},{4,5},{5,4},{6,7},{7,6},{8,9},{9,8},{10,11... | collective-permute-start | bytes 196616 | tf_op jit(solution)/shard_map/ppermute | solution.py:274
  11.2 2.8 %collective-permute-done.2 = f32[32,128]{1,0:T(8,128)S(1)} collective-permute-done((f32[32,128]{1,0:T(8,128)S(1)}, f32[32,128]{1,0:T(8,128)S(1)}, u32[]{:S(2)}, u32[]{:S(2)}) %collective-permute-start.2) | collective-permute-done | bytes 16416 | tf_op jit(solution)/shard_map/ppermute | solution.py:274
  14.1 0.0 collective-permute-done.rest_1_
  14.1 0.5 collective-permute-start.3
  14.6 0.7 %pad_maximum_fusion = bf16[64,1024]{1,0:T(8,128)(2,1)} fusion(bf16[32,1024]{1,0:T(8,128)(2,1)S(1)} %collective-permute-done.rest_1_, bf16[32,1024]{1,0:T(8,128)(2,1)S(1)} %get-tuple-element.20.rest_0_), kind=kLoop, calls=%fused_computation | loop fusion | flops 262144 | bytes 262144 | tf_op jit(solution)/shard_map/concatenate | solution.py:322
  15.2 1.5 %collective-permute-start.5 = (bf16[64,1024]{1,0:T(8,128)(2,1)}, bf16[64,1024]{1,0:T(8,128)(2,1)S(1)}, u32[]{:S(2)}, u32[]{:S(2)}) collective-permute-start(bf16[64,1024]{1,0:T(8,128)(2,1)} %pad_maximum_fusion), channel_id=1, source_target_pairs={{0,1},{1,0},{2,3},{3,2},{4,5},{5,4},{6,7},{7,6},{8,9},{9,8},{10,11... | collective-permute-start | bytes 393224 | tf_op jit(solution)/shard_map/ppermute | solution.py:274
  16.8 1.8 %collective-permute-done.3.rest_0_ = bf16[32,1152]{1,0:T(8,128)(2,1)S(1)} collective-permute-done((bf16[32,1152]{1,0:T(8,128)(2,1)S(1)}, bf16[32,1152]{1,0:T(8,128)(2,1)S(1)}, u32[]{:S(2)}, u32[]{:S(2)}) %collective-permute-start.3) | collective-permute-done | bytes 73760 | tf_op jit(solution)/shard_map/ppermute | solution.py:274
  18.5 0.6 %pad_maximum_fusion.2 = bf16[32,1152]{1,0:T(8,128)(2,1)} fusion(bf16[32,128]{1,0:T(8,128)(2,1)S(1)} %fusion.2, bf16[32,1024]{1,0:T(8,128)(2,1)S(1)} %slice.37), kind=kLoop, calls=%fused_computation.9 | loop fusion | flops 147456 | bytes 147456 | tf_op jit(solution)/shard_map/concatenate | solution.py:312
  19.2 1.5 %collective-permute-start.4 = (bf16[32,1152]{1,0:T(8,128)(2,1)}, bf16[32,1152]{1,0:T(8,128)(2,1)}, u32[]{:S(2)}, u32[]{:S(2)}) collective-permute-start(bf16[32,1152]{1,0:T(8,128)(2,1)} %pad_maximum_fusion.2), channel_id=1, source_target_pairs={{0,1},{1,0},{2,3},{3,2},{4,5},{5,4},{6,7},{7,6},{8,9},{9,8},{10,11... | collective-permute-start | bytes 221192 | tf_op jit(solution)/shard_map/ppermute | solution.py:274
  20.7 0.0 copy-done.4
  20.7 0.7 %fusion.1.refs_13_ = f32[32,1024]{1,0:T(8,128)S(1)} fusion(s32[32]{0:T(128)} %param.23, s32[1024]{0:T(1024)S(1)} %get-tuple-element.40, s32[1024]{0:T(1024)S(1)} %get-tuple-element.41, s32[32]{0:T(128)S(1)} %get-tuple-element.45, s32[32]{0:T(128)S(1)} %get-tuple-element.46, s32[1024]{0:T(1024)S(1)} %get-tuple-element.39, s32[1024]{0:T(1024)S(1)} %get-tuple-element.42, ...), kind=kLoop, calls=%fused_computation.7 | loop fusion | flops 229376 | bytes 149920 | tf_op jit(solution)/shard_map/convert_element_type | solution.py:297
  21.5 0.0 copy-start
  21.5 5.8 %copy-done = bf16[8192,1024]{1,0:T(8,128)(2,1)S(1)} copy-done((bf16[8192,1024]{1,0:T(8,128)(2,1)S(1)}, bf16[8192,1024]{1,0:T(8,128)(2,1)}, u32[]{:S(2)}) %copy-start) | copy-done | bytes 16777240
  27.2 0.0 slice-start.5
  27.2 0.0 slice-start.6
  27.3 2.2 %shard_map.118.rest_3_ = f32[32,1024]{1,0:T(8,128)S(1)} custom-call(s32[1]{0:T(128)} %bitcast.tensor_ref.refs_0_, bf16[8192,1024]{1,0:T(8,128)(2,1)S(1)} %copy-done, bf16[32,1024]{1,0:T(8,128)(2,1)S(1)} %get-tuple-element.20.rest_0_, bf16[32,1024]{1,0:T(8,128)(2,1)S(1)} %collective-permute-done.rest_1_, bf16[32,1024]{1,0:T(8,128)(2,1)} %collective-permute-done.6.rest_2_, ...), custom_call_target="tpu_custom_call" | custom-call | flops 201326592 | bytes 1000000 | tf_op jit(solution)/shard_map/pallas_call | solution.py:141
  29.4 0.0 slice-start.3
  29.5 0.0 slice-start.7
  29.5 0.0 copy-start.1
  29.5 0.0 copy-start.2
  29.5 0.0 collective-permute-done.7.rest_2_
  29.5 0.0 collective-permute-done.5.rest_1_
  29.5 4.9 %shard_map.119 = (f32[32,1024]{1,0:T(8,128)S(1)}, bf16[32,1,32,128]{3,2,1,0:T(8,128)(2,1)S(1)}, bf16[32,1,32,128]{3,2,1,0:T(8,128)(2,1)S(1)}) custom-call(s32[1]{0:T(128)} %bitcast.tensor_ref.refs_0_, bf16[8192,1024]{1,0:T(8,128)(2,1)S(1)} %copy-done, bf16[32,1152]{1,0:T(8,128)(2,1)S(1)} %collective-permute-done.3.rest_0_, ...), custom_call_target="tpu_custom_call" | custom-call | flops 268435456 | bytes 1000000 | tf_op jit(solution)/shard_map/pallas_call | solution.py:141
  34.4 0.0 collective-permute-done.4.refs_1_
  34.4 0.0 copy-done.5
  34.4 1.5 %convert_add_fusion.1.refs_5_ = f32[32,128]{1,0:T(8,128)S(1)} fusion(f32[32,128]{1,0:T(8,128)S(1)} %copy-done.5, bf16[32,1152]{1,0:T(8,128)(2,1)} %collective-permute-done.4.refs_1_, bf16[32,1152]{1,0:T(8,128)(2,1)S(1)} %collective-permute-done.3.rest_0_), kind=kLoop, calls=%fused_computation.15 | loop fusion | flops 16384 | bytes 49152 | tf_op jit(solution)/shard_map/add | solution.py:315
  36.0 0.0 collective-permute-done.8.refs_8_
  36.0 0.0 collective-permute-done.9.refs_10_
  36.0 1.1 %slice-done.3 = s8[4194304]{0:T(1024)(128)(4,1)S(1)} async-done(((s8[16777216]{0:T(1024)(128)(4,1)}), s8[4194304]{0:T(1024)(128)(4,1)S(1)}, s32[]{:S(2)}) %slice-start.3) | async-done | bytes 4194328
  37.1 1.2 %slice-done.7 = s8[4194304]{0:T(1024)(128)(4,1)S(1)} async-done(((s8[16777216]{0:T(1024)(128)(4,1)}), s8[4194304]{0:T(1024)(128)(4,1)S(1)}, s32[]{:S(2)}) %slice-start.7) | async-done | bytes 4194328
  38.3 0.0 copy-done.1
  38.3 0.2 copy-done.2
  38.5 3.2 %mix.1 = (f32[32,128]{1,0:T(8,128)S(1)}, bf16[32,1024]{1,0:T(8,128)(2,1)S(1)}, bf16[32,1152]{1,0:T(8,128)(2,1)S(1)}) custom-call(s32[1]{0:T(128)} %bitcast.tensor_ref.refs_0_, bf16[32,1152]{1,0:T(8,128)(2,1)} %collective-permute-done.4.refs_1_, bf16[8192,1024]{1,0:T(8,128)(2,1)S(1)} %bitcast.8, bf16[1024,8192]{1,0:T(8,128)(2,1)S(1)} %bitcast.6, ...), custom_call_target="tpu_custom_call" | custom-call | flops 1000000000 | bytes 6291456 | tf_op jit(solution)/shard_map/mix/pallas_call | solution.py:355
  41.7 0.0 copy-start.3
  41.7 0.6 collective-permute-start.11
  42.3 1.5 %shard_map.120 = (f32[32,1024]{1,0:T(8,128)S(1)}, bf16[64,1024]{1,0:T(8,128)(2,1)S(1)}, bf16[32,1024]{1,0:T(8,128)(2,1)S(1)}) custom-call(s32[1]{0:T(128)} %bitcast.tensor_ref.refs_0_, bf16[32,1024]{1,0:T(8,128)(2,1)S(1)} %get-tuple-element.26.x_ref, bf16[1024,8192]{1,0:T(8,128)(2,1)S(1)} %bitcast.6), custom_call_target="tpu_custom_call" | custom-call | tf_op jit(solution)/shard_map/pallas_call | solution.py:215
  43.8 1.5 %collective-permute-start.13 = (bf16[64,1024]{1,0:T(8,128)(2,1)S(1)}, bf16[64,1024]{1,0:T(8,128)(2,1)S(1)}, u32[]{:S(2)}, u32[]{:S(2)}) collective-permute-start(bf16[64,1024]{1,0:T(8,128)(2,1)S(1)} %get-tuple-element.29), channel_id=1, source_target_pairs={{0,1},{1,0},{2,3},{3,2},{4,5},{5,4},{6,7},{7,6},{8,9},{9,8},{10,11... | collective-permute-start | bytes 393224 | tf_op jit(solution)/shard_map/ppermute | solution.py:274
  45.4 0.8 %collective-permute-done.11.rest_2_ = bf16[32,1152]{1,0:T(8,128)(2,1)S(1)} collective-permute-done((bf16[32,1152]{1,0:T(8,128)(2,1)S(1)}, bf16[32,1152]{1,0:T(8,128)(2,1)S(1)}, u32[]{:S(2)}, u32[]{:S(2)}) %collective-permute-start.11) | collective-permute-done | bytes 73760 | tf_op jit(solution)/shard_map/ppermute | solution.py:274
  46.2 0.5 collective-permute-start.12
  46.6 0.0 collective-permute-start.10
  46.6 1.2 %shard_map.121 = (f32[32,1024]{1,0:T(8,128)S(1)}, f32[32,1024]{1,0:T(8,128)S(1)}, f32[32,1024]{1,0:T(8,128)S(1)}) custom-call(s32[1]{0:T(128)} %bitcast.tensor_ref.refs_0_, bf16[32,1024]{1,0:T(8,128)(2,1)S(1)} %get-tuple-element.26.x_ref, bf16[1024,8192]{1,0:T(8,128)(2,1)S(1)} %bitcast.6), custom_call_target="tpu_custom_call" | custom-call | tf_op jit(solution)/shard_map/pallas_call | solution.py:215
  47.8 1.3 %collective-permute-start.15 = (bf16[32,1024]{1,0:T(8,128)(2,1)S(1)}, bf16[32,1024]{1,0:T(8,128)(2,1)S(1)}, u32[]{:S(2)}, u32[]{:S(2)}) collective-permute-start(bf16[32,1024]{1,0:T(8,128)(2,1)S(1)} %get-tuple-element.31), channel_id=1, source_target_pairs={{0,1},{1,0},{2,3},{3,2},{4,5},{5,4},{6,7},{7,6},{8,9},{9,8},{10,11... | collective-permute-start | bytes 196616 | tf_op jit(solution)/shard_map/ppermute | solution.py:274
  49.1 0.0 collective-permute-done.13
  49.1 1.4 %collective-permute-done.12.rest_3_ = bf16[32,1152]{1,0:T(8,128)(2,1)S(1)} collective-permute-done((bf16[32,1152]{1,0:T(8,128)(2,1)S(1)}, bf16[32,1152]{1,0:T(8,128)(2,1)S(1)}, u32[]{:S(2)}, u32[]{:S(2)}) %collective-permute-start.12) | collective-permute-done | bytes 73760 | tf_op jit(solution)/shard_map/ppermute | solution.py:274
  50.6 0.5 collective-permute-start.14
  51.2 0.5 collective-permute-start.16
  51.7 0.5 begin.1
  52.2 0.0 collective-permute-done.10.rest_1_
  52.2 0.1 collective-permute-done.15.rest_6_
  52.3 3.5 %collective-permute-done.16.rest_7_ = bf16[32,1024]{1,0:T(8,128)(2,1)S(1)} collective-permute-done((bf16[32,1024]{1,0:T(8,128)(2,1)S(1)}, bf16[32,1024]{1,0:T(8,128)(2,1)S(1)}, u32[]{:S(2)}, u32[]{:S(2)}) %collective-permute-start.16) | collective-permute-done | bytes 65568 | tf_op jit(solution)/shard_map/ppermute | solution.py:274
  55.8 0.9 %collective-permute-done.14.rest_4_ = bf16[32,1152]{1,0:T(8,128)(2,1)S(1)} collective-permute-done((bf16[32,1152]{1,0:T(8,128)(2,1)S(1)}, bf16[32,1152]{1,0:T(8,128)(2,1)S(1)}, u32[]{:S(2)}, u32[]{:S(2)}) %collective-permute-start.14) | collective-permute-done | bytes 73760 | tf_op jit(solution)/shard_map/ppermute | solution.py:274
  56.7 0.9 %final.1 = bf16[32,1024]{1,0:T(8,128)(2,1)} custom-call(f32[32,512]{1,0:T(8,128)S(1)} %add_convert_fusion.3.picks_ref.refs_6_, f32[32,128]{1,0:T(8,128)S(1)} %get-tuple-element.24.low_ref, bf16[256,1024]{1,0:T(8,128)(2,1)S(1)} %bitcast.14, bf16[256,1024]{1,0:T(8,128)(2,1)S(1)} %collective-permute-done.10.rest_1_, ...), custom_call_target="tpu_custom_call" | custom-call | flops 100000000 | bytes 1000000 | tf_op jit(solution)/shard_map/final/pallas_call | solution.py:426
  (34 shorter events, 0.2 us)
Async XLA Ops:
  0.0 14.1 %collective-permute-start = (bf16[32,1024]{1,0:T(8,128)(2,1)}, bf16[32,1024]{1,0:T(8,128)(2,1)S(1)}, u32[]{:S(2)}, u32[]{:S(2)}) collective-permute-start(bf16[32,1024]{1,0:T(8,128)(2,1)} %x_hbm.1), channel_id=1, source_target_pairs={{0,4},{1,5},{2,6},{3,7},{4,0},{5,1},{6,2},{7,3},{8,12},{9,13},{10,... | collective-permute-start | bytes 196616 | tf_op jit(solution)/shard_map/ppermute | solution.py:274
  4.1 5.6 %collective-permute-start.6 = (bf16[32,1024]{1,0:T(8,128)(2,1)}, bf16[32,1024]{1,0:T(8,128)(2,1)}, u32[]{:S(2)}, u32[]{:S(2)}) collective-permute-start(bf16[32,1024]{1,0:T(8,128)(2,1)} %x_hbm.1), channel_id=1, source_target_pairs={{0,2},{1,3},{2,0},{3,1},{4,6},{5,7},{6,4},{7,5},{8,10},{9,11},{10,... | collective-permute-start | bytes 196616 | tf_op jit(solution)/shard_map/ppermute | solution.py:274
  5.6 2.1 %collective-permute-start.1 = (bf16[256,1024]{1,0:T(8,128)(2,1)}, bf16[256,1024]{1,0:T(8,128)(2,1)S(1)}, u32[]{:S(2)}, u32[]{:S(2)}) collective-permute-start(bf16[256,1024]{1,0:T(8,128)(2,1)} %bitcast.15), channel_id=1, source_target_pairs={{0,8},{8,0},{1,9},{9,1},{2,10},{10,2},{3,11},{11,3},{4,12},{12,4},... | collective-permute-start | bytes 1572872 | tf_op jit(solution)/shard_map/ppermute | solution.py:279
  5.6 30.3 %collective-permute-start.8 = (bf16[256,1024]{1,0:T(8,128)(2,1)}, bf16[256,1024]{1,0:T(8,128)(2,1)S(1)}, u32[]{:S(2)}, u32[]{:S(2)}) collective-permute-start(bf16[256,1024]{1,0:T(8,128)(2,1)} %bitcast.9), channel_id=1, source_target_pairs={{0,8},{8,0},{1,9},{9,1},{2,10},{10,2},{3,11},{11,3},{4,12},{12,4},... | collective-permute-start | bytes 1572872 | tf_op jit(solution)/shard_map/ppermute | solution.py:279
  6.2 29.8 %collective-permute-start.9 = (bf16[256,1024]{1,0:T(8,128)(2,1)}, bf16[256,1024]{1,0:T(8,128)(2,1)}, u32[]{:S(2)}, u32[]{:S(2)}) collective-permute-start(bf16[256,1024]{1,0:T(8,128)(2,1)} %bitcast.11), channel_id=1, source_target_pairs={{0,8},{8,0},{1,9},{9,1},{2,10},{10,2},{3,11},{11,3},{4,12},{12,4},... | collective-permute-start | bytes 1572872 | tf_op jit(solution)/shard_map/ppermute | solution.py:279
  9.3 4.8 %collective-permute-start.2 = (f32[32,128]{1,0:T(8,128)S(1)}, f32[32,128]{1,0:T(8,128)S(1)}, u32[]{:S(2)}, u32[]{:S(2)}) collective-permute-start(f32[32,128]{1,0:T(8,128)S(1)} %get-tuple-element.19), channel_id=1, source_target_pairs={{0,4},{1,5},{2,6},{3,7},{4,0},{5,1},{6,2},{7,3},{8,12},{9,13},{10,... | collective-permute-start | bytes 49160 | tf_op jit(solution)/shard_map/ppermute | solution.py:274
  9.7 19.8 %collective-permute-start.7 = (bf16[32,1024]{1,0:T(8,128)(2,1)}, bf16[32,1024]{1,0:T(8,128)(2,1)}, u32[]{:S(2)}, u32[]{:S(2)}) collective-permute-start(bf16[32,1024]{1,0:T(8,128)(2,1)} %collective-permute-done.6.rest_2_), channel_id=1, source_target_pairs={{0,1},{1,0},{2,3},{3,2},{4,5},{5,4},{6,7},{7,6},{8,9},{9,8},{10,11... | collective-permute-start | bytes 196616 | tf_op jit(solution)/shard_map/ppermute | solution.py:274
  14.1 6.6 %copy-start.4 = (f32[32,128]{1,0:T(8,128)}, f32[32,128]{1,0:T(8,128)S(1)}, u32[]{:S(2)}) copy-start(f32[32,128]{1,0:T(8,128)S(1)} %get-tuple-element.34) | copy-start | bytes 49156
  14.1 4.4 %collective-permute-start.3 = (bf16[32,1152]{1,0:T(8,128)(2,1)S(1)}, bf16[32,1152]{1,0:T(8,128)(2,1)S(1)}, u32[]{:S(2)}, u32[]{:S(2)}) collective-permute-start(bf16[32,1152]{1,0:T(8,128)(2,1)S(1)} %pad_maximum_fusion.1), channel_id=1, source_target_pairs={{0,2},{1,3},{2,0},{3,1},{4,6},{5,7},{6,4},{7,5},{8,10},{9,11},{10,... | collective-permute-start | bytes 221192 | tf_op jit(solution)/shard_map/ppermute | solution.py:274
  15.2 14.3 %collective-permute-start.5 = (bf16[64,1024]{1,0:T(8,128)(2,1)}, bf16[64,1024]{1,0:T(8,128)(2,1)S(1)}, u32[]{:S(2)}, u32[]{:S(2)}) collective-permute-start(bf16[64,1024]{1,0:T(8,128)(2,1)} %pad_maximum_fusion), channel_id=1, source_target_pairs={{0,1},{1,0},{2,3},{3,2},{4,5},{5,4},{6,7},{7,6},{8,9},{9,8},{10,11... | collective-permute-start | bytes 393224 | tf_op jit(solution)/shard_map/ppermute | solution.py:274
  19.2 15.2 %collective-permute-start.4 = (bf16[32,1152]{1,0:T(8,128)(2,1)}, bf16[32,1152]{1,0:T(8,128)(2,1)}, u32[]{:S(2)}, u32[]{:S(2)}) collective-permute-start(bf16[32,1152]{1,0:T(8,128)(2,1)} %pad_maximum_fusion.2), channel_id=1, source_target_pairs={{0,1},{1,0},{2,3},{3,2},{4,5},{5,4},{6,7},{7,6},{8,9},{9,8},{10,11... | collective-permute-start | bytes 221192 | tf_op jit(solution)/shard_map/ppermute | solution.py:274
  21.5 5.8 %copy-start = (bf16[8192,1024]{1,0:T(8,128)(2,1)S(1)}, bf16[8192,1024]{1,0:T(8,128)(2,1)}, u32[]{:S(2)}) copy-start(bf16[8192,1024]{1,0:T(8,128)(2,1)} %refs_2_.1) | copy-start | bytes 50331652
  27.2 8.8 %slice-start = ((s8[16777216]{0:T(1024)(128)(4,1)}), s8[4194304]{0:T(1024)(128)(4,1)S(1)}, s32[]{:S(2)}) async-start(s8[16777216]{0:T(1024)(128)(4,1)} %bitcast.5), calls=%async_computation | async-start | bytes 8388608
  27.2 8.8 %slice-start.1 = ((s8[16777216]{0:T(1024)(128)(4,1)}), s8[4194304]{0:T(1024)(128)(4,1)S(1)}, s32[]{:S(2)}) async-start(s8[16777216]{0:T(1024)(128)(4,1)} %bitcast.5), calls=%async_computation.1 | async-start | bytes 8388608
  27.2 8.8 %slice-start.2 = ((s8[16777216]{0:T(1024)(128)(4,1)}), s8[4194304]{0:T(1024)(128)(4,1)S(1)}, s32[]{:S(2)}) async-start(s8[16777216]{0:T(1024)(128)(4,1)} %bitcast.5), calls=%async_computation.2 | async-start | bytes 8388608
  27.2 8.8 %slice-start.4 = ((s8[16777216]{0:T(1024)(128)(4,1)}), s8[4194304]{0:T(1024)(128)(4,1)S(1)}, s32[]{:S(2)}) async-start(s8[16777216]{0:T(1024)(128)(4,1)} %bitcast.7), calls=%async_computation.4 | async-start | bytes 8388608
  27.2 8.8 %slice-start.5 = ((s8[16777216]{0:T(1024)(128)(4,1)}), s8[4194304]{0:T(1024)(128)(4,1)S(1)}, s32[]{:S(2)}) async-start(s8[16777216]{0:T(1024)(128)(4,1)} %bitcast.7), calls=%async_computation.5 | async-start | bytes 8388608
  27.2 8.8 %slice-start.6 = ((s8[16777216]{0:T(1024)(128)(4,1)}), s8[4194304]{0:T(1024)(128)(4,1)S(1)}, s32[]{:S(2)}) async-start(s8[16777216]{0:T(1024)(128)(4,1)} %bitcast.7), calls=%async_computation.6 | async-start | bytes 8388608
  29.4 5.0 %copy-start.5 = (f32[32,128]{1,0:T(8,128)S(1)}, f32[32,128]{1,0:T(8,128)}, u32[]{:S(2)}) copy-start(f32[32,128]{1,0:T(8,128)} %copy-done.4) | copy-start | bytes 49156
  29.4 7.7 %slice-start.3 = ((s8[16777216]{0:T(1024)(128)(4,1)}), s8[4194304]{0:T(1024)(128)(4,1)S(1)}, s32[]{:S(2)}) async-start(s8[16777216]{0:T(1024)(128)(4,1)} %bitcast.5), calls=%async_computation.3 | async-start | bytes 8388608
  29.5 8.9 %slice-start.7 = ((s8[16777216]{0:T(1024)(128)(4,1)}), s8[4194304]{0:T(1024)(128)(4,1)S(1)}, s32[]{:S(2)}) async-start(s8[16777216]{0:T(1024)(128)(4,1)} %bitcast.7), calls=%async_computation.7 | async-start | bytes 8388608
  29.5 8.9 %copy-start.1 = (bf16[4,64,1024]{2,1,0:T(8,128)(2,1)S(1)}, bf16[4,64,1024]{2,1,0:T(8,128)(2,1)}, u32[]{:S(2)}) copy-start(bf16[4,64,1024]{2,1,0:T(8,128)(2,1)} %param.18) | copy-start | bytes 1572868
  29.5 9.0 %copy-start.2 = (bf16[4,64,1024]{2,1,0:T(8,128)(2,1)S(1)}, bf16[4,64,1024]{2,1,0:T(8,128)(2,1)}, u32[]{:S(2)}) copy-start(bf16[4,64,1024]{2,1,0:T(8,128)(2,1)} %param.19) | copy-start | bytes 1572868
  41.7 4.9 %copy-start.3 = (bf16[4,64,1024]{2,1,0:T(8,128)(2,1)S(1)}, bf16[4,64,1024]{2,1,0:T(8,128)(2,1)}, u32[]{:S(2)}) copy-start(bf16[4,64,1024]{2,1,0:T(8,128)(2,1)} %param.20) | copy-start | bytes 1572868
  41.7 4.4 %collective-permute-start.11 = (bf16[32,1152]{1,0:T(8,128)(2,1)S(1)}, bf16[32,1152]{1,0:T(8,128)(2,1)S(1)}, u32[]{:S(2)}, u32[]{:S(2)}) collective-permute-start(bf16[32,1152]{1,0:T(8,128)(2,1)S(1)} %get-tuple-element.25), channel_id=1, source_target_pairs={{0,1},{1,0},{2,3},{3,2},{4,5},{5,4},{6,7},{7,6},{8,9},{9,8},{10,11... | collective-permute-start | bytes 221192 | tf_op jit(solution)/shard_map/ppermute | solution.py:274
  43.8 5.3 %collective-permute-start.13 = (bf16[64,1024]{1,0:T(8,128)(2,1)S(1)}, bf16[64,1024]{1,0:T(8,128)(2,1)S(1)}, u32[]{:S(2)}, u32[]{:S(2)}) collective-permute-start(bf16[64,1024]{1,0:T(8,128)(2,1)S(1)} %get-tuple-element.29), channel_id=1, source_target_pairs={{0,1},{1,0},{2,3},{3,2},{4,5},{5,4},{6,7},{7,6},{8,9},{9,8},{10,11... | collective-permute-start | bytes 393224 | tf_op jit(solution)/shard_map/ppermute | solution.py:274
  46.2 4.4 %collective-permute-start.12 = (bf16[32,1152]{1,0:T(8,128)(2,1)S(1)}, bf16[32,1152]{1,0:T(8,128)(2,1)S(1)}, u32[]{:S(2)}, u32[]{:S(2)}) collective-permute-start(bf16[32,1152]{1,0:T(8,128)(2,1)S(1)} %pad_maximum_fusion.3), channel_id=1, source_target_pairs={{0,2},{1,3},{2,0},{3,1},{4,6},{5,7},{6,4},{7,5},{8,10},{9,11},{10,... | collective-permute-start | bytes 221192 | tf_op jit(solution)/shard_map/ppermute | solution.py:274
  46.6 5.6 %collective-permute-start.10 = (bf16[256,1024]{1,0:T(8,128)(2,1)S(1)}, bf16[256,1024]{1,0:T(8,128)(2,1)S(1)}, u32[]{:S(2)}, u32[]{:S(2)}) collective-permute-start(bf16[256,1024]{1,0:T(8,128)(2,1)S(1)} %bitcast.13), channel_id=1, source_target_pairs={{0,8},{8,0},{1,9},{9,1},{2,10},{10,2},{3,11},{11,3},{4,12},{12,4},... | collective-permute-start | bytes 1572872 | tf_op jit(solution)/shard_map/ppermute | solution.py:279
  47.8 4.5 %collective-permute-start.15 = (bf16[32,1024]{1,0:T(8,128)(2,1)S(1)}, bf16[32,1024]{1,0:T(8,128)(2,1)S(1)}, u32[]{:S(2)}, u32[]{:S(2)}) collective-permute-start(bf16[32,1024]{1,0:T(8,128)(2,1)S(1)} %get-tuple-element.31), channel_id=1, source_target_pairs={{0,1},{1,0},{2,3},{3,2},{4,5},{5,4},{6,7},{7,6},{8,9},{9,8},{10,11... | collective-permute-start | bytes 196616 | tf_op jit(solution)/shard_map/ppermute | solution.py:274
  50.6 6.0 %collective-permute-start.14 = (bf16[32,1152]{1,0:T(8,128)(2,1)S(1)}, bf16[32,1152]{1,0:T(8,128)(2,1)S(1)}, u32[]{:S(2)}, u32[]{:S(2)}) collective-permute-start(bf16[32,1152]{1,0:T(8,128)(2,1)S(1)} %pad_maximum_fusion.4), channel_id=1, source_target_pairs={{0,4},{1,5},{2,6},{3,7},{4,0},{5,1},{6,2},{7,3},{8,12},{9,13},{10,... | collective-permute-start | bytes 221192 | tf_op jit(solution)/shard_map/ppermute | solution.py:274
  51.2 4.6 %collective-permute-start.16 = (bf16[32,1024]{1,0:T(8,128)(2,1)S(1)}, bf16[32,1024]{1,0:T(8,128)(2,1)S(1)}, u32[]{:S(2)}, u32[]{:S(2)}) collective-permute-start(bf16[32,1024]{1,0:T(8,128)(2,1)S(1)} %add_convert_fusion), channel_id=1, source_target_pairs={{0,2},{1,3},{2,0},{3,1},{4,6},{5,7},{6,4},{7,5},{8,10},{9,11},{10,... | collective-permute-start | bytes 196616 | tf_op jit(solution)/shard_map/ppermute | solution.py:274

commit v7 on v6

--- a/solution.py
+++ b/solution.py
@@ -94,20 +94,20 @@
     )(in_hbm(x), picks, *[in_hbm(h) for h in hints], in_hbm(downs[0]), *downs[1:])
 
 
-def begin_kernel(tensor_ref, weight, out_ref):
-    out_ref[0] = tensor_ref[0]
-
-
-def begin_call(tensor_at, weight):
+def begin_kernel(tensor_ref, *rest):
+    rest[-1][0] = tensor_ref[0]
+
+
+def begin_call(tensor_at, weights):
     return pl.pallas_call(
         begin_kernel,
-        in_specs=[SMEM, HBM],
+        in_specs=[SMEM] + [HBM] * len(weights),
         out_specs=SMEM,
         out_shape=jax.ShapeDtypeStruct(tensor_at.shape, tensor_at.dtype),
         name="begin",
         compiler_params=pltpu.CompilerParams(vmem_limit_bytes=4 << 20, has_side_effects=True),
         cost_estimate=pl.CostEstimate(flops=1000, bytes_accessed=1000, transcendentals=0),
-    )(tensor_at, in_hbm(weight))
+    )(tensor_at, *[in_hbm(w) for w in weights])
 
 
 def dense_kernel(shards, ks, spans, given, first, kv, tensor_ref, weight, *rest):
@@ -331,7 +331,7 @@
     last = chain
     first = [k for k in where if not k & 1 and k != last ^ 1]
     second = [last ^ 1] + [k for k in where if k & 1 and k != last]
-    begin_call(tensor_at, w_query)
+    begin_call(tensor_at, [w_query, output_weight])
     wide = w_query.shape[1]
     local_heads = wide // head
     group_all = HEADS // KVS
@@ -393,8 +393,8 @@
     parts = dict(zip(k_outs[1:], blocks))
     even = [k for k in even if k not in parts]
     plan = [
-        [([k], f32) for k in even[:1]] + [(odd, bf16)] * bool(odd) + [([1], bf16)] * (whole > 1),
-        [([k], f32) for k in even[1:]],
+        [(odd, bf16)] * bool(odd),
+        [([k], f32) for k in even] + [([1], bf16)] * (whole > 1),
     ]
     plan = [groups for groups in plan if groups]
     for groups in plan:

time: 57.8 us -> 59.2 us (1.024)
  waiting for transfers between devices: 11.9 us -> 15.3 us
  starting transfers between devices: 16.4 us -> 14.4 us
    ppermute x13, waiting for transfers between devices: 11.3 us -> 14.7 us  [across(): return lax.ppermute(x, 'tensor', [(i, i ^ bit) for i in range(shards)])]
    ppermute x13, starting transfers between devices: 15.9 us -> 13.9 us  [across(): return lax.ppermute(x, 'tensor', [(i, i ^ bit) for i in range(shards)])]
  transfers between devices with their start and end apart: 17 -> 17, of which waited for: 8 -> 8; matrix products, arithmetic and copies ran while one was open for 8% -> 8% of each run, Pallas kernels for 21% -> 20%
where the time goes in v7:
time: 59.2 us; the launch traced here: 59 us
  Pallas kernels  16 us (27%)
  waiting for transfers between devices  15.3 us (26%)
  starting transfers between devices  14.4 us (24%)
  local copies, waits for them, and re-layouts  8.37 us (14%)
  other arithmetic  4.56 us (8%)
    ppermute x13, waiting for transfers between devices, across(): return lax.ppermute(x, 'tensor', [(i, i ^ bit) for i in range(shards)])  14.7 us
    ppermute x13, starting transfers between devices, across(): return lax.ppermute(x, 'tensor', [(i, i ^ bit) for i in range(shards)])  13.9 us
    unnamed x28, local copies, waits for them, and re-layouts  8.28 us
    pallas_call x2, Pallas kernels, dense_call(): pl.pallas_call(functools.partial(dense_kernel, shards, ks, spans, len(arr...  7.07 us
    pallas_call x1, Pallas kernels, per_device(): pl.pallas_call(functools.partial(mix_kernel, sizes), in_specs=[SMEM, VMEM...  3.18 us
    pallas_call x2, Pallas kernels, resident_call(): pl.pallas_call(functools.partial(resident_kernel, ks, spans), in_specs=[S...  2.75 us
    add x1, other arithmetic, per_device(): low = low + got[:, width:].astype(jnp.float32)  1.53 us
    pallas_call x1, Pallas kernels, low_call(): pl.pallas_call(functools.partial(low_kernel, len(downs), len(hints)), in_...  1.53 us
  transfers between devices with their start and end apart: 17, of which 8 were waited for; matrix products, arithmetic and copies ran while one was open for 8% of the time, Pallas kernels for 20%

profile of v7, /device:TPU:0, one launch (start us, length us, event | category | flops | bytes accessed | tf_op | source)
XLA Modules:
  0.0 59.0 jit_solution(9596728756657410469)
XLA Ops:
  0.0 4.1 %collective-permute-start = (bf16[32,1024]{1,0:T(8,128)(2,1)}, bf16[32,1024]{1,0:T(8,128)(2,1)S(1)}, u32[]{:S(2)}, u32[]{:S(2)}) collective-permute-start(bf16[32,1024]{1,0:T(8,128)(2,1)} %x_hbm.1), channel_id=1, source_target_pairs={{0,4},{1,5},{2,6},{3,7},{4,0},{5,1},{6,2},{7,3},{8,12},{9,13},{10,... | collective-permute-start | bytes 196616 | tf_op jit(solution)/shard_map/ppermute | solution.py:274
  4.1 1.6 %collective-permute-start.6 = (bf16[32,1024]{1,0:T(8,128)(2,1)}, bf16[32,1024]{1,0:T(8,128)(2,1)}, u32[]{:S(2)}, u32[]{:S(2)}) collective-permute-start(bf16[32,1024]{1,0:T(8,128)(2,1)} %x_hbm.1), channel_id=1, source_target_pairs={{0,2},{1,3},{2,0},{3,1},{4,6},{5,7},{6,4},{7,5},{8,10},{9,11},{10,... | collective-permute-start | bytes 196616 | tf_op jit(solution)/shard_map/ppermute | solution.py:274
  5.6 0.0 collective-permute-start.1
  5.6 0.5 collective-permute-start.8
  6.2 0.0 collective-permute-start.9
  6.2 0.8 %select_reduce_fusion = s32[64]{0:T(128)S(1)} fusion(s32[8]{0:T(128)} %param.22, s32[64]{0:T(128)} %param.21), kind=kLoop, calls=%fused_computation.30 | loop fusion | flops 1472 | bytes 544 | tf_op jit(solution)/shard_map/reduce_sum | solution.py:284
  7.0 0.1 dynamic_slice.3
  7.0 0.1 broadcast_compare_fusion.1
  7.1 0.6 %collective-permute-done.1.rest_1_ = bf16[256,1024]{1,0:T(8,128)(2,1)S(1)} collective-permute-done((bf16[256,1024]{1,0:T(8,128)(2,1)}, bf16[256,1024]{1,0:T(8,128)(2,1)S(1)}, u32[]{:S(2)}, u32[]{:S(2)}) %collective-permute-start.1) | collective-permute-done | bytes 524320 | tf_op jit(solution)/shard_map/ppermute | solution.py:279
  7.8 1.5 %low.1 = (f32[32,128]{1,0:T(8,128)S(1)}, bf16[32,1024]{1,0:T(8,128)(2,1)S(1)}) custom-call(bf16[32,1024]{1,0:T(8,128)(2,1)} %x_hbm.1, f32[32,512]{1,0:T(8,128)S(1)} %add_convert_fusion.3.picks_ref.refs_6_, bf16[256,1024]{1,0:T(8,128)(2,1)} %bitcast.16, bf16[256,1024]{1,0:T(8,128)(2,1)S(1)} %collective-permute-done.1.rest_1_), custom_call_target="tpu_custom_call" | custom-call | flops 100000000 | bytes 1000000 | tf_op jit(solution)/shard_map/low/pallas_call | solution.py:82
  9.3 0.4 collective-permute-start.2
  9.7 0.0 collective-permute-done.6.rest_2_
  9.7 1.5 %collective-permute-start.7 = (bf16[32,1024]{1,0:T(8,128)(2,1)}, bf16[32,1024]{1,0:T(8,128)(2,1)}, u32[]{:S(2)}, u32[]{:S(2)}) collective-permute-start(bf16[32,1024]{1,0:T(8,128)(2,1)} %collective-permute-done.6.rest_2_), channel_id=1, source_target_pairs={{0,1},{1,0},{2,3},{3,2},{4,5},{5,4},{6,7},{7,6},{8,9},{9,8},{10,11... | collective-permute-start | bytes 196616 | tf_op jit(solution)/shard_map/ppermute | solution.py:274
  11.2 2.8 %collective-permute-done.2 = f32[32,128]{1,0:T(8,128)S(1)} collective-permute-done((f32[32,128]{1,0:T(8,128)S(1)}, f32[32,128]{1,0:T(8,128)S(1)}, u32[]{:S(2)}, u32[]{:S(2)}) %collective-permute-start.2) | collective-permute-done | bytes 16416 | tf_op jit(solution)/shard_map/ppermute | solution.py:274
  14.1 0.0 collective-permute-done.rest_1_
  14.1 0.5 collective-permute-start.3
  14.6 0.7 %pad_maximum_fusion = bf16[64,1024]{1,0:T(8,128)(2,1)} fusion(bf16[32,1024]{1,0:T(8,128)(2,1)S(1)} %collective-permute-done.rest_1_, bf16[32,1024]{1,0:T(8,128)(2,1)S(1)} %get-tuple-element.19.rest_0_), kind=kLoop, calls=%fused_computation | loop fusion | flops 262144 | bytes 262144 | tf_op jit(solution)/shard_map/concatenate | solution.py:322
  15.2 1.5 %collective-permute-start.5 = (bf16[64,1024]{1,0:T(8,128)(2,1)}, bf16[64,1024]{1,0:T(8,128)(2,1)S(1)}, u32[]{:S(2)}, u32[]{:S(2)}) collective-permute-start(bf16[64,1024]{1,0:T(8,128)(2,1)} %pad_maximum_fusion), channel_id=1, source_target_pairs={{0,1},{1,0},{2,3},{3,2},{4,5},{5,4},{6,7},{7,6},{8,9},{9,8},{10,11... | collective-permute-start | bytes 393224 | tf_op jit(solution)/shard_map/ppermute | solution.py:274
  16.7 1.8 %collective-permute-done.3.rest_0_ = bf16[32,1152]{1,0:T(8,128)(2,1)S(1)} collective-permute-done((bf16[32,1152]{1,0:T(8,128)(2,1)S(1)}, bf16[32,1152]{1,0:T(8,128)(2,1)S(1)}, u32[]{:S(2)}, u32[]{:S(2)}) %collective-permute-start.3) | collective-permute-done | bytes 73760 | tf_op jit(solution)/shard_map/ppermute | solution.py:274
  18.5 0.6 %pad_maximum_fusion.2 = bf16[32,1152]{1,0:T(8,128)(2,1)} fusion(bf16[32,128]{1,0:T(8,128)(2,1)S(1)} %fusion.2, bf16[32,1024]{1,0:T(8,128)(2,1)S(1)} %slice.37), kind=kLoop, calls=%fused_computation.9 | loop fusion | flops 147456 | bytes 147456 | tf_op jit(solution)/shard_map/concatenate | solution.py:312
  19.2 1.5 %collective-permute-start.4 = (bf16[32,1152]{1,0:T(8,128)(2,1)}, bf16[32,1152]{1,0:T(8,128)(2,1)}, u32[]{:S(2)}, u32[]{:S(2)}) collective-permute-start(bf16[32,1152]{1,0:T(8,128)(2,1)} %pad_maximum_fusion.2), channel_id=1, source_target_pairs={{0,1},{1,0},{2,3},{3,2},{4,5},{5,4},{6,7},{7,6},{8,9},{9,8},{10,11... | collective-permute-start | bytes 221192 | tf_op jit(solution)/shard_map/ppermute | solution.py:274
  20.7 0.0 copy-done.4
  20.7 0.7 %fusion.1.refs_13_ = f32[32,1024]{1,0:T(8,128)S(1)} fusion(s32[32]{0:T(128)} %param.23, s32[1024]{0:T(1024)S(1)} %get-tuple-element.38, s32[1024]{0:T(1024)S(1)} %get-tuple-element.39, s32[32]{0:T(128)S(1)} %get-tuple-element.43, s32[32]{0:T(128)S(1)} %get-tuple-element.44, s32[1024]{0:T(1024)S(1)} %get-tuple-element.37, s32[1024]{0:T(1024)S(1)} %get-tuple-element.40, ...), kind=kLoop, calls=%fused_computation.7 | loop fusion | flops 229376 | bytes 149920 | tf_op jit(solution)/shard_map/convert_element_type | solution.py:297
  21.5 0.0 copy-start
  21.5 5.8 %copy-done = bf16[8192,1024]{1,0:T(8,128)(2,1)S(1)} copy-done((bf16[8192,1024]{1,0:T(8,128)(2,1)S(1)}, bf16[8192,1024]{1,0:T(8,128)(2,1)}, u32[]{:S(2)}) %copy-start) | copy-done | bytes 16777240
  27.2 0.0 slice-start.5
  27.2 0.0 slice-start.6
  27.3 2.2 %shard_map.118.rest_3_ = f32[32,1024]{1,0:T(8,128)S(1)} custom-call(s32[1]{0:T(128)} %bitcast.tensor_ref.refs_0_, bf16[8192,1024]{1,0:T(8,128)(2,1)S(1)} %copy-done, bf16[32,1024]{1,0:T(8,128)(2,1)S(1)} %get-tuple-element.19.rest_0_, bf16[32,1024]{1,0:T(8,128)(2,1)S(1)} %collective-permute-done.rest_1_, bf16[32,1024]{1,0:T(8,128)(2,1)} %collective-permute-done.6.rest_2_, ...), custom_call_target="tpu_custom_call" | custom-call | flops 201326592 | bytes 1000000 | tf_op jit(solution)/shard_map/pallas_call | solution.py:141
  29.4 0.0 slice-start.3
  29.5 0.0 slice-start.7
  29.5 0.0 copy-start.1
  29.5 0.0 copy-start.2
  29.5 0.0 collective-permute-done.7.rest_2_
  29.5 0.0 collective-permute-done.5.rest_1_
  29.5 4.9 %shard_map.119 = (f32[32,1024]{1,0:T(8,128)S(1)}, bf16[32,1,32,128]{3,2,1,0:T(8,128)(2,1)S(1)}, bf16[32,1,32,128]{3,2,1,0:T(8,128)(2,1)S(1)}) custom-call(s32[1]{0:T(128)} %bitcast.tensor_ref.refs_0_, bf16[8192,1024]{1,0:T(8,128)(2,1)S(1)} %copy-done, bf16[32,1152]{1,0:T(8,128)(2,1)S(1)} %collective-permute-done.3.rest_0_, ...), custom_call_target="tpu_custom_call" | custom-call | flops 268435456 | bytes 1000000 | tf_op jit(solution)/shard_map/pallas_call | solution.py:141
  34.4 0.0 collective-permute-done.4.refs_1_
  34.4 0.0 copy-done.5
  34.4 1.5 %convert_add_fusion.1.refs_5_ = f32[32,128]{1,0:T(8,128)S(1)} fusion(f32[32,128]{1,0:T(8,128)S(1)} %copy-done.5, bf16[32,1152]{1,0:T(8,128)(2,1)} %collective-permute-done.4.refs_1_, bf16[32,1152]{1,0:T(8,128)(2,1)S(1)} %collective-permute-done.3.rest_0_), kind=kLoop, calls=%fused_computation.15 | loop fusion | flops 16384 | bytes 49152 | tf_op jit(solution)/shard_map/add | solution.py:315
  36.0 0.0 collective-permute-done.8.refs_8_
  36.0 0.0 collective-permute-done.9.refs_10_
  36.0 0.0 slice-done
  36.0 1.1 %slice-done.3 = s8[4194304]{0:T(1024)(128)(4,1)S(1)} async-done(((s8[16777216]{0:T(1024)(128)(4,1)}), s8[4194304]{0:T(1024)(128)(4,1)S(1)}, s32[]{:S(2)}) %slice-start.3) | async-done | bytes 4194328
  37.1 1.2 %slice-done.7 = s8[4194304]{0:T(1024)(128)(4,1)S(1)} async-done(((s8[16777216]{0:T(1024)(128)(4,1)}), s8[4194304]{0:T(1024)(128)(4,1)S(1)}, s32[]{:S(2)}) %slice-start.7) | async-done | bytes 4194328
  38.3 0.0 copy-done.1
  38.3 0.2 copy-done.2
  38.5 3.2 %mix.1 = (f32[32,128]{1,0:T(8,128)S(1)}, bf16[32,1024]{1,0:T(8,128)(2,1)S(1)}, bf16[32,1152]{1,0:T(8,128)(2,1)S(1)}) custom-call(s32[1]{0:T(128)} %bitcast.tensor_ref.refs_0_, bf16[32,1152]{1,0:T(8,128)(2,1)} %collective-permute-done.4.refs_1_, bf16[8192,1024]{1,0:T(8,128)(2,1)S(1)} %bitcast.8, bf16[1024,8192]{1,0:T(8,128)(2,1)S(1)} %bitcast.6, ...), custom_call_target="tpu_custom_call" | custom-call | flops 1000000000 | bytes 6291456 | tf_op jit(solution)/shard_map/mix/pallas_call | solution.py:355
  41.7 0.6 collective-permute-start.11
  42.3 0.8 %shard_map.121 = bf16[64,1024]{1,0:T(8,128)(2,1)S(1)} custom-call(s32[1]{0:T(128)} %bitcast.tensor_ref.refs_0_, bf16[32,1024]{1,0:T(8,128)(2,1)S(1)} %get-tuple-element.25.x_ref, bf16[1024,8192]{1,0:T(8,128)(2,1)S(1)} %bitcast.6), custom_call_target="tpu_custom_call" | custom-call | tf_op jit(solution)/shard_map/pallas_call | solution.py:215
  43.1 1.9 %shard_map.120 = (f32[32,1024]{1,0:T(8,128)S(1)}, f32[32,1024]{1,0:T(8,128)S(1)}, f32[32,1024]{1,0:T(8,128)S(1)}, f32[32,1024]{1,0:T(8,128)S(1)}, bf16[32,1024]{1,0:T(8,128)(2,1)S(1)}) custom-call(s32[1]{0:T(128)} %bitcast.tensor_ref.refs_0_, bf16[32,1024]{1,0:T(8,128)(2,1)S(1)} %get-tuple-element.25.x_ref, bf16[1024,8192]{1,0:T(8,128)(2,1)S(1)} %bitcast.6), custom_call_target="tpu_custom_call" | custom-call | tf_op jit(solution)/shard_map/pallas_call | solution.py:215
  45.0 1.5 %collective-permute-start.13 = (bf16[64,1024]{1,0:T(8,128)(2,1)S(1)}, bf16[64,1024]{1,0:T(8,128)(2,1)S(1)}, u32[]{:S(2)}, u32[]{:S(2)}) collective-permute-start(bf16[64,1024]{1,0:T(8,128)(2,1)S(1)} %shard_map.121), channel_id=1, source_target_pairs={{0,1},{1,0},{2,3},{3,2},{4,5},{5,4},{6,7},{7,6},{8,9},{9,8},{10,11... | collective-permute-start | bytes 393224 | tf_op jit(solution)/shard_map/ppermute | solution.py:274
  46.5 0.3 collective-permute-done.11.rest_2_
  46.9 0.4 collective-permute-start.12
  47.4 0.0 collective-permute-start.10
  47.4 0.2 collective-permute-start.15
  47.6 2.4 %collective-permute-done.13 = bf16[64,1024]{1,0:T(8,128)(2,1)S(1)} collective-permute-done((bf16[64,1024]{1,0:T(8,128)(2,1)S(1)}, bf16[64,1024]{1,0:T(8,128)(2,1)S(1)}, u32[]{:S(2)}, u32[]{:S(2)}) %collective-permute-start.13) | collective-permute-done | bytes 131104 | tf_op jit(solution)/shard_map/ppermute | solution.py:274
  50.0 2.7 %collective-permute-done.12.rest_3_ = bf16[32,1152]{1,0:T(8,128)(2,1)S(1)} collective-permute-done((bf16[32,1152]{1,0:T(8,128)(2,1)S(1)}, bf16[32,1152]{1,0:T(8,128)(2,1)S(1)}, u32[]{:S(2)}, u32[]{:S(2)}) %collective-permute-start.12) | collective-permute-done | bytes 73760 | tf_op jit(solution)/shard_map/ppermute | solution.py:274
  52.8 0.1 collective-permute-start.14
  52.9 0.1 collective-permute-start.16
  52.9 0.5 begin.1
  53.5 0.0 collective-permute-done.10.rest_1_
  53.5 0.0 collective-permute-done.15.rest_6_
  53.5 3.7 %collective-permute-done.16.rest_7_ = bf16[32,1024]{1,0:T(8,128)(2,1)S(1)} collective-permute-done((bf16[32,1024]{1,0:T(8,128)(2,1)S(1)}, bf16[32,1024]{1,0:T(8,128)(2,1)S(1)}, u32[]{:S(2)}, u32[]{:S(2)}) %collective-permute-start.16) | collective-permute-done | bytes 65568 | tf_op jit(solution)/shard_map/ppermute | solution.py:274
  57.2 0.9 %collective-permute-done.14.rest_4_ = bf16[32,1152]{1,0:T(8,128)(2,1)S(1)} collective-permute-done((bf16[32,1152]{1,0:T(8,128)(2,1)S(1)}, bf16[32,1152]{1,0:T(8,128)(2,1)S(1)}, u32[]{:S(2)}, u32[]{:S(2)}) %collective-permute-start.14) | collective-permute-done | bytes 73760 | tf_op jit(solution)/shard_map/ppermute | solution.py:274
  58.1 0.9 %final.1 = bf16[32,1024]{1,0:T(8,128)(2,1)} custom-call(f32[32,512]{1,0:T(8,128)S(1)} %add_convert_fusion.3.picks_ref.refs_6_, f32[32,128]{1,0:T(8,128)S(1)} %get-tuple-element.23.low_ref, bf16[256,1024]{1,0:T(8,128)(2,1)S(1)} %bitcast.14, bf16[256,1024]{1,0:T(8,128)(2,1)S(1)} %collective-permute-done.10.rest_1_, ...), custom_call_target="tpu_custom_call" | custom-call | flops 100000000 | bytes 1000000 | tf_op jit(solution)/shard_map/final/pallas_call | solution.py:426
  (34 shorter events, 0.2 us)
Async XLA Ops:
  0.0 14.1 %collective-permute-start = (bf16[32,1024]{1,0:T(8,128)(2,1)}, bf16[32,1024]{1,0:T(8,128)(2,1)S(1)}, u32[]{:S(2)}, u32[]{:S(2)}) collective-permute-start(bf16[32,1024]{1,0:T(8,128)(2,1)} %x_hbm.1), channel_id=1, source_target_pairs={{0,4},{1,5},{2,6},{3,7},{4,0},{5,1},{6,2},{7,3},{8,12},{9,13},{10,... | collective-permute-start | bytes 196616 | tf_op jit(solution)/shard_map/ppermute | solution.py:274
  4.1 5.6 %collective-permute-start.6 = (bf16[32,1024]{1,0:T(8,128)(2,1)}, bf16[32,1024]{1,0:T(8,128)(2,1)}, u32[]{:S(2)}, u32[]{:S(2)}) collective-permute-start(bf16[32,1024]{1,0:T(8,128)(2,1)} %x_hbm.1), channel_id=1, source_target_pairs={{0,2},{1,3},{2,0},{3,1},{4,6},{5,7},{6,4},{7,5},{8,10},{9,11},{10,... | collective-permute-start | bytes 196616 | tf_op jit(solution)/shard_map/ppermute | solution.py:274
  5.6 2.1 %collective-permute-start.1 = (bf16[256,1024]{1,0:T(8,128)(2,1)}, bf16[256,1024]{1,0:T(8,128)(2,1)S(1)}, u32[]{:S(2)}, u32[]{:S(2)}) collective-permute-start(bf16[256,1024]{1,0:T(8,128)(2,1)} %bitcast.15), channel_id=1, source_target_pairs={{0,8},{8,0},{1,9},{9,1},{2,10},{10,2},{3,11},{11,3},{4,12},{12,4},... | collective-permute-start | bytes 1572872 | tf_op jit(solution)/shard_map/ppermute | solution.py:279
  5.6 30.3 %collective-permute-start.8 = (bf16[256,1024]{1,0:T(8,128)(2,1)}, bf16[256,1024]{1,0:T(8,128)(2,1)S(1)}, u32[]{:S(2)}, u32[]{:S(2)}) collective-permute-start(bf16[256,1024]{1,0:T(8,128)(2,1)} %bitcast.9), channel_id=1, source_target_pairs={{0,8},{8,0},{1,9},{9,1},{2,10},{10,2},{3,11},{11,3},{4,12},{12,4},... | collective-permute-start | bytes 1572872 | tf_op jit(solution)/shard_map/ppermute | solution.py:279
  6.2 29.8 %collective-permute-start.9 = (bf16[256,1024]{1,0:T(8,128)(2,1)}, bf16[256,1024]{1,0:T(8,128)(2,1)}, u32[]{:S(2)}, u32[]{:S(2)}) collective-permute-start(bf16[256,1024]{1,0:T(8,128)(2,1)} %bitcast.11), channel_id=1, source_target_pairs={{0,8},{8,0},{1,9},{9,1},{2,10},{10,2},{3,11},{11,3},{4,12},{12,4},... | collective-permute-start | bytes 1572872 | tf_op jit(solution)/shard_map/ppermute | solution.py:279
  9.3 4.8 %collective-permute-start.2 = (f32[32,128]{1,0:T(8,128)S(1)}, f32[32,128]{1,0:T(8,128)S(1)}, u32[]{:S(2)}, u32[]{:S(2)}) collective-permute-start(f32[32,128]{1,0:T(8,128)S(1)} %get-tuple-element.18), channel_id=1, source_target_pairs={{0,4},{1,5},{2,6},{3,7},{4,0},{5,1},{6,2},{7,3},{8,12},{9,13},{10,... | collective-permute-start | bytes 49160 | tf_op jit(solution)/shard_map/ppermute | solution.py:274
  9.7 19.8 %collective-permute-start.7 = (bf16[32,1024]{1,0:T(8,128)(2,1)}, bf16[32,1024]{1,0:T(8,128)(2,1)}, u32[]{:S(2)}, u32[]{:S(2)}) collective-permute-start(bf16[32,1024]{1,0:T(8,128)(2,1)} %collective-permute-done.6.rest_2_), channel_id=1, source_target_pairs={{0,1},{1,0},{2,3},{3,2},{4,5},{5,4},{6,7},{7,6},{8,9},{9,8},{10,11... | collective-permute-start | bytes 196616 | tf_op jit(solution)/shard_map/ppermute | solution.py:274
  14.1 6.6 %copy-start.4 = (f32[32,128]{1,0:T(8,128)}, f32[32,128]{1,0:T(8,128)S(1)}, u32[]{:S(2)}) copy-start(f32[32,128]{1,0:T(8,128)S(1)} %get-tuple-element.32) | copy-start | bytes 49156
  14.1 4.4 %collective-permute-start.3 = (bf16[32,1152]{1,0:T(8,128)(2,1)S(1)}, bf16[32,1152]{1,0:T(8,128)(2,1)S(1)}, u32[]{:S(2)}, u32[]{:S(2)}) collective-permute-start(bf16[32,1152]{1,0:T(8,128)(2,1)S(1)} %pad_maximum_fusion.1), channel_id=1, source_target_pairs={{0,2},{1,3},{2,0},{3,1},{4,6},{5,7},{6,4},{7,5},{8,10},{9,11},{10,... | collective-permute-start | bytes 221192 | tf_op jit(solution)/shard_map/ppermute | solution.py:274
  15.2 14.3 %collective-permute-start.5 = (bf16[64,1024]{1,0:T(8,128)(2,1)}, bf16[64,1024]{1,0:T(8,128)(2,1)S(1)}, u32[]{:S(2)}, u32[]{:S(2)}) collective-permute-start(bf16[64,1024]{1,0:T(8,128)(2,1)} %pad_maximum_fusion), channel_id=1, source_target_pairs={{0,1},{1,0},{2,3},{3,2},{4,5},{5,4},{6,7},{7,6},{8,9},{9,8},{10,11... | collective-permute-start | bytes 393224 | tf_op jit(solution)/shard_map/ppermute | solution.py:274
  19.2 15.2 %collective-permute-start.4 = (bf16[32,1152]{1,0:T(8,128)(2,1)}, bf16[32,1152]{1,0:T(8,128)(2,1)}, u32[]{:S(2)}, u32[]{:S(2)}) collective-permute-start(bf16[32,1152]{1,0:T(8,128)(2,1)} %pad_maximum_fusion.2), channel_id=1, source_target_pairs={{0,1},{1,0},{2,3},{3,2},{4,5},{5,4},{6,7},{7,6},{8,9},{9,8},{10,11... | collective-permute-start | bytes 221192 | tf_op jit(solution)/shard_map/ppermute | solution.py:274
  21.5 5.8 %copy-start = (bf16[8192,1024]{1,0:T(8,128)(2,1)S(1)}, bf16[8192,1024]{1,0:T(8,128)(2,1)}, u32[]{:S(2)}) copy-start(bf16[8192,1024]{1,0:T(8,128)(2,1)} %refs_2_.1) | copy-start | bytes 50331652
  27.2 8.8 %slice-start = ((s8[16777216]{0:T(1024)(128)(4,1)}), s8[4194304]{0:T(1024)(128)(4,1)S(1)}, s32[]{:S(2)}) async-start(s8[16777216]{0:T(1024)(128)(4,1)} %bitcast.5), calls=%async_computation | async-start | bytes 8388608
  27.2 8.8 %slice-start.1 = ((s8[16777216]{0:T(1024)(128)(4,1)}), s8[4194304]{0:T(1024)(128)(4,1)S(1)}, s32[]{:S(2)}) async-start(s8[16777216]{0:T(1024)(128)(4,1)} %bitcast.5), calls=%async_computation.1 | async-start | bytes 8388608
  27.2 8.8 %slice-start.2 = ((s8[16777216]{0:T(1024)(128)(4,1)}), s8[4194304]{0:T(1024)(128)(4,1)S(1)}, s32[]{:S(2)}) async-start(s8[16777216]{0:T(1024)(128)(4,1)} %bitcast.5), calls=%async_computation.2 | async-start | bytes 8388608
  27.2 8.8 %slice-start.4 = ((s8[16777216]{0:T(1024)(128)(4,1)}), s8[4194304]{0:T(1024)(128)(4,1)S(1)}, s32[]{:S(2)}) async-start(s8[16777216]{0:T(1024)(128)(4,1)} %bitcast.7), calls=%async_computation.4 | async-start | bytes 8388608
  27.2 8.8 %slice-start.5 = ((s8[16777216]{0:T(1024)(128)(4,1)}), s8[4194304]{0:T(1024)(128)(4,1)S(1)}, s32[]{:S(2)}) async-start(s8[16777216]{0:T(1024)(128)(4,1)} %bitcast.7), calls=%async_computation.5 | async-start | bytes 8388608
  27.2 8.8 %slice-start.6 = ((s8[16777216]{0:T(1024)(128)(4,1)}), s8[4194304]{0:T(1024)(128)(4,1)S(1)}, s32[]{:S(2)}) async-start(s8[16777216]{0:T(1024)(128)(4,1)} %bitcast.7), calls=%async_computation.6 | async-start | bytes 8388608
  29.4 5.0 %copy-start.5 = (f32[32,128]{1,0:T(8,128)S(1)}, f32[32,128]{1,0:T(8,128)}, u32[]{:S(2)}) copy-start(f32[32,128]{1,0:T(8,128)} %copy-done.4) | copy-start | bytes 49156
  29.4 7.7 %slice-start.3 = ((s8[16777216]{0:T(1024)(128)(4,1)}), s8[4194304]{0:T(1024)(128)(4,1)S(1)}, s32[]{:S(2)}) async-start(s8[16777216]{0:T(1024)(128)(4,1)} %bitcast.5), calls=%async_computation.3 | async-start | bytes 8388608
  29.5 8.9 %slice-start.7 = ((s8[16777216]{0:T(1024)(128)(4,1)}), s8[4194304]{0:T(1024)(128)(4,1)S(1)}, s32[]{:S(2)}) async-start(s8[16777216]{0:T(1024)(128)(4,1)} %bitcast.7), calls=%async_computation.7 | async-start | bytes 8388608
  29.5 8.9 %copy-start.1 = (bf16[4,64,1024]{2,1,0:T(8,128)(2,1)S(1)}, bf16[4,64,1024]{2,1,0:T(8,128)(2,1)}, u32[]{:S(2)}) copy-start(bf16[4,64,1024]{2,1,0:T(8,128)(2,1)} %param.18) | copy-start | bytes 1572868
  29.5 9.0 %copy-start.2 = (bf16[4,64,1024]{2,1,0:T(8,128)(2,1)S(1)}, bf16[4,64,1024]{2,1,0:T(8,128)(2,1)}, u32[]{:S(2)}) copy-start(bf16[4,64,1024]{2,1,0:T(8,128)(2,1)} %param.19) | copy-start | bytes 1572868
  41.7 5.2 %collective-permute-start.11 = (bf16[32,1152]{1,0:T(8,128)(2,1)S(1)}, bf16[32,1152]{1,0:T(8,128)(2,1)S(1)}, u32[]{:S(2)}, u32[]{:S(2)}) collective-permute-start(bf16[32,1152]{1,0:T(8,128)(2,1)S(1)} %get-tuple-element.24), channel_id=1, source_target_pairs={{0,1},{1,0},{2,3},{3,2},{4,5},{5,4},{6,7},{7,6},{8,9},{9,8},{10,11... | collective-permute-start | bytes 221192 | tf_op jit(solution)/shard_map/ppermute | solution.py:274
  42.3 5.1 %copy-start.3 = (bf16[4,64,1024]{2,1,0:T(8,128)(2,1)S(1)}, bf16[4,64,1024]{2,1,0:T(8,128)(2,1)}, u32[]{:S(2)}) copy-start(bf16[4,64,1024]{2,1,0:T(8,128)(2,1)} %param.20) | copy-start | bytes 1572868
  45.0 5.0 %collective-permute-start.13 = (bf16[64,1024]{1,0:T(8,128)(2,1)S(1)}, bf16[64,1024]{1,0:T(8,128)(2,1)S(1)}, u32[]{:S(2)}, u32[]{:S(2)}) collective-permute-start(bf16[64,1024]{1,0:T(8,128)(2,1)S(1)} %shard_map.121), channel_id=1, source_target_pairs={{0,1},{1,0},{2,3},{3,2},{4,5},{5,4},{6,7},{7,6},{8,9},{9,8},{10,11... | collective-permute-start | bytes 393224 | tf_op jit(solution)/shard_map/ppermute | solution.py:274
  46.9 5.8 %collective-permute-start.12 = (bf16[32,1152]{1,0:T(8,128)(2,1)S(1)}, bf16[32,1152]{1,0:T(8,128)(2,1)S(1)}, u32[]{:S(2)}, u32[]{:S(2)}) collective-permute-start(bf16[32,1152]{1,0:T(8,128)(2,1)S(1)} %pad_maximum_fusion.3), channel_id=1, source_target_pairs={{0,2},{1,3},{2,0},{3,1},{4,6},{5,7},{6,4},{7,5},{8,10},{9,11},{10,... | collective-permute-start | bytes 221192 | tf_op jit(solution)/shard_map/ppermute | solution.py:274
  47.4 6.1 %collective-permute-start.10 = (bf16[256,1024]{1,0:T(8,128)(2,1)S(1)}, bf16[256,1024]{1,0:T(8,128)(2,1)S(1)}, u32[]{:S(2)}, u32[]{:S(2)}) collective-permute-start(bf16[256,1024]{1,0:T(8,128)(2,1)S(1)} %bitcast.13), channel_id=1, source_target_pairs={{0,8},{8,0},{1,9},{9,1},{2,10},{10,2},{3,11},{11,3},{4,12},{12,4},... | collective-permute-start | bytes 1572872 | tf_op jit(solution)/shard_map/ppermute | solution.py:279
  47.4 6.1 %collective-permute-start.15 = (bf16[32,1024]{1,0:T(8,128)(2,1)S(1)}, bf16[32,1024]{1,0:T(8,128)(2,1)S(1)}, u32[]{:S(2)}, u32[]{:S(2)}) collective-permute-start(bf16[32,1024]{1,0:T(8,128)(2,1)S(1)} %get-tuple-element.29), channel_id=1, source_target_pairs={{0,1},{1,0},{2,3},{3,2},{4,5},{5,4},{6,7},{7,6},{8,9},{9,8},{10,11... | collective-permute-start | bytes 196616 | tf_op jit(solution)/shard_map/ppermute | solution.py:274
  52.8 5.3 %collective-permute-start.14 = (bf16[32,1152]{1,0:T(8,128)(2,1)S(1)}, bf16[32,1152]{1,0:T(8,128)(2,1)S(1)}, u32[]{:S(2)}, u32[]{:S(2)}) collective-permute-start(bf16[32,1152]{1,0:T(8,128)(2,1)S(1)} %pad_maximum_fusion.4), channel_id=1, source_target_pairs={{0,4},{1,5},{2,6},{3,7},{4,0},{5,1},{6,2},{7,3},{8,12},{9,13},{10,... | collective-permute-start | bytes 221192 | tf_op jit(solution)/shard_map/ppermute | solution.py:274
  52.9 4.3 %collective-permute-start.16 = (bf16[32,1024]{1,0:T(8,128)(2,1)S(1)}, bf16[32,1024]{1,0:T(8,128)(2,1)S(1)}, u32[]{:S(2)}, u32[]{:S(2)}) collective-permute-start(bf16[32,1024]{1,0:T(8,128)(2,1)S(1)} %add_convert_fusion), channel_id=1, source_target_pairs={{0,2},{1,3},{2,0},{3,1},{4,6},{5,7},{6,4},{7,5},{8,10},{9,11},{10,... | collective-permute-start | bytes 196616 | tf_op jit(solution)/shard_map/ppermute | solution.py:274
